TPU v7x, 32 devices: a whole 2x2x4 slice. The times are simulated.
32 devices in a mesh: design: 4 (over x, core), graph: 8 (over z, y).
Axes of the slice: x: 2, y: 2, z: 4, core: 2. Of those that a mesh axis runs over, the one named last changes fastest.
Arguments:
- nodes: bfloat16 [4, 65536, 128], P('design', 'graph'), may hold values from -6 to 6
- adjacency: bfloat16 [4, 512, 4, 128, 128], P('design', 'graph'), may hold values from -0.25 to 0.25
- tile_src: int32 [4, 512, 4], P('design', 'graph'), may hold values from 0 to 67, as said below
- pool_dst: int32 [4, 512, 1], P('design', 'graph'), may hold values from 0 to 7; in each aligned block of 64 rows (0 to 63, 64 to 127, ..., all dimensions but the last counted through in order) at most 16 rows name the same one
- pool_weight: bfloat16 [4, 512, 128, 128], P('design', 'graph'), may hold values from -0.0625 to 0.0625
- coarse_cot: bfloat16 [4, 1024, 128], P('design', 'graph'), may hold values from -48 to 48
- w_msg: bfloat16 [128, 128], replicated, may hold values from -0.5 to 0.5
- w_in: bfloat16 [256, 128], replicated, may hold values from -0.375 to 0.375
- b_in: float32 [128], replicated, may hold values from -3 to 3
- w_out: bfloat16 [128, 128], replicated, may hold values from -0.5 to 0.5
Outputs:
- fine_out: bfloat16 [4, 65536, 128], P('design', 'graph')
- coarse: bfloat16 [4, 1024, 128], P('design', 'graph')
- grad_msg: float32 [128, 128], replicated
- grad_in: float32 [256, 128], replicated
- grad_bias: float32 [128], replicated
- grad_out: float32 [128, 128], replicated
Inputs may be any that keep to these rules, and one draw needn't show every extreme that they name: `tile_src`: entry 0 is the destination tile itself (its slab index plus 2); every entry lies within 2 tiles of the destination tile; each slab's first and last tiles list the outermost neighbouring tile. `pool_dst`: among the 64 fine tiles of one slab, at most 16 name the same coarse tile.
All inputs are finite; a program needn't handle non-finite values.
Results may differ from a plain program's by a relative error of at most 0.0067.
Values may be sent and summed in bfloat16 or wider, within the bound.
No kernel may reach another device: no remote copies, remote signals or barrier semaphores. Data moves between devices by JAX's collectives and lax.ppermute only.
A program may use at most 128 MiB of HBM per device.

v0:
```python
import math

import jax
import jax.numpy as jnp
from jax import lax
from jax.sharding import PartitionSpec as P

H = 128
TILE = 128
NBR = 4
HT = 2


def padded(block, sides, width):
    for axis, dim in sides:
        count = lax.axis_size(axis)
        forward = [(i, i + 1) for i in range(count - 1)]
        backward = [(target, source) for source, target in forward]
        low = lax.ppermute(
            lax.slice_in_dim(block, block.shape[dim] - width, None, axis=dim), axis, forward
        )
        high = lax.ppermute(lax.slice_in_dim(block, 0, width, axis=dim), axis, backward)
        block = jnp.concatenate([low, block, high], axis=dim)
    return block


def silu_slope(pre):
    sig = jax.nn.sigmoid(pre)
    return sig * (1.0 + pre * (1.0 - sig))


def on_device(
    nodes, adjacency, tile_src, pool_dst, pool_weight, coarse_cot, w_msg, w_in, b_in, w_out
):
    feats = nodes[0]
    edge_w = adjacency[0]
    source = tile_src[0]
    target = pool_dst[0][:, 0]
    pooling = pool_weight[0]
    cot_tile = coarse_cot[0]
    rows = feats.shape[0]
    count = rows // TILE
    slabs = lax.axis_size("graph")
    designs = lax.axis_size("design")
    holders = jnp.arange(slabs)
    messages = jnp.dot(feats, w_msg, preferred_element_type=jnp.float32).astype(jnp.bfloat16)
    extended = padded(messages, (("graph", 0),), HT * TILE)
    extended = extended.reshape(count + 2 * HT, TILE, H)
    picked = extended[source]
    agg = jnp.einsum("tkij,tkjh->tih", edge_w, picked, preferred_element_type=jnp.float32)
    agg_b = agg.astype(jnp.bfloat16).reshape(rows, H)
    pre = (
        jnp.dot(feats, w_in[:H], preferred_element_type=jnp.float32)
        + jnp.dot(agg_b, w_in[H:], preferred_element_type=jnp.float32)
        + b_in
    )
    act = jax.nn.silu(pre).astype(jnp.bfloat16)
    fine = (
        feats.astype(jnp.float32) + jnp.dot(act, w_out, preferred_element_type=jnp.float32)
    ).astype(jnp.bfloat16)
    contrib = jnp.einsum(
        "tij,tjh->tih", pooling, fine.reshape(count, TILE, H), preferred_element_type=jnp.float32
    ).astype(jnp.bfloat16)
    owner_of = (target[None, :] == holders[:, None]).astype(jnp.bfloat16)
    partial_sums = jnp.einsum("ot,tih->oih", owner_of, contrib, preferred_element_type=jnp.float32)
    coarse_sum = lax.psum_scatter(partial_sums, "graph", scatter_dimension=0, tiled=True)[0]
    coarse = coarse_sum.astype(jnp.bfloat16)
    every_cot = lax.all_gather(cot_tile, "graph", axis=0, tiled=True).reshape(slabs, TILE, H)
    selector = (target[:, None] == holders[None, :]).astype(jnp.bfloat16)
    chosen = jnp.einsum(
        "to,oih->tih", selector, every_cot, preferred_element_type=jnp.float32
    ).astype(jnp.bfloat16)
    grad_y = (
        jnp.einsum("tji,tjh->tih", pooling, chosen, preferred_element_type=jnp.float32)
        .astype(jnp.bfloat16)
        .reshape(rows, H)
    )
    grad_out = jnp.dot(act.T, grad_y, preferred_element_type=jnp.float32)
    grad_act = jnp.dot(grad_y, w_out.T, preferred_element_type=jnp.float32)
    grad_pre = (grad_act * silu_slope(pre)).astype(jnp.bfloat16)
    grad_in = jnp.concatenate(
        [
            jnp.dot(feats.T, grad_pre, preferred_element_type=jnp.float32),
            jnp.dot(agg_b.T, grad_pre, preferred_element_type=jnp.float32),
        ],
        axis=0,
    )
    grad_bias = jnp.sum(grad_pre.astype(jnp.float32), axis=0)
    grad_agg = (
        jnp.dot(grad_pre, w_in[H:].T, preferred_element_type=jnp.float32)
        .astype(jnp.bfloat16)
        .reshape(count, TILE, H)
    )
    returned = jnp.einsum("tkij,tih->tkjh", edge_w, grad_agg, preferred_element_type=jnp.float32)
    grad_ext = (
        jnp.zeros((count + 2 * HT, TILE, H), jnp.float32)
        .at[source.reshape(-1)]
        .add(returned.reshape(count * NBR, TILE, H))
    )
    margins = jnp.concatenate([grad_ext[:HT], grad_ext[count + HT :]], axis=0).reshape(
        2 * HT * TILE, H
    )
    beside_all = padded(margins, (("graph", 0),), HT * TILE)
    from_left = beside_all[: HT * TILE]
    from_right = beside_all[beside_all.shape[0] - HT * TILE :]
    own_grad = grad_ext[HT : HT + count].reshape(rows, H)
    own_grad = own_grad.at[: HT * TILE].add(from_left)
    own_grad = own_grad.at[rows - HT * TILE :].add(from_right)
    grad_m = own_grad.astype(jnp.bfloat16)
    grad_msg = jnp.dot(feats.T, grad_m, preferred_element_type=jnp.float32)
    totals = lax.psum((grad_msg, grad_in, grad_bias, grad_out), ("design", "graph"))
    scale = 1.0 / math.sqrt(designs * rows * slabs)
    return (
        fine[None],
        coarse[None],
        totals[0] * scale,
        totals[1] * scale,
        totals[2] * scale,
        totals[3] * scale,
    )


def solution(mesh):
    in_specs = (
        P("design", "graph", None),
        P("design", "graph", None, None, None),
        P("design", "graph", None),
        P("design", "graph", None),
        P("design", "graph", None, None),
        P("design", "graph", None),
        P(),
        P(),
        P(),
        P(),
    )
    out_specs = (P("design", "graph", None), P("design", "graph", None), P(), P(), P(), P())
    return jax.shard_map(
        on_device, mesh=mesh, in_specs=in_specs, out_specs=out_specs, check_vma=False
    )
```

profile of v0, /device:TPU:0, one launch (start us, length us, event | category | flops | bytes accessed | tf_op | source)
XLA Modules:
  0.0 338.6 jit_solution(5713422980382294656)
XLA Ops:
  8.1 2.4 convolution_convert_fusion.1
  10.5 1.3 copy-done.7
  11.9 4.9 %collective-permute-start = (bf16[256,128]{1,0:T(8,128)(2,1)S(1)}, bf16[256,128]{1,0:T(8,128)(2,1)S(1)}, u32[]{:S(2)}, u32[]{:S(2)}) collective-permute-start(bf16[256,128]{1,0:T(8,128)(2,1)S(1)} %get-tuple-element.60), channel_id=1, source_target_pairs={{0,1},{1,2},{2,3},{3,4},{4,5},{5,6},{6,7},{8,9},{9,10},{10,11},{11... | collective-permute-start | bytes 196616 | tf_op jit(solution)/shard_map/ppermute | solution.py:19
  16.8 1.3 collective-permute-start.1
  18.5 33.1 %all-gather = bf16[1,1024,128]{2,1,0:T(8,128)(2,1)S(1)} all-gather(bf16[1,128,128]{2,1,0:T(8,128)(2,1)S(1)} %copy-done.13), channel_id=2, replica_groups=mesh['design'=4,'graph'=8] {'graph'}, dimensions={1}, use_global_device_ids=true | all-gather | bytes 294912 | tf_op jit(solution)/shard_map/all_gather | solution.py:68
  51.6 4.3 %fusion.18 = f32[8192,128]{1,0:T(8,128)} fusion(bf16[1,8192,128]{2,1,0:T(8,128)(2,1)} %param.14, bf16[256,128]{1,0:T(8,128)(2,1)S(1)} %copy-done.11), kind=kOutput, calls=%fused_computation.28 | convolution fusion | flops 268435456 | bytes 6324224 | tf_op jit(solution)/shard_map/dot_general | solution.py:53
  56.7 3.6 %fusion.24 = bf16[64,128,128]{1,2,0:T(8,128)(2,1)} fusion(bf16[1,64,128,128]{3,2,1,0:T(8,128)(2,1)S(1)} %copy-done, bf16[64,128,128]{2,0,1:T(8,128)(2,1)S(1)} %convolution_convert_fusion.2), kind=kOutput, calls=%fused_computation.33 | convolution fusion | flops 269484032 | bytes 6291456 | tf_op jit(solution)/shard_map/tji,tjh->tih/dot_general | solution.py:74
  60.3 5.8 %pad_maximum_fusion = bf16[8704,128]{1,0:T(8,128)(2,1)} fusion(bf16[256,128]{1,0:T(8,128)(2,1)S(1)} %collective-permute-done.1, bf16[8192,128]{1,0:T(8,128)(2,1)S(1)} %copy-done.8, bf16[256,128]{1,0:T(8,128)(2,1)S(1)} %collective-permute-done), kind=kLoop, calls=%fused_computation.18 | loop fusion | flops 6684672 | bytes 4456448 | tf_op jit(solution)/shard_map/concatenate | solution.py:23
  66.1 10.3 %gather_fusion = bf16[256,128,128]{2,1,0:T(8,128)(2,1)} fusion(bf16[68,128,128]{2,1,0:T(8,128)(2,1)} %bitcast.95, s32[1024]{0:T(1024)S(1)} %pad_clamp_fusion), kind=kCustom, calls=%fused_computation | custom fusion | bytes 16778240 | tf_op jit(solution)/shard_map/gather | solution.py:49
  76.4 8.3 %bitcast_convert_fusion = bf16[64,128,128]{1,2,0:T(8,128)(2,1)S(1)} fusion(bf16[64,4,128,128]{3,2,1,0:T(8,128)(2,1)} %bitcast.94, bf16[1,64,4,128,128]{4,3,2,1,0:T(8,128)(2,1)} %param.15), kind=kOutput, calls=%fused_computation.14 | convolution fusion | flops 1074790400 | bytes 18874368 | tf_op jit(solution)/shard_map/tkij,tkjh->tih/dot_general | solution.py:50
  84.7 1.4 multiply_convert_fusion
  86.3 1.4 fusion.52
  88.6 1.8 convert_reduce_fusion
  92.5 2.9 convert_bitcast_fusion
  95.5 8.1 %fusion.3 = f32[64,128,4,128]{3,1,2,0:T(8,128)} fusion(bf16[64,128,128,1]{2,1,3,0:T(8,128)(2,1)S(1)} %bitcast.96, bf16[1,64,4,128,128]{4,3,2,1,0:T(8,128)(2,1)S(1)} %bitcast.93), kind=kOutput, calls=%fused_computation.10 | convolution fusion | flops 1073741824 | bytes 27262976 | tf_op jit(solution)/shard_map/tkij,tih->tkjh/dot_general | solution.py:94
  103.6 17.4 %copy.52 = f32[256,128,128]{2,1,0:T(8,128)} copy(f32[256,128,128]{1,2,0:T(8,128)} %bitcast.91) | data formatting | bytes 33554432 | tf_op jit(solution)/shard_map/reshape | solution.py:98
  121.0 2.6 broadcast_in_dim.5
  123.6 49.6 %scatter_fusion = f32[68,128,128]{2,1,0:T(8,128)} fusion(f32[68,128,128]{2,1,0:T(8,128)} %broadcast_in_dim.5, s32[256]{0:T(256)S(1)} %bitcast.107, f32[256,128,128]{2,1,0:T(8,128)} %copy.52), kind=kCustom, calls=%fused_computation.1 | custom fusion | flops 4194304 | bytes 50332672 | tf_op jit(solution)/shard_map/scatter-add | solution.py:98
  173.2 1.2 fusion.49
  174.4 2.8 collective-permute-start.2
  177.2 2.4 fusion.29
  179.6 2.2 slice.85
  181.8 4.2 %copy.45 = bf16[64,128,128]{2,0,1:T(8,128)(2,1)} copy(bf16[64,128,128]{1,2,0:T(8,128)(2,1)} %convert_bitcast_fusion) | data formatting | bytes 4194304 | tf_op jit(solution)/shard_map/convert_element_type | solution.py:63
  185.9 1.3 collective-permute-start.3
  188.6 4.2 %collective-permute-done.3 = f32[256,128]{1,0:T(8,128)S(1)} collective-permute-done((f32[256,128]{1,0:T(8,128)S(1)}, f32[256,128]{1,0:T(8,128)S(1)}, u32[]{:S(2)}, u32[]{:S(2)}) %collective-permute-start.3) | collective-permute-done | bytes 131104 | tf_op jit(solution)/shard_map/ppermute | solution.py:22
  192.8 1.6 fusion.38
  194.4 3.6 %fusion.32 = f32[128,128]{0,1:T(8,128)} fusion(bf16[1,8192,128]{2,1,0:T(8,128)(2,1)S(1)} %copy-done.4, f32[8192,128]{1,0:T(8,128)} %fusion.38), kind=kOutput, calls=%fused_computation.36 | convolution fusion | flops 269484032 | bytes 6356992 | tf_op jit(solution)/shard_map/dot_general | solution.py:110
  198.0 2.1 fusion.43
  201.1 39.8 %psum.30 = f32[128]{0:T(128)S(1)} all-reduce(f32[128]{0:T(128)S(1)} %get-tuple-element.64), channel_id=1, replica_groups=mesh['design'=4,'graph'=8] {'design','graph'}, use_global_device_ids=true, to_apply=%region_5.6 | all-reduce | flops 128 | bytes 1024 | tf_op jit(solution)/shard_map/psum | solution.py:111
  241.4 84.4 %all-reduce.3.cloned.1.call-done = (f32[128,128]{0,1:T(8,128)}, f32[256,128]{1,0:T(8,128)}, f32[128,128]{0,1:T(8,128)}) async-done(((f32[128,128]{0,1:T(8,128)}, f32[256,128]{1,0:T(8,128)}, f32[128,128]{0,1:T(8,128)}), (f32[128,128]{0,1:T(8,128)}, f32[256,128]{1,0:T(8,128)}, f32[128,128]{0,1:T(8,128)})) %all-reduce.3.cloned.1.call-update) | async-done | bytes 262160 | tf_op jit(solution)/shard_map/psum | solution.py:111
  328.1 1.6 broadcast_multiply_fusion
  329.7 1.5 convert_element_type.59
  (65 shorter events, 9.6 us)
Async XLA Ops:
  8.0 48.7 %copy-start = (bf16[1,64,128,128]{3,2,1,0:T(8,128)(2,1)S(1)}, bf16[1,64,128,128]{3,2,1,0:T(8,128)(2,1)}, u32[]{:S(2)}) copy-start(bf16[1,64,128,128]{3,2,1,0:T(8,128)(2,1)} %param.18) | copy-start | bytes 6291460
  8.0 10.1 %copy-start.14 = (s32[1,64,4]{1,2,0:T(4,128)S(1)}, s32[1,64,4]{1,2,0:T(4,128)}, u32[]{:S(2)}) copy-start(s32[1,64,4]{1,2,0:T(4,128)} %param.16) | copy-start | bytes 3076
  8.0 10.5 %copy-start.13 = (bf16[1,128,128]{2,1,0:T(8,128)(2,1)S(1)}, bf16[1,128,128]{2,1,0:T(8,128)(2,1)}, u32[]{:S(2)}) copy-start(bf16[1,128,128]{2,1,0:T(8,128)(2,1)} %param.19) | copy-start | bytes 98308
  8.0 43.6 %copy-start.11 = (bf16[256,128]{1,0:T(8,128)(2,1)S(1)}, bf16[256,128]{1,0:T(8,128)(2,1)}, u32[]{:S(2)}) copy-start(bf16[256,128]{1,0:T(8,128)(2,1)} %param.21) | copy-start | bytes 196612
  8.0 317.7 %all-reduce.3.cloned.1.call-start = ((), (), s32[]{:S(2)}) async-start(), calls=%async_computation.2 | async-start | bytes 524288 | tf_op jit(solution)/shard_map/psum | solution.py:111
  10.5 1.3 copy-start.7
  11.9 48.4 %collective-permute-start = (bf16[256,128]{1,0:T(8,128)(2,1)S(1)}, bf16[256,128]{1,0:T(8,128)(2,1)S(1)}, u32[]{:S(2)}, u32[]{:S(2)}) collective-permute-start(bf16[256,128]{1,0:T(8,128)(2,1)S(1)} %get-tuple-element.60), channel_id=1, source_target_pairs={{0,1},{1,2},{2,3},{3,4},{4,5},{5,6},{6,7},{8,9},{9,10},{10,11},{11... | collective-permute-start | bytes 196616 | tf_op jit(solution)/shard_map/ppermute | solution.py:19
  16.8 43.5 %collective-permute-start.1 = (bf16[256,128]{1,0:T(8,128)(2,1)S(1)}, bf16[256,128]{1,0:T(8,128)(2,1)S(1)}, u32[]{:S(2)}, u32[]{:S(2)}) collective-permute-start(bf16[256,128]{1,0:T(8,128)(2,1)S(1)} %get-tuple-element.61), channel_id=1, source_target_pairs={{1,0},{2,1},{3,2},{4,3},{5,4},{6,5},{7,6},{9,8},{10,9},{11,10},{12... | collective-permute-start | bytes 196616 | tf_op jit(solution)/shard_map/ppermute | solution.py:22
  51.6 4.3 %copy-start.15 = (s32[1,64,1]{1,2,0:T(1,128)S(1)}, s32[1,64,1]{1,2,0:T(1,128)}, u32[]{:S(2)}) copy-start(s32[1,64,1]{1,2,0:T(1,128)} %param.17) | copy-start | bytes 772
  56.7 3.6 %copy-start.8 = (bf16[8192,128]{1,0:T(8,128)(2,1)S(1)}, bf16[8192,128]{1,0:T(8,128)(2,1)}, u32[]{:S(2)}) copy-start(bf16[8192,128]{1,0:T(8,128)(2,1)} %copy-done.7) | copy-start | bytes 6291460
  76.4 8.3 %copy-start.9 = (f32[8192,128]{1,0:T(8,128)S(1)}, f32[8192,128]{1,0:T(8,128)}, u32[]{:S(2)}) copy-start(f32[8192,128]{1,0:T(8,128)} %fusion.18) | copy-start | bytes 12582916
  76.4 8.3 %copy-start.16 = (f32[128]{0:T(128)S(1)}, f32[128]{0:T(128)}, u32[]{:S(2)}) copy-start(f32[128]{0:T(128)} %param.22) | copy-start | bytes 1540
  84.7 1.6 copy-start.10
  86.2 1.6 copy-start.3
  86.3 1.6 copy-start.12
  88.6 3.9 %copy-start.6 = (bf16[8192,128]{1,0:T(8,128)(2,1)}, bf16[8192,128]{1,0:T(8,128)(2,1)S(1)}, u32[]{:S(2)}) copy-start(bf16[8192,128]{1,0:T(8,128)(2,1)S(1)} %fusion.1) | copy-start | bytes 6291460
  90.4 1.4 copy-start.5
  90.4 5.0 %slice-start = ((s8[8388608]{0:T(1024)(128)(4,1)}), s8[4194304]{0:T(1024)(128)(4,1)S(1)}, s32[]{:S(2)}) async-start(s8[8388608]{0:T(1024)(128)(4,1)} %bitcast.92), calls=%async_computation.3 | async-start | bytes 8388608
  91.8 3.7 %slice-start.1 = ((s8[8388608]{0:T(1024)(128)(4,1)}), s8[4194304]{0:T(1024)(128)(4,1)S(1)}, s32[]{:S(2)}) async-start(s8[8388608]{0:T(1024)(128)(4,1)} %bitcast.92), calls=%async_computation.4 | async-start | bytes 8388608
  123.6 53.6 %copy-start.4 = (bf16[1,8192,128]{2,1,0:T(8,128)(2,1)S(1)}, bf16[1,8192,128]{2,1,0:T(8,128)(2,1)}, u32[]{:S(2)}) copy-start(bf16[1,8192,128]{2,1,0:T(8,128)(2,1)} %param.14) | copy-start | bytes 6291460
  173.2 6.3 %copy-start.2 = (f32[68,128,128]{2,1,0:T(8,128)S(1)}, f32[68,128,128]{2,1,0:T(8,128)}, u32[]{:S(2)}) copy-start(f32[68,128,128]{2,1,0:T(8,128)} %scatter_fusion) | copy-start | bytes 13369348
  174.4 13.5 %collective-permute-start.2 = (f32[256,128]{1,0:T(8,128)S(1)}, f32[256,128]{1,0:T(8,128)S(1)}, u32[]{:S(2)}, u32[]{:S(2)}) collective-permute-start(f32[256,128]{1,0:T(8,128)S(1)} %bitcast.106), channel_id=1, source_target_pairs={{0,1},{1,2},{2,3},{3,4},{4,5},{5,6},{6,7},{8,9},{9,10},{10,11},{11... | collective-permute-start | bytes 393224 | tf_op jit(solution)/shard_map/ppermute | solution.py:19
  185.9 6.8 %collective-permute-start.3 = (f32[256,128]{1,0:T(8,128)S(1)}, f32[256,128]{1,0:T(8,128)S(1)}, u32[]{:S(2)}, u32[]{:S(2)}) collective-permute-start(f32[256,128]{1,0:T(8,128)S(1)} %bitcast.105), channel_id=1, source_target_pairs={{1,0},{2,1},{3,2},{4,3},{5,4},{6,5},{7,6},{9,8},{10,9},{11,10},{12... | collective-permute-start | bytes 393224 | tf_op jit(solution)/shard_map/ppermute | solution.py:22
  198.0 133.2 %copy-start.1 = (bf16[1,64,128,128]{3,2,1,0:T(8,128)(2,1)S(1)}, bf16[1,64,128,128]{3,2,1,0:T(8,128)(2,1)}, u32[]{:S(2)}) copy-start(bf16[1,64,128,128]{3,2,1,0:T(8,128)(2,1)} %param.18) | copy-start | bytes 6291460
  198.0 131.7 %reduce-scatter.2.cloned.1.call-start = ((), (), s32[]{:S(2)}) async-start(), calls=%async_computation.1 | async-start | bytes 589824 | tf_op jit(solution)/shard_map/reduce_scatter | solution.py:66
Sparse Core Ops, SparseCore 0:
  198.1 127.6 all-reduce.2
Sparse Core Ops, SparseCore 1:
  201.8 62.8 reduce-scatter.1
where the time goes:
time: 340 us; the launch traced here: 339 us
  waiting for transfers between devices  88.7 us (26%)
  blocking collectives  72.9 us (21%)
  other arithmetic  62.7 us (18%)
  matrix products  45.2 us (13%)
  local copies, waits for them, and re-layouts  43 us (13%)
  between operations  15.8 us (5%)
  starting transfers between devices  10.3 us (3%)
    psum x1, waiting for transfers between devices, on_device(): lax.psum((grad_msg, grad_in, grad_bias, grad_out), ('design', 'graph'))  84.4 us
    scatter-add x1, other arithmetic, on_device(): grad_ext = jnp.zeros((count + 2 * HT, TILE, H), jnp.float32).at[source.re...  49.6 us
    psum x1, blocking collectives, on_device(): lax.psum((grad_msg, grad_in, grad_bias, grad_out), ('design', 'graph'))  39.8 us
    all_gather x1, blocking collectives, on_device(): lax.all_gather(cot_tile, 'graph', axis=0, tiled=True)  33.1 us
    reshape x1, local copies, waits for them, and re-layouts, on_device(): returned.reshape(count * NBR, TILE, H)  17.4 us
    gather x1, local copies, waits for them, and re-layouts, on_device(): picked = extended[source]  10.3 us
    dot_general x1, matrix products, on_device(): jnp.einsum('tkij,tkjh->tih', edge_w, picked, preferred_element_type=jnp.f...  8.25 us
    dot_general x1, matrix products, on_device(): jnp.einsum('tkij,tih->tkjh', edge_w, grad_agg, preferred_element_type=jnp...  8.12 us
  transfers between devices with their start and end apart: 6, of which 2 were waited for; matrix products, arithmetic and copies ran while one was open for 8% of the time, Pallas kernels for 0%

commit v1 on v0

v1 whole, which is shorter than its diff:
```python
import math

import jax
import jax.numpy as jnp
from jax import lax
from jax.experimental import pallas as pl
from jax.experimental.pallas import tpu as pltpu
from jax.sharding import PartitionSpec as P

H = 128
TILE = 128
NBR = 4
HT = 2
STEPS = 8
F32 = jnp.float32
BF16 = jnp.bfloat16


def dot(a, b, ca=1, cb=0):
    return lax.dot_general(a, b, (((ca,), (cb,)), ((), ())), preferred_element_type=F32)


def split(x):
    hi = x.astype(BF16)
    return hi, (x - hi.astype(F32)).astype(BF16)


def bit_order(count):
    bits = count.bit_length() - 1
    return [sum(((q >> b) & 1) << (bits - 1 - b) for b in range(bits)) for q in range(count)]


def exchange(x, axis, mask):
    return lax.ppermute(x, axis, [(i, i ^ mask) for i in range(lax.axis_size(axis))])


def forward_tiles(per, first, src, dst, me, ext, adj, pw, wcat, bias, a_out, d_out, acc):
    rows = per * TILE
    for j in range(per):
        t = first + j
        picked = [
            ext[pl.ds(pl.multiple_of(src[t, k] * TILE, TILE), TILE), :] for k in range(NBR)
        ]
        weights = jnp.concatenate([adj[j, k] for k in range(NBR)], axis=1)
        summed = dot(weights, jnp.concatenate(picked, axis=0))
        a_out[pl.ds(j * TILE, TILE), :] = summed.astype(BF16)
    own = ext[pl.ds(pl.multiple_of((first + HT) * TILE, TILE), rows), :]
    both = jnp.concatenate([own, a_out[...]], axis=1)
    pre = dot(both, wcat[...]) + bias[...]
    sig = 0.5 * jnp.tanh(0.5 * pre) + 0.5
    act = (pre * sig).astype(BF16)
    d_out[...] = sig * (1.0 + pre * (1.0 - sig))
    for j in range(per):
        part = slice(j * TILE, (j + 1) * TILE)
        term = dot(pw[j], jnp.concatenate([own[part], act[part]], axis=1))
        slot = dst[first + j, 0] ^ me
        acc[slot] += term


def join_weights(w_msg, w_in, wcat):
    wcat[:H] = w_in[:H]
    wcat[H:] = dot(w_msg[...], w_in[H:]).astype(BF16)


def inner_kernel(
    per, base, src, dst, nodes, adj, pw, w_msg, w_in, bias, a_out, d_out, acc, ext, wcat, sem
):
    i = pl.program_id(0)
    me = lax.axis_index("graph")
    total = nodes.shape[0]

    @pl.when(i == 0)
    def _():
        copy = pltpu.make_async_copy(nodes, ext.at[pl.ds(HT * TILE, total)], sem)
        copy.start()
        join_weights(w_msg, w_in, wcat)
        acc[...] = jnp.zeros_like(acc)
        copy.wait()

    forward_tiles(
        per, (base + i) * per, src, dst, me, ext, adj, pw, wcat, bias, a_out, d_out, acc
    )


def outer_kernel(
    per, steps, order, src, dst, nodes, near, far, adj, pw, w_msg, w_in, bias, w_out,
    acc_in, a_in, d_in, a_out, d_out, p_out, send, keep, ext, wcat, acc, sem,
):
    i = pl.program_id(0)
    me = lax.axis_index("graph")
    total = nodes.shape[0]
    margin = HT * TILE

    @pl.when(i == 0)
    def _():
        odd = me & 1
        right = margin + total
        near_at = pl.multiple_of((1 - odd) * right, TILE)
        far_at = pl.multiple_of(odd * right, TILE)
        copies = [
            pltpu.make_async_copy(nodes, ext.at[pl.ds(margin, total)], sem.at[0]),
            pltpu.make_async_copy(near, ext.at[pl.ds(near_at, margin)], sem.at[1]),
            pltpu.make_async_copy(far, ext.at[pl.ds(far_at, margin)], sem.at[2]),
        ]
        for copy in copies:
            copy.start()
        join_weights(w_msg, w_in, wcat)
        acc[...] = acc_in[...]
        for copy in copies:
            copy.wait()

    block = outer_block(i, steps)
    forward_tiles(per, block * per, src, dst, me, ext, adj, pw, wcat, bias, a_out, d_out, acc)

    @pl.when(i == pl.num_programs(0) - 1)
    def _():
        count = len(order)
        for q, r in enumerate(order):
            p_sum = acc[r, :, H:]
            p_out[r] = p_sum
            hi, lo = split(p_sum)
            whole = acc[r, :, :H] + dot(hi, w_out[...]) + dot(lo, w_out[...])
            if q < count // 2:
                keep[q] = whole
            else:
                send[q - count // 2] = whole.astype(BF16)


def outer_block(i, steps):
    return jnp.where(i < steps // 4, i, i + steps // 2)


def backward_kernel(per, levels, dst, *refs):
    cots = refs[:levels]
    nodes, a_in, d_in, pw, p_in, w_out, out, cot_w, total = refs[levels:]
    i = pl.program_id(0)
    me = lax.axis_index("graph")

    @pl.when(i == 0)
    def _():
        grad_out = jnp.zeros((H, H), F32)
        at = 0
        for cot in cots:
            for j in range(cot.shape[0] // TILE):
                tile = cot[j * TILE : (j + 1) * TILE, :]
                cot_w[at] = dot(tile, w_out[...], 1, 1).astype(BF16)
                hi, lo = split(p_in[at])
                grad_out += dot(hi, tile, 0, 0) + dot(lo, tile, 0, 0)
                at += 1
        out[:H] = grad_out.astype(out.dtype)
        total[...] = jnp.zeros_like(total)

    parts = []
    for j in range(per):
        slot = dst[i * per + j, 0] ^ me
        grad_act = dot(pw[j], cot_w[slot], 0, 0)
        parts.append((grad_act * d_in[j * TILE : (j + 1) * TILE, :]).astype(BF16))
    grad_pre = jnp.concatenate(parts, axis=0)
    total[:H] += dot(grad_pre, jnp.concatenate([nodes[...], a_in[...]], axis=1), 0, 0)
    total[H:, :H] += jnp.sum(grad_pre.astype(F32).reshape(-1, 8, H), axis=0)

    @pl.when(i == pl.num_programs(0) - 1)
    def _():
        out[H : 2 * H] = total[:H, :H].astype(out.dtype)
        out[2 * H : 3 * H] = total[:H, H:].astype(out.dtype)
        row = jnp.sum(total[H:, :H], axis=0, keepdims=True)
        first = lax.broadcasted_iota(jnp.int32, (16, H), 0) == 0
        out[3 * H :] = jnp.where(first, row, 0.0).astype(out.dtype)


def finish_kernel(scale, mine, other, w_msg, w_in, g_msg, g_in, g_bias, g_out):
    sums = (mine[...].astype(F32) + other[...].astype(F32)) * scale
    g_out[...] = sums[:H]
    g_in[:H] = sums[H : 2 * H].T
    hi, lo = split(sums[2 * H : 3 * H])
    g_in[H:] = dot(w_msg[...], hi, 0, 1) + dot(w_msg[...], lo, 0, 1)
    w_low = w_in[H:]
    g_msg[...] = dot(hi, w_low, 0, 1) + dot(lo, w_low, 0, 1)
    g_bias[...] = sums[3 * H : 3 * H + 1]


def on_device(
    nodes, adjacency, tile_src, pool_dst, pool_weight, coarse_cot, w_msg, w_in, b_in, w_out
):
    feats = nodes[0]
    adj = adjacency[0]
    src = tile_src[0]
    dst = pool_dst[0]
    pw = pool_weight[0]
    cot = coarse_cot[0]
    rows = feats.shape[0]
    count = rows // TILE
    slabs = lax.axis_size("graph")
    designs = lax.axis_size("design")
    assert slabs & (slabs - 1) == 0 and designs & (designs - 1) == 0 and slabs > 1
    steps = STEPS
    assert count % steps == 0 and steps % 4 == 0
    per = count // steps
    block = per * TILE
    levels = slabs.bit_length()
    margin = HT * TILE
    bias = b_in.reshape(1, H)

    odd = lax.axis_index("graph") & 1
    first, last = feats[:margin], feats[rows - margin :]
    near_send = jnp.where(odd == 0, last, first)
    far_send = jnp.where(odd == 0, first, last)
    near_msg = exchange(jnp.concatenate([cot, near_send], axis=0), "graph", 1)
    across = [(i, i + 1) for i in range(1, slabs - 1, 2)]
    far = lax.ppermute(far_send, "graph", across + [(b, a) for a, b in across])
    near = near_msg[TILE:]
    cots = [cot, near_msg[:TILE]]
    for level in range(1, levels - 1):
        cots.append(exchange(jnp.concatenate(cots, axis=0), "graph", 1 << level))

    smem = pl.BlockSpec(memory_space=pltpu.SMEM)
    vmem = pl.BlockSpec(memory_space=pltpu.VMEM)
    hbm = pl.BlockSpec(memory_space=pl.ANY)
    acc_shape = (slabs, TILE, 2 * H)
    base = steps // 4
    params = pltpu.CompilerParams(
        dimension_semantics=("arbitrary",), vmem_limit_bytes=40 * 1024 * 1024
    )

    def tiles(where):
        return pl.BlockSpec((per, TILE, TILE), lambda i: (where(i), 0, 0))

    def edges(where):
        return pl.BlockSpec((per, NBR, TILE, TILE), lambda i: (where(i), 0, 0, 0))

    def row_block(where):
        return pl.BlockSpec((block, H), lambda i: (where(i), 0))

    inner = lambda i: i + base
    a_mid, d_mid, acc_mid = pl.pallas_call(
        lambda *refs: inner_kernel(per, base, *refs),
        grid=(steps // 2,),
        in_specs=[smem, smem, hbm, edges(inner), tiles(inner), vmem, vmem, vmem],
        out_specs=[row_block(inner), row_block(inner), vmem],
        out_shape=[
            jax.ShapeDtypeStruct((rows, H), BF16),
            jax.ShapeDtypeStruct((rows, H), F32),
            jax.ShapeDtypeStruct(acc_shape, F32),
        ],
        scratch_shapes=[
            pltpu.VMEM((rows + 2 * margin, H), BF16),
            pltpu.VMEM((2 * H, H), BF16),
            pltpu.SemaphoreType.DMA,
        ],
        compiler_params=params,
        cost_estimate=pl.CostEstimate(
            flops=8 * rows * H * H, bytes_accessed=rows * H * 9, transcendentals=rows * H // 2
        ),
        name="inner",
    )(src, dst, feats, adj, pw, w_msg, w_in, bias)

    order = bit_order(slabs)
    outer = lambda i: outer_block(i, steps)
    half = (slabs // 2, TILE, H)
    a_all, d_all, p_all, send, keep = pl.pallas_call(
        lambda *refs: outer_kernel(per, steps, order, *refs),
        grid=(steps // 2,),
        in_specs=[
            smem, smem, hbm, hbm, hbm, edges(outer), tiles(outer), vmem, vmem, vmem, vmem,
            vmem, hbm, hbm,
        ],
        out_specs=[row_block(outer), row_block(outer), vmem, vmem, vmem],
        out_shape=[
            jax.ShapeDtypeStruct((rows, H), BF16),
            jax.ShapeDtypeStruct((rows, H), F32),
            jax.ShapeDtypeStruct((slabs, TILE, H), F32),
            jax.ShapeDtypeStruct(half, BF16),
            jax.ShapeDtypeStruct(half, F32),
        ],
        scratch_shapes=[
            pltpu.VMEM((rows + 2 * margin, H), BF16),
            pltpu.VMEM((2 * H, H), BF16),
            pltpu.VMEM(acc_shape, F32),
            pltpu.SemaphoreType.DMA((3,)),
        ],
        input_output_aliases={12: 0, 13: 1},
        compiler_params=params,
        cost_estimate=pl.CostEstimate(
            flops=8 * rows * H * H, bytes_accessed=rows * H * 9, transcendentals=rows * H // 2
        ),
        name="outer",
    )(src, dst, feats, near, far, adj, pw, w_msg, w_in, bias, w_out, acc_mid, a_mid, d_mid)

    same = lambda i: i
    partial = pl.pallas_call(
        lambda *refs: backward_kernel(per, levels, *refs),
        grid=(steps,),
        in_specs=[smem] + [vmem] * levels
        + [row_block(same), row_block(same), row_block(same), tiles(same), vmem, vmem],
        out_specs=vmem,
        out_shape=jax.ShapeDtypeStruct((3 * H + 16, H), BF16),
        scratch_shapes=[
            pltpu.VMEM((slabs, TILE, H), BF16),
            pltpu.VMEM((H + 8, 2 * H), F32),
        ],
        compiler_params=params,
        cost_estimate=pl.CostEstimate(
            flops=6 * rows * H * H, bytes_accessed=rows * H * 10, transcendentals=0
        ),
        name="backward",
    )(dst, *cots, feats, a_all, d_all, pw, p_all, w_out)

    got = exchange(send, "graph", 1)
    held = keep + got.astype(F32)
    mask = 2
    while mask < slabs:
        size = held.shape[0] // 2
        got = exchange(held[size:].astype(BF16), "graph", mask)
        held = held[:size] + got.astype(F32)
        mask *= 2
    coarse = held[0].astype(BF16)

    rounds = [("design", 1 << b) for b in range(designs.bit_length() - 1)]
    rounds += [("graph", 1 << b) for b in range(slabs.bit_length() - 1)]
    mine = partial
    for axis, mask in rounds[:-1]:
        mine = (mine.astype(F32) + exchange(mine, axis, mask).astype(F32)).astype(BF16)
    other = exchange(mine, *rounds[-1])
    scale = 1.0 / math.sqrt(designs * rows * slabs)
    g_msg, g_in, g_bias, g_out = pl.pallas_call(
        lambda *refs: finish_kernel(scale, *refs),
        in_specs=[vmem] * 4,
        out_specs=[vmem] * 4,
        out_shape=[
            jax.ShapeDtypeStruct((H, H), F32),
            jax.ShapeDtypeStruct((2 * H, H), F32),
            jax.ShapeDtypeStruct((1, H), F32),
            jax.ShapeDtypeStruct((H, H), F32),
        ],
        name="finish",
    )(mine, other, w_msg, w_in)

    size = rows // steps

    def fine_kernel(nodes_ref, a_ref, w_msg_ref, w_in_ref, bias_ref, w_out_ref, out, wcat):
        @pl.when(pl.program_id(0) == 0)
        def _():
            join_weights(w_msg_ref, w_in_ref, wcat)

        own = nodes_ref[...]
        pre = dot(jnp.concatenate([own, a_ref[...]], axis=1), wcat[...]) + bias_ref[...]
        act = (pre * (0.5 * jnp.tanh(0.5 * pre) + 0.5)).astype(BF16)
        out[...] = (own.astype(F32) + dot(act, w_out_ref[...])).astype(BF16)

    fine = pl.pallas_call(
        fine_kernel,
        grid=(steps,),
        in_specs=[row_block(same), row_block(same), vmem, vmem, vmem, vmem],
        out_specs=row_block(same),
        out_shape=jax.ShapeDtypeStruct((rows, H), BF16),
        scratch_shapes=[pltpu.VMEM((2 * H, H), BF16)],
        compiler_params=params,
        cost_estimate=pl.CostEstimate(
            flops=6 * rows * H * H, bytes_accessed=rows * H * 6, transcendentals=rows * H
        ),
        name="fine",
    )(feats, a_all, w_msg, w_in, bias, w_out)
    return fine[None], coarse[None], g_msg, g_in, g_bias.reshape(H), g_out


def solution(mesh):
    in_specs = (
        P("design", "graph", None),
        P("design", "graph", None, None, None),
        P("design", "graph", None),
        P("design", "graph", None),
        P("design", "graph", None, None),
        P("design", "graph", None),
        P(),
        P(),
        P(),
        P(),
    )
    out_specs = (P("design", "graph", None), P("design", "graph", None), P(), P(), P(), P())
    return jax.shard_map(
        on_device, mesh=mesh, in_specs=in_specs, out_specs=out_specs, check_vma=False
    )
```

time: 340 us -> 71.3 us (0.21)
  waiting for transfers between devices: 88.7 us -> 11.9 us
  blocking collectives: 72.9 us -> 0 us
  other arithmetic: 62.7 us -> 3.98 us
  matrix products: 45.2 us -> 0 us
  local copies, waits for them, and re-layouts: 43 us -> 7.65 us
  Pallas kernels: 0 us -> 25.6 us
  between operations: 15.8 us -> 0.84 us
  starting transfers between devices: 10.3 us -> 20.6 us
    psum x1 -> x0, waiting for transfers between devices: 84.4 us -> none  [on_device(): lax.psum((grad_msg, grad_in, grad_bias, grad_out), ('design', 'graph'))]
    scatter-add x3 -> x0, other arithmetic: 51.9 us -> none  [the longest x1 49.6 us: on_device(): grad_ext = jnp.zeros((count + 2 * HT, TILE, H), jnp.float32).at[source.re...]
    dot_general x16 -> x0, matrix products: 45.2 us -> none  [the longest x1 8.25 us: on_device(): jnp.einsum('tkij,tkjh->tih', edge_w, picked, preferred_element_type=jnp.f...]
    psum x1 -> x0, blocking collectives: 39.8 us -> none  [on_device(): lax.psum((grad_msg, grad_in, grad_bias, grad_out), ('design', 'graph'))]
    all_gather x1 -> x0, blocking collectives: 33.1 us -> none  [on_device(): lax.all_gather(cot_tile, 'graph', axis=0, tiled=True)]
    pallas_call x0 -> x5, Pallas kernels: none -> 25.6 us  [the longest x1 6.46 us: on_device(): pl.pallas_call(lambda *refs: outer_kernel(per, steps, order, *refs), grid...]
    reshape x1 -> x0, local copies, waits for them, and re-layouts: 17.4 us -> none  [on_device(): returned.reshape(count * NBR, TILE, H)]
    ppermute x4 -> x12, starting transfers between devices: 10.2 us -> 20.6 us  [the longest x11 19.9 us: exchange(): lax.ppermute(x, axis, [(i, i ^ mask) for i in range(lax.axis_size(axis))])]
  transfers between devices with their start and end apart: 6 -> 12, of which waited for: 2 -> 7; matrix products, arithmetic and copies ran while one was open for 8% -> 4% of each run, Pallas kernels for 0% -> 25%
where the time goes in v1:
time: 71.3 us; the launch traced here: 70.6 us
  Pallas kernels  25.6 us (36%)
  starting transfers between devices  20.6 us (29%)
  waiting for transfers between devices  11.9 us (17%)
  local copies, waits for them, and re-layouts  7.65 us (11%)
  other arithmetic  3.98 us (6%)
  between operations  0.84 us (1%)
    ppermute x11, starting transfers between devices, exchange(): lax.ppermute(x, axis, [(i, i ^ mask) for i in range(lax.axis_size(axis))])  19.9 us
    ppermute x11, waiting for transfers between devices, exchange(): lax.ppermute(x, axis, [(i, i ^ mask) for i in range(lax.axis_size(axis))])  11.9 us
    unnamed x25, local copies, waits for them, and re-layouts  6.88 us
    pallas_call x1, Pallas kernels, on_device(): pl.pallas_call(lambda *refs: outer_kernel(per, steps, order, *refs), grid...  6.46 us
    pallas_call x1, Pallas kernels, on_device(): pl.pallas_call(lambda *refs: inner_kernel(per, base, *refs), grid=(steps...  5.9 us
    pallas_call x1, Pallas kernels, on_device(): pl.pallas_call(lambda *refs: backward_kernel(per, levels, *refs), grid=(s...  5.8 us
    pallas_call x1, Pallas kernels, on_device(): pl.pallas_call(fine_kernel, grid=(steps,), in_specs=[row_block(same), row...  5.61 us
    pallas_call x1, Pallas kernels, on_device(): pl.pallas_call(lambda *refs: finish_kernel(scale, *refs), in_specs=[vmem]...  1.86 us
  transfers between devices with their start and end apart: 12, of which 7 were waited for; matrix products, arithmetic and copies ran while one was open for 4% of the time, Pallas kernels for 25%

profile of v1, /device:TPU:0, one launch (start us, length us, event | category | flops | bytes accessed | tf_op | source)
XLA Modules:
  0.0 70.6 jit_solution(5391357401691115694)
XLA Ops:
  0.6 0.9 %select_bitcast_fusion = (bf16[256,128]{1,0:T(8,128)(2,1)S(1)}, bf16[256,128]{1,0:T(8,128)(2,1)S(1)}) fusion(pred[]{:T(512)S(6)} %eq.4, bf16[1,8192,128]{2,1,0:T(8,128)(2,1)} %param.10), kind=kLoop, calls=%fused_computation.13 | loop fusion | flops 65536 | bytes 262145 | tf_op jit(solution)/shard_map/jit(_where)/select_n | solution.py:207
  1.5 0.8 %pad_maximum_fusion.1 = bf16[384,128]{1,0:T(8,128)(2,1)S(1)} fusion(bf16[256,128]{1,0:T(8,128)(2,1)S(1)} %get-tuple-element.31, bf16[128,128]{1,0:T(8,128)(2,1)} %bitcast.20), kind=kLoop, calls=%fused_computation.8 | loop fusion | flops 196608 | bytes 196608 | tf_op jit(solution)/shard_map/concatenate | solution.py:208
  2.3 3.0 %collective-permute-start = (bf16[384,128]{1,0:T(8,128)(2,1)S(1)}, bf16[384,128]{1,0:T(8,128)(2,1)S(1)}, u32[]{:S(2)}, u32[]{:S(2)}) collective-permute-start(bf16[384,128]{1,0:T(8,128)(2,1)S(1)} %pad_maximum_fusion.1), channel_id=1, source_target_pairs={{0,1},{1,0},{2,3},{3,2},{4,5},{5,4},{6,7},{7,6},{8,9},{9,8},{10,11... | collective-permute-start | bytes 294920 | tf_op jit(solution)/shard_map/ppermute | solution.py:34
  5.3 2.8 %collective-permute-done = bf16[384,128]{1,0:T(8,128)(2,1)S(1)} collective-permute-done((bf16[384,128]{1,0:T(8,128)(2,1)S(1)}, bf16[384,128]{1,0:T(8,128)(2,1)S(1)}, u32[]{:S(2)}, u32[]{:S(2)}) %collective-permute-start) | collective-permute-done | bytes 98336 | tf_op jit(solution)/shard_map/ppermute | solution.py:34
  8.1 0.8 %pad_maximum_fusion.2 = bf16[256,128]{1,0:T(8,128)(2,1)S(1)} fusion(bf16[128,128]{1,0:T(8,128)(2,1)S(1)} %slice.41.refs_2_, bf16[128,128]{1,0:T(8,128)(2,1)} %bitcast.21), kind=kLoop, calls=%fused_computation.12 | loop fusion | flops 131072 | bytes 131072 | tf_op jit(solution)/shard_map/concatenate | solution.py:214
  8.8 1.9 %collective-permute-start.5 = (bf16[256,128]{1,0:T(8,128)(2,1)S(1)}, bf16[256,128]{1,0:T(8,128)(2,1)S(1)}, u32[]{:S(2)}, u32[]{:S(2)}) collective-permute-start(bf16[256,128]{1,0:T(8,128)(2,1)S(1)} %pad_maximum_fusion.2), channel_id=1, source_target_pairs={{0,2},{1,3},{2,0},{3,1},{4,6},{5,7},{6,4},{7,5},{8,10},{9,11},{10,... | collective-permute-start | bytes 196616 | tf_op jit(solution)/shard_map/ppermute | solution.py:34
  10.7 0.7 collective-permute-start.1
  11.4 0.7 %copy.20.refs_1_.refs_0_ = s32[64,1]{1,0:T(8,128)S(1)} copy(s32[64,1]{0,1:T(1,128)} %bitcast.32) | data formatting | bytes 512 | tf_op jit(solution)/shard_map/squeeze | solution.py:188
  12.1 0.8 %copy.18 = s32[1,64,4]{2,1,0:T(8,128)S(1)} copy(s32[1,64,4]{1,2,0:T(4,128)} %param.12) | data formatting | bytes 2048 | tf_op args[2]
  13.1 0.8 %pad_maximum_fusion = bf16[512,128]{1,0:T(8,128)(2,1)S(1)} fusion(bf16[256,128]{1,0:T(8,128)(2,1)S(1)} %collective-permute-done.5.refs_3_, bf16[128,128]{1,0:T(8,128)(2,1)S(1)} %slice.41.refs_2_, bf16[128,128]{1,0:T(8,128)(2,1)} %bitcast.22), kind=kLoop, calls=%fused_computation.7 | loop fusion | flops 393216 | bytes 262144 | tf_op jit(solution)/shard_map/concatenate | solution.py:214
  13.9 4.0 %collective-permute-start.6 = (bf16[512,128]{1,0:T(8,128)(2,1)S(1)}, bf16[512,128]{1,0:T(8,128)(2,1)S(1)}, u32[]{:S(2)}, u32[]{:S(2)}) collective-permute-start(bf16[512,128]{1,0:T(8,128)(2,1)S(1)} %pad_maximum_fusion), channel_id=1, source_target_pairs={{0,4},{1,5},{2,6},{3,7},{4,0},{5,1},{6,2},{7,3},{8,12},{9,13},{10,... | collective-permute-start | bytes 393224 | tf_op jit(solution)/shard_map/ppermute | solution.py:34
  17.9 1.6 %copy-done = bf16[1,8192,128]{2,1,0:T(8,128)(2,1)S(1)} copy-done((bf16[1,8192,128]{2,1,0:T(8,128)(2,1)S(1)}, bf16[1,8192,128]{2,1,0:T(8,128)(2,1)}, u32[]{:S(2)}) %copy-start) | copy-done | bytes 2097176
  19.5 1.6 %copy-done.2 = bf16[1,64,128,128]{3,2,1,0:T(8,128)(2,1)S(1)} copy-done((bf16[1,64,128,128]{3,2,1,0:T(8,128)(2,1)S(1)}, bf16[1,64,128,128]{3,2,1,0:T(8,128)(2,1)}, u32[]{:S(2)}) %copy-start.2) | copy-done | bytes 2097176
  21.0 0.8 %copy-done.4 = bf16[256,128]{1,0:T(8,128)(2,1)S(1)} copy-done((bf16[256,128]{1,0:T(8,128)(2,1)S(1)}, bf16[256,128]{1,0:T(8,128)(2,1)}, u32[]{:S(2)}) %copy-start.4) | copy-done | bytes 65560
  21.9 0.8 %copy-done.6 = bf16[128,128]{1,0:T(8,128)(2,1)S(1)} copy-done((bf16[128,128]{1,0:T(8,128)(2,1)S(1)}, bf16[128,128]{1,0:T(8,128)(2,1)}, u32[]{:S(2)}) %copy-start.6) | copy-done | bytes 32792
  22.6 0.7 copy-done.9
  23.3 5.9 %inner.1 = (bf16[8192,128]{1,0:T(8,128)(2,1)S(1)}, f32[8192,128]{1,0:T(8,128)S(1)}, f32[8,128,256]{2,1,0:T(8,128)S(1)}) custom-call(s32[64,4]{1,0:T(8,128)S(1)} %bitcast.24, s32[64,1]{1,0:T(8,128)S(1)} %copy.20.refs_1_.refs_0_, bf16[8192,128]{1,0:T(8,128)(2,1)S(1)} %bitcast.13, bf16[64,4,128,128]{3,2,1,0:T(8,128)(2,1)} %bitcast.29, ...), custom_call_target="tpu_custom_call" | custom-call | flops 1073741824 | bytes 9437184 | tf_op jit(solution)/shard_map/inner/pallas_call | solution.py:235
  29.3 6.5 %outer.1 = (bf16[8192,128]{1,0:T(8,128)(2,1)S(1)}, f32[8192,128]{1,0:T(8,128)S(1)}, f32[8,128,128]{2,1,0:T(8,128)S(1)}, bf16[4,128,128]{2,1,0:T(8,128)(2,1)S(1)}, f32[4,128,128]{2,1,0:T(8,128)S(1)}) custom-call(s32[64,4]{1,0:T(8,128)S(1)} %bitcast.25, s32[64,1]{1,0:T(8,128)S(1)} %copy.20.refs_1_.refs_0_, ...), custom_call_target="tpu_custom_call", output_to_operand_aliasing={{0}: (12, {}), {1}: (13, {})} | custom-call | flops 1073741824 | bytes 9437184 | tf_op jit(solution)/shard_map/outer/pallas_call | solution.py:260
  35.8 5.8 %backward.1 = bf16[400,128]{1,0:T(8,128)(2,1)S(1)} custom-call(s32[64,1]{1,0:T(8,128)S(1)} %copy.20.refs_1_.refs_0_, bf16[128,128]{1,0:T(8,128)(2,1)S(1)} %bitcast.23, bf16[128,128]{1,0:T(8,128)(2,1)S(1)} %slice.41.refs_2_, bf16[256,128]{1,0:T(8,128)(2,1)S(1)} %collective-permute-done.5.refs_3_, bf16[512,128]{1,0:T(8,128)(2,1)S(1)} %collective-permute-done.6.refs_4_, ...), custom_call_target="tpu_custom_call" | custom-call | flops 805306368 | bytes 10485760 | tf_op jit(solution)/shard_map/backward/pallas_call | solution.py:290
  41.7 1.3 %collective-permute-done.7 = bf16[400,128]{1,0:T(8,128)(2,1)S(1)} collective-permute-done((bf16[400,128]{1,0:T(8,128)(2,1)S(1)}, bf16[400,128]{1,0:T(8,128)(2,1)S(1)}, u32[]{:S(2)}, u32[]{:S(2)}) %collective-permute-start.7) | collective-permute-done | bytes 102432 | tf_op jit(solution)/shard_map/ppermute | solution.py:34
  43.0 1.6 %collective-permute-start.8 = (bf16[400,128]{1,0:T(8,128)(2,1)S(1)}, bf16[400,128]{1,0:T(8,128)(2,1)S(1)}, u32[]{:S(2)}, u32[]{:S(2)}) collective-permute-start(bf16[400,128]{1,0:T(8,128)(2,1)S(1)} %add_convert_fusion.3), channel_id=1, source_target_pairs={{0,16},{8,24},{16,0},{24,8},{1,17},{9,25},{17,1},{25,9},{2,18},{10... | collective-permute-start | bytes 307208 | tf_op jit(solution)/shard_map/ppermute | solution.py:34
  44.6 1.6 %collective-permute-start.2 = (bf16[4,128,128]{2,1,0:T(8,128)(2,1)S(1)}, bf16[4,128,128]{2,1,0:T(8,128)(2,1)S(1)}, u32[]{:S(2)}, u32[]{:S(2)}) collective-permute-start(bf16[4,128,128]{2,1,0:T(8,128)(2,1)S(1)} %get-tuple-element.23), channel_id=1, source_target_pairs={{0,1},{1,0},{2,3},{3,2},{4,5},{5,4},{6,7},{7,6},{8,9},{9,8},{10,11... | collective-permute-start | bytes 393224 | tf_op jit(solution)/shard_map/ppermute | solution.py:34
  46.2 5.6 %fine.1 = bf16[8192,128]{1,0:T(8,128)(2,1)} custom-call(bf16[8192,128]{1,0:T(8,128)(2,1)S(1)} %bitcast.16, bf16[8192,128]{1,0:T(8,128)(2,1)S(1)} %get-tuple-element.21.a_ref.refs_6_, bf16[128,128]{1,0:T(8,128)(2,1)S(1)} %copy-done.6, bf16[256,128]{1,0:T(8,128)(2,1)S(1)} %copy-done.5, f32[1,128]{1,0:T(1,128)S(1)} %bitcast.28, bf16[128,128]{1,0:T(8,128)(2,1)S(1)} %copy-done.8), custom_call_target="tpu_custom_call" | custom-call | flops 805306368 | bytes 6291456 | tf_op jit(solution)/shard_map/fine/pallas_call | solution.py:350
  52.4 2.8 %collective-permute-start.3 = (bf16[2,128,128]{2,1,0:T(8,128)(2,1)S(1)}, bf16[2,128,128]{2,1,0:T(8,128)(2,1)S(1)}, u32[]{:S(2)}, u32[]{:S(2)}) collective-permute-start(bf16[2,128,128]{2,1,0:T(8,128)(2,1)S(1)} %slice.52), channel_id=1, source_target_pairs={{0,2},{1,3},{2,0},{3,1},{4,6},{5,7},{6,4},{7,5},{8,10},{9,11},{10,... | collective-permute-start | bytes 196616 | tf_op jit(solution)/shard_map/ppermute | solution.py:34
  55.1 1.4 %collective-permute-done.9 = bf16[400,128]{1,0:T(8,128)(2,1)S(1)} collective-permute-done((bf16[400,128]{1,0:T(8,128)(2,1)S(1)}, bf16[400,128]{1,0:T(8,128)(2,1)S(1)}, u32[]{:S(2)}, u32[]{:S(2)}) %collective-permute-start.9) | collective-permute-done | bytes 102432 | tf_op jit(solution)/shard_map/ppermute | solution.py:34
  56.6 1.1 %collective-permute-start.10 = (bf16[400,128]{1,0:T(8,128)(2,1)S(1)}, bf16[400,128]{1,0:T(8,128)(2,1)S(1)}, u32[]{:S(2)}, u32[]{:S(2)}) collective-permute-start(bf16[400,128]{1,0:T(8,128)(2,1)S(1)} %add_convert_fusion.1), channel_id=1, source_target_pairs={{0,2},{1,3},{2,0},{3,1},{4,6},{5,7},{6,4},{7,5},{8,10},{9,11},{10,... | collective-permute-start | bytes 307208 | tf_op jit(solution)/shard_map/ppermute | solution.py:34
  57.8 2.0 %collective-permute-start.4 = (bf16[1,128,128]{2,1,0:T(8,128)(2,1)S(1)}, bf16[1,128,128]{2,1,0:T(8,128)(2,1)S(1)}, u32[]{:S(2)}, u32[]{:S(2)}) collective-permute-start(bf16[1,128,128]{2,1,0:T(8,128)(2,1)S(1)} %slice.53), channel_id=1, source_target_pairs={{0,4},{1,5},{2,6},{3,7},{4,0},{5,1},{6,2},{7,3},{8,12},{9,13},{10,... | collective-permute-start | bytes 98312 | tf_op jit(solution)/shard_map/ppermute | solution.py:34
  59.8 1.5 %collective-permute-done.10 = bf16[400,128]{1,0:T(8,128)(2,1)S(1)} collective-permute-done((bf16[400,128]{1,0:T(8,128)(2,1)S(1)}, bf16[400,128]{1,0:T(8,128)(2,1)S(1)}, u32[]{:S(2)}, u32[]{:S(2)}) %collective-permute-start.10) | collective-permute-done | bytes 102432 | tf_op jit(solution)/shard_map/ppermute | solution.py:34
  61.4 1.4 %collective-permute-start.11 = (bf16[400,128]{1,0:T(8,128)(2,1)S(1)}, bf16[400,128]{1,0:T(8,128)(2,1)S(1)}, u32[]{:S(2)}, u32[]{:S(2)}) collective-permute-start(bf16[400,128]{1,0:T(8,128)(2,1)S(1)} %add_convert_fusion.refs_0_), channel_id=1, source_target_pairs={{0,4},{1,5},{2,6},{3,7},{4,0},{5,1},{6,2},{7,3},{8,12},{9,13},{10,... | collective-permute-start | bytes 307208 | tf_op jit(solution)/shard_map/ppermute | solution.py:34
  63.6 4.5 %collective-permute-done.11.refs_1_ = bf16[400,128]{1,0:T(8,128)(2,1)S(1)} collective-permute-done((bf16[400,128]{1,0:T(8,128)(2,1)S(1)}, bf16[400,128]{1,0:T(8,128)(2,1)S(1)}, u32[]{:S(2)}, u32[]{:S(2)}) %collective-permute-start.11) | collective-permute-done | bytes 102432 | tf_op jit(solution)/shard_map/ppermute | solution.py:34
  68.1 0.6 copy-done.11
  68.8 1.9 %finish.1 = (f32[128,128]{1,0:T(8,128)}, f32[256,128]{1,0:T(8,128)}, f32[1,128]{1,0:T(1,128)}, f32[128,128]{1,0:T(8,128)}) custom-call(bf16[400,128]{1,0:T(8,128)(2,1)} %copy-done.10, bf16[400,128]{1,0:T(8,128)(2,1)} %copy-done.11, bf16[128,128]{1,0:T(8,128)(2,1)} %refs_2_.1, bf16[256,128]{1,0:T(8,128)(2,1)} %refs_3_.1), custom_call_target="tpu_custom_call" | custom-call | tf_op jit(solution)/shard_map/finish/pallas_call | solution.py:325
  (38 shorter events, 1.8 us)
Async XLA Ops:
  2.3 5.8 %collective-permute-start = (bf16[384,128]{1,0:T(8,128)(2,1)S(1)}, bf16[384,128]{1,0:T(8,128)(2,1)S(1)}, u32[]{:S(2)}, u32[]{:S(2)}) collective-permute-start(bf16[384,128]{1,0:T(8,128)(2,1)S(1)} %pad_maximum_fusion.1), channel_id=1, source_target_pairs={{0,1},{1,0},{2,3},{3,2},{4,5},{5,4},{6,7},{7,6},{8,9},{9,8},{10,11... | collective-permute-start | bytes 294920 | tf_op jit(solution)/shard_map/ppermute | solution.py:34
  8.8 4.3 %collective-permute-start.5 = (bf16[256,128]{1,0:T(8,128)(2,1)S(1)}, bf16[256,128]{1,0:T(8,128)(2,1)S(1)}, u32[]{:S(2)}, u32[]{:S(2)}) collective-permute-start(bf16[256,128]{1,0:T(8,128)(2,1)S(1)} %pad_maximum_fusion.2), channel_id=1, source_target_pairs={{0,2},{1,3},{2,0},{3,1},{4,6},{5,7},{6,4},{7,5},{8,10},{9,11},{10,... | collective-permute-start | bytes 196616 | tf_op jit(solution)/shard_map/ppermute | solution.py:34
  10.7 18.5 %collective-permute-start.1 = (bf16[256,128]{1,0:T(8,128)(2,1)S(1)}, bf16[256,128]{1,0:T(8,128)(2,1)S(1)}, u32[]{:S(2)}, u32[]{:S(2)}) collective-permute-start(bf16[256,128]{1,0:T(8,128)(2,1)S(1)} %get-tuple-element.30), channel_id=1, source_target_pairs={{1,2},{3,4},{5,6},{2,1},{4,3},{6,5},{9,10},{11,12},{13,14},{10,9},... | collective-permute-start | bytes 196616 | tf_op jit(solution)/shard_map/ppermute | solution.py:210
  13.9 21.9 %collective-permute-start.6 = (bf16[512,128]{1,0:T(8,128)(2,1)S(1)}, bf16[512,128]{1,0:T(8,128)(2,1)S(1)}, u32[]{:S(2)}, u32[]{:S(2)}) collective-permute-start(bf16[512,128]{1,0:T(8,128)(2,1)S(1)} %pad_maximum_fusion), channel_id=1, source_target_pairs={{0,4},{1,5},{2,6},{3,7},{4,0},{5,1},{6,2},{7,3},{8,12},{9,13},{10,... | collective-permute-start | bytes 393224 | tf_op jit(solution)/shard_map/ppermute | solution.py:34
  17.9 1.6 %copy-start = (bf16[1,8192,128]{2,1,0:T(8,128)(2,1)S(1)}, bf16[1,8192,128]{2,1,0:T(8,128)(2,1)}, u32[]{:S(2)}) copy-start(bf16[1,8192,128]{2,1,0:T(8,128)(2,1)} %param.10) | copy-start | bytes 6291460
  19.5 1.6 %copy-start.2 = (bf16[1,64,128,128]{3,2,1,0:T(8,128)(2,1)S(1)}, bf16[1,64,128,128]{3,2,1,0:T(8,128)(2,1)}, u32[]{:S(2)}) copy-start(bf16[1,64,128,128]{3,2,1,0:T(8,128)(2,1)} %param.14) | copy-start | bytes 6291460
  21.0 0.8 %copy-start.4 = (bf16[256,128]{1,0:T(8,128)(2,1)S(1)}, bf16[256,128]{1,0:T(8,128)(2,1)}, u32[]{:S(2)}) copy-start(bf16[256,128]{1,0:T(8,128)(2,1)} %refs_3_.1) | copy-start | bytes 196612
  21.9 0.8 %copy-start.6 = (bf16[128,128]{1,0:T(8,128)(2,1)S(1)}, bf16[128,128]{1,0:T(8,128)(2,1)}, u32[]{:S(2)}) copy-start(bf16[128,128]{1,0:T(8,128)(2,1)} %refs_2_.1) | copy-start | bytes 98308
  22.6 0.7 copy-start.9
  23.3 5.9 %copy-start.8 = (bf16[128,128]{1,0:T(8,128)(2,1)S(1)}, bf16[128,128]{1,0:T(8,128)(2,1)}, u32[]{:S(2)}) copy-start(bf16[128,128]{1,0:T(8,128)(2,1)} %refs_10_.3) | copy-start | bytes 98308
  29.2 6.5 %copy-start.1 = (bf16[1,8192,128]{2,1,0:T(8,128)(2,1)S(1)}, bf16[1,8192,128]{2,1,0:T(8,128)(2,1)}, u32[]{:S(2)}) copy-start(bf16[1,8192,128]{2,1,0:T(8,128)(2,1)} %param.10) | copy-start | bytes 6291460
  29.3 6.5 %copy-start.3 = (bf16[1,64,128,128]{3,2,1,0:T(8,128)(2,1)S(1)}, bf16[1,64,128,128]{3,2,1,0:T(8,128)(2,1)}, u32[]{:S(2)}) copy-start(bf16[1,64,128,128]{3,2,1,0:T(8,128)(2,1)} %param.14) | copy-start | bytes 6291460
  29.3 6.5 %copy-start.7 = (bf16[1,128,128]{2,1,0:T(8,128)(2,1)S(1)}, bf16[1,128,128]{2,1,0:T(8,128)(2,1)}, u32[]{:S(2)}) copy-start(bf16[1,128,128]{2,1,0:T(8,128)(2,1)} %param.15) | copy-start | bytes 98308
  35.8 10.4 %copy-start.5 = (bf16[256,128]{1,0:T(8,128)(2,1)S(1)}, bf16[256,128]{1,0:T(8,128)(2,1)}, u32[]{:S(2)}) copy-start(bf16[256,128]{1,0:T(8,128)(2,1)} %refs_3_.1) | copy-start | bytes 196612
  41.6 1.4 %collective-permute-start.7 = (bf16[400,128]{1,0:T(8,128)(2,1)S(1)}, bf16[400,128]{1,0:T(8,128)(2,1)S(1)}, u32[]{:S(2)}, u32[]{:S(2)}) collective-permute-start(bf16[400,128]{1,0:T(8,128)(2,1)S(1)} %backward.1), channel_id=1, source_target_pairs={{0,8},{8,0},{16,24},{24,16},{1,9},{9,1},{17,25},{25,17},{2,10},{10... | collective-permute-start | bytes 307208 | tf_op jit(solution)/shard_map/ppermute | solution.py:34
  43.0 8.8 %collective-permute-start.8 = (bf16[400,128]{1,0:T(8,128)(2,1)S(1)}, bf16[400,128]{1,0:T(8,128)(2,1)S(1)}, u32[]{:S(2)}, u32[]{:S(2)}) collective-permute-start(bf16[400,128]{1,0:T(8,128)(2,1)S(1)} %add_convert_fusion.3), channel_id=1, source_target_pairs={{0,16},{8,24},{16,0},{24,8},{1,17},{9,25},{17,1},{25,9},{2,18},{10... | collective-permute-start | bytes 307208 | tf_op jit(solution)/shard_map/ppermute | solution.py:34
  44.6 7.7 %collective-permute-start.2 = (bf16[4,128,128]{2,1,0:T(8,128)(2,1)S(1)}, bf16[4,128,128]{2,1,0:T(8,128)(2,1)S(1)}, u32[]{:S(2)}, u32[]{:S(2)}) collective-permute-start(bf16[4,128,128]{2,1,0:T(8,128)(2,1)S(1)} %get-tuple-element.23), channel_id=1, source_target_pairs={{0,1},{1,0},{2,3},{3,2},{4,5},{5,4},{6,7},{7,6},{8,9},{9,8},{10,11... | collective-permute-start | bytes 393224 | tf_op jit(solution)/shard_map/ppermute | solution.py:34
  51.9 4.7 %collective-permute-start.9 = (bf16[400,128]{1,0:T(8,128)(2,1)S(1)}, bf16[400,128]{1,0:T(8,128)(2,1)S(1)}, u32[]{:S(2)}, u32[]{:S(2)}) collective-permute-start(bf16[400,128]{1,0:T(8,128)(2,1)S(1)} %add_convert_fusion.2), channel_id=1, source_target_pairs={{0,1},{1,0},{2,3},{3,2},{4,5},{5,4},{6,7},{7,6},{8,9},{9,8},{10,11... | collective-permute-start | bytes 307208 | tf_op jit(solution)/shard_map/ppermute | solution.py:34
  52.4 5.4 %collective-permute-start.3 = (bf16[2,128,128]{2,1,0:T(8,128)(2,1)S(1)}, bf16[2,128,128]{2,1,0:T(8,128)(2,1)S(1)}, u32[]{:S(2)}, u32[]{:S(2)}) collective-permute-start(bf16[2,128,128]{2,1,0:T(8,128)(2,1)S(1)} %slice.52), channel_id=1, source_target_pairs={{0,2},{1,3},{2,0},{3,1},{4,6},{5,7},{6,4},{7,5},{8,10},{9,11},{10,... | collective-permute-start | bytes 196616 | tf_op jit(solution)/shard_map/ppermute | solution.py:34
  56.6 4.7 %collective-permute-start.10 = (bf16[400,128]{1,0:T(8,128)(2,1)S(1)}, bf16[400,128]{1,0:T(8,128)(2,1)S(1)}, u32[]{:S(2)}, u32[]{:S(2)}) collective-permute-start(bf16[400,128]{1,0:T(8,128)(2,1)S(1)} %add_convert_fusion.1), channel_id=1, source_target_pairs={{0,2},{1,3},{2,0},{3,1},{4,6},{5,7},{6,4},{7,5},{8,10},{9,11},{10,... | collective-permute-start | bytes 307208 | tf_op jit(solution)/shard_map/ppermute | solution.py:34
  57.8 5.2 %collective-permute-start.4 = (bf16[1,128,128]{2,1,0:T(8,128)(2,1)S(1)}, bf16[1,128,128]{2,1,0:T(8,128)(2,1)S(1)}, u32[]{:S(2)}, u32[]{:S(2)}) collective-permute-start(bf16[1,128,128]{2,1,0:T(8,128)(2,1)S(1)} %slice.53), channel_id=1, source_target_pairs={{0,4},{1,5},{2,6},{3,7},{4,0},{5,1},{6,2},{7,3},{8,12},{9,13},{10,... | collective-permute-start | bytes 98312 | tf_op jit(solution)/shard_map/ppermute | solution.py:34
  61.4 6.7 %copy-start.10 = (bf16[400,128]{1,0:T(8,128)(2,1)}, bf16[400,128]{1,0:T(8,128)(2,1)S(1)}, u32[]{:S(2)}) copy-start(bf16[400,128]{1,0:T(8,128)(2,1)S(1)} %add_convert_fusion.refs_0_) | copy-start | bytes 307204
  61.4 6.7 %collective-permute-start.11 = (bf16[400,128]{1,0:T(8,128)(2,1)S(1)}, bf16[400,128]{1,0:T(8,128)(2,1)S(1)}, u32[]{:S(2)}, u32[]{:S(2)}) collective-permute-start(bf16[400,128]{1,0:T(8,128)(2,1)S(1)} %add_convert_fusion.refs_0_), channel_id=1, source_target_pairs={{0,4},{1,5},{2,6},{3,7},{4,0},{5,1},{6,2},{7,3},{8,12},{9,13},{10,... | collective-permute-start | bytes 307208 | tf_op jit(solution)/shard_map/ppermute | solution.py:34
  68.1 0.6 copy-start.11

commit v2 on v0

v2 whole, which is shorter than its diff:
```python
import math

import jax
import jax.numpy as jnp
from jax import lax
from jax.experimental import pallas as pl
from jax.experimental.pallas import tpu as pltpu
from jax.sharding import PartitionSpec as P

H = 128
TILE = 128
NBR = 4
HT = 2
QUAD = 4
BODY = 4
F32 = jnp.float32
BF16 = jnp.bfloat16
MARGIN = HT * TILE
HALF = H // 2
PACK = 3 * HALF


def dot(a, b, ca=1, cb=0):
    return lax.dot_general(a, b, (((ca,), (cb,)), ((), ())), preferred_element_type=F32)


def split(x):
    hi = x.astype(BF16)
    return hi, (x - hi.astype(F32)).astype(BF16)


def diagonal(a, b):
    top = jnp.concatenate([a, jnp.zeros(b.shape, b.dtype)], axis=1)
    low = jnp.concatenate([jnp.zeros(a.shape, a.dtype), b], axis=1)
    return jnp.concatenate([top, low], axis=0)


def beside(a, b):
    return jnp.concatenate([a, b], axis=1)


def bit_order(count):
    bits = count.bit_length() - 1
    return [sum(((q >> b) & 1) << (bits - 1 - b) for b in range(bits)) for q in range(count)]


def exchange(x, axis, mask):
    return lax.ppermute(x, axis, [(i, i ^ mask) for i in range(lax.axis_size(axis))])


def rows_at(tile, count=1):
    return pl.ds(pl.multiple_of(tile * TILE, TILE), count * TILE)


def pack_kernel(nodes, near, far, sem):
    odd = lax.axis_index("graph") & 1
    gap = nodes.shape[0] - MARGIN
    near_at = pl.multiple_of((1 - odd) * gap, TILE)
    far_at = pl.multiple_of(odd * gap, TILE)
    copies = [
        pltpu.make_async_copy(nodes.at[pl.ds(near_at, MARGIN)], near, sem.at[0]),
        pltpu.make_async_copy(nodes.at[pl.ds(far_at, MARGIN)], far, sem.at[1]),
    ]
    for copy in copies:
        copy.start()
    for copy in copies:
        copy.wait()


def join_weights(w_msg, w_in, wcat):
    wcat[:H] = (0.5 * w_in[:H].astype(F32)).astype(BF16)
    wcat[H:] = (0.5 * dot(w_msg[...], w_in[H:])).astype(BF16)


def spans(count):
    quads = count // QUAD
    low = quads // 2 - quads // 8
    middle = list(range(low, low + quads // 4))
    return middle, [q for q in range(quads) if q not in middle]


def run_stages(count, *stages):
    held = {}
    for tick in range(count + len(stages) - 1):
        for k, stage in enumerate(stages):
            i = tick - k
            if 0 <= i < count:
                held[k, i] = stage(i, held.get((k - 1, i)))


def forward_quads(firsts, at_adj, src, dst, ext, adj, pw, wcat, bias, outs, acc, ready=None):
    a_out, act_out, slope_out = outs
    me = lax.axis_index("graph")
    h_bias = 0.5 * bias[...]

    def gather(i, _):
        if ready is not None:
            ready(i)
        sums = []
        for j in range(QUAD):
            t = firsts[i] + j
            picked = [ext[rows_at(src[k, t]), :] for k in range(NBR)]
            weights = jnp.concatenate([adj[at_adj[i] + j, k] for k in range(NBR)], axis=1)
            sums.append(dot(weights, jnp.concatenate(picked, axis=0)).astype(BF16))
        summed = jnp.concatenate(sums, axis=0)
        a_out[rows_at(firsts[i], QUAD), :] = summed
        return summed

    def activate(i, summed):
        own = ext[rows_at(firsts[i] + HT, QUAD), :]
        h = dot(beside(own, summed), wcat[...]) + h_bias
        s = jnp.tanh(h)
        hs = h * s
        act = (h + hs).astype(BF16)
        act_out[rows_at(firsts[i], QUAD), :] = act
        slope = (1.0 + s) * ((1.0 + h) - hs)
        for j in range(QUAD):
            slope_out[firsts[i] + j] = slope[j * TILE : (j + 1) * TILE].T
        return act

    def pool(i, act):
        add_pooled(firsts[i], act, dst, me, pw, acc)

    run_stages(len(firsts), gather, activate, pool)


def add_pooled(first, values, dst, me, pw, acc):
    for j in range(0, QUAD, 2):
        a, b = values[j * TILE : (j + 1) * TILE], values[(j + 1) * TILE : (j + 2) * TILE]
        t = first + j
        term = dot(beside(pw[t], pw[t + 1]), diagonal(a, b))
        acc[dst[0, t] ^ me] += term[:, :H]
        acc[dst[0, t + 1] ^ me] += term[:, H:]


def inner_kernel(
    middle, rest, src, dst, nodes, adj, pw, w_msg, w_in, bias,
    ext, adj_v, pw_v, a_out, act_out, slope_out, acc, wcat, adj_m, sem,
):
    quads = len(middle) + len(rest)
    chunk = QUAD * TILE
    near = [middle[0] - 1] + middle + [middle[-1] + 1]
    far = [q for q in range(quads) if q not in near]

    def node_copy(q):
        return pltpu.make_async_copy(
            nodes.at[pl.ds(q * chunk, chunk)],
            ext.at[pl.ds(MARGIN + q * chunk, chunk)],
            sem.at[0, q],
        )

    def pool_copy(q):
        part = pl.ds(q * QUAD, QUAD)
        return pltpu.make_async_copy(pw.at[part], pw_v.at[part], sem.at[1, q])

    def edge_copy(q):
        to, n = (adj_m, middle.index(q)) if q in middle else (adj_v, rest.index(q))
        return pltpu.make_async_copy(
            adj.at[pl.ds(q * QUAD, QUAD)], to.at[pl.ds(n * QUAD, QUAD)], sem.at[2, q]
        )

    first = [edge_copy(middle[0])] + [node_copy(q) for q in near]
    first += [edge_copy(q) for q in middle[1:]] + [pool_copy(q) for q in middle]
    later = [node_copy(q) for q in far] + [edge_copy(q) for q in rest]
    later += [pool_copy(q) for q in rest]
    for copy in first + later:
        copy.start()
    join_weights(w_msg, w_in, wcat)
    acc[...] = jnp.zeros_like(acc)

    def ready(i):
        if i == 0:
            for q in near[:3]:
                node_copy(q).wait()
        elif near[i + 2 :]:
            node_copy(near[i + 2]).wait()
        edge_copy(middle[i]).wait()
        pool_copy(middle[i]).wait()

    forward_quads(
        [q * QUAD for q in middle], [n * QUAD for n in range(len(middle))], src, dst, ext,
        adj_m, pw_v, wcat, bias, (a_out, act_out, slope_out), acc, ready,
    )
    for copy in later:
        copy.wait()


def outer_kernel(
    middle, rest, src, dst, near, far, w_msg, w_in, bias,
    ext_in, a_in, act_in, slope_in, acc_in, adj, pw,
    ext, a_out, act_out, slope_out, p_out, acc, wcat,
):
    odd = lax.axis_index("graph") & 1
    right = ext.shape[0] - MARGIN
    ext[pl.ds(pl.multiple_of((1 - odd) * right, TILE), MARGIN), :] = near[...]
    ext[pl.ds(pl.multiple_of(odd * right, TILE), MARGIN), :] = far[...]
    join_weights(w_msg, w_in, wcat)
    acc[...] = acc_in[...]

    def body(step, _):
        spots = [step * BODY + n for n in range(BODY)]
        firsts = [QUAD * jnp.where(s < middle[0], s, s + len(middle)) for s in spots]
        forward_quads(
            firsts, [QUAD * s for s in spots], src, dst, ext, adj, pw, wcat, bias,
            (a_out, act_out, slope_out), acc,
        )
        return 0

    lax.fori_loop(0, len(rest) // BODY, body, 0)
    for r in range(acc.shape[0]):
        hi, lo = split(acc[r])
        p_out[r * TILE : (r + 1) * TILE, :H] = hi
        p_out[r * TILE : (r + 1) * TILE, H:] = lo


def backward_kernel(pieces, dst, *refs):
    cots = refs[:pieces]
    (ext, a_in, slope_in, pw, p_in, w_out) = refs[pieces : pieces + 6]
    keep, send, cot_all, cot_w, total, bias, mats = refs[pieces + 6 :]
    me = lax.axis_index("graph")
    core = lax.axis_index("design") & 1
    at = 0
    for cot in cots:
        size = cot.shape[0]
        cot_all[at : at + size] = cot[...]
        at += size
    for r in range(cot_w.shape[0]):
        tile = cot_all[r * TILE : (r + 1) * TILE]
        cot_w[r] = (0.5 * dot(w_out[...], tile, 1, 1)).astype(BF16)
    both = dot(cot_all[...], p_in[...], 0, 0)
    mats[0] = both[:, :H] + both[:, H:]
    total[...] = jnp.zeros_like(total)
    bias[...] = jnp.zeros_like(bias)

    def body(step, _):
        firsts = [(step * BODY + n) * QUAD for n in range(BODY)]

        def unpool(i, _):
            parts = []
            for j in range(0, QUAD, 2):
                t = firsts[i] + j
                left = beside(cot_w[dst[0, t] ^ me], cot_w[dst[0, t + 1] ^ me])
                parts.append(dot(left, diagonal(pw[t], pw[t + 1])))
            return parts

        def slopes(i, parts):
            done = []
            for j, part in enumerate(parts):
                t = firsts[i] + 2 * j
                grad = part * beside(slope_in[t], slope_in[t + 1])
                bias[...] += grad
                done.append(grad.astype(BF16))
            return jnp.concatenate(done, axis=1)

        def weights(i, grad_pre):
            own = ext[rows_at(firsts[i] + HT, QUAD), :]
            total[...] += dot(grad_pre, beside(own, a_in[rows_at(firsts[i], QUAD), :]))

        run_stages(BODY, unpool, slopes, weights)
        return 0

    lax.fori_loop(0, slope_in.shape[0] // (QUAD * BODY), body, 0)
    mats[1] = total[:, :H]
    mats[2] = total[:, H:]
    column = jnp.sum(bias[...], axis=1, keepdims=True)
    row = jnp.broadcast_to(column, (H, H)).T[:8]
    for out, half in ((keep, core), (send, 1 - core)):
        for m in range(3):
            at = pl.multiple_of(half * HALF, HALF)
            out[m * HALF : (m + 1) * HALF] = mats[m, pl.ds(at, HALF), :]
        out[PACK:] = row


def tail_kernel(order, dst, ext, act_in, pw, w_out, fine, send, keep, acc, wdiag, out_v, sem):
    me = lax.axis_index("graph")
    wdiag[...] = diagonal(w_out[...], w_out[...])
    acc[...] = jnp.zeros_like(acc)
    chunk = QUAD * BODY
    steps = act_in.shape[0] // (chunk * TILE)
    half = QUAD * TILE // 2

    def copy(step):
        part = rows_at(step * chunk, chunk)
        return pltpu.make_async_copy(out_v.at[part], fine.at[part], sem.at[step])

    def body(step, _):
        firsts = [(step * BODY + n) * QUAD for n in range(BODY)]

        def project(i, _):
            act = act_in[rows_at(firsts[i], QUAD), :]
            return dot(beside(act[:half], act[half:]), wdiag[...])

        def update(i, delta):
            own = ext[rows_at(firsts[i] + HT, QUAD), :].astype(F32)
            out = jnp.concatenate([own[:half] + delta[:, :H], own[half:] + delta[:, H:]], axis=0)
            out = out.astype(BF16)
            out_v[rows_at(firsts[i], QUAD), :] = out
            return out

        def pool(i, out):
            add_pooled(firsts[i], out, dst, me, pw, acc)

        run_stages(BODY, project, update, pool)
        copy(step).start()
        return 0

    lax.fori_loop(0, steps, body, 0)
    count = len(order)
    for q, r in enumerate(order):
        if q < count // 2:
            keep[q] = acc[r]
        else:
            send[q - count // 2] = acc[r].astype(BF16)

    def drain(step, _):
        copy(step).wait()
        return 0

    lax.fori_loop(0, steps, drain, 0)


def finish_kernel(scale, held, other, w_msg, w_in, g_msg, g_in, g_bias, g_out, mats):
    core = lax.axis_index("design") & 1
    for part, half in ((held, core), (other, 1 - core)):
        for m in range(3):
            at = pl.multiple_of(half * HALF, HALF)
            mats[m, pl.ds(at, HALF), :] = part[m * HALF : (m + 1) * HALF] * scale
    g_out[...] = mats[0].T
    g_in[:H] = mats[1].T
    hi, lo = split(mats[2])
    g_in[H:] = dot(w_msg[...], hi, 0, 1) + dot(w_msg[...], lo, 0, 1)
    w_low = w_in[H:]
    g_msg[...] = dot(hi, w_low, 0, 1) + dot(lo, w_low, 0, 1)
    g_bias[...] = jnp.where(core == 0, held[PACK : PACK + 1], other[PACK : PACK + 1]) * scale


def on_device(
    nodes, adjacency, tile_src, pool_dst, pool_weight, coarse_cot, w_msg, w_in, b_in, w_out
):
    def stay(x):
        return pltpu.with_memory_space_constraint(x, pltpu.HBM)

    feats = stay(nodes[0])
    adj = stay(adjacency[0])
    src = tile_src[0].T
    dst = pool_dst[0].T
    pw = stay(pool_weight[0])
    cot = coarse_cot[0]
    rows = feats.shape[0]
    count = rows // TILE
    slabs = lax.axis_size("graph")
    designs = lax.axis_size("design")
    assert slabs & (slabs - 1) == 0 and designs & (designs - 1) == 0
    assert slabs > 1 and designs > 1
    assert count % (4 * QUAD * BODY) == 0
    middle, rest = spans(count)
    bias = stay(b_in.reshape(1, H))
    w_msg, w_in, w_out = stay(w_msg), stay(w_in), stay(w_out)

    smem = pl.BlockSpec(memory_space=pltpu.SMEM)
    vmem = pl.BlockSpec(memory_space=pltpu.VMEM)
    hbm = pl.BlockSpec(memory_space=pl.ANY)

    def shape(*dims, dtype=F32):
        return jax.ShapeDtypeStruct(dims, dtype)

    def fixed(x):
        return pl.BlockSpec(x.shape, lambda *_: (0,) * x.ndim)

    def params(mib):
        return pltpu.CompilerParams(vmem_limit_bytes=mib * 1024 * 1024)

    def cost(units, mib, trans=0):
        return pl.CostEstimate(
            flops=2 * units * rows * H * H,
            bytes_accessed=mib * 1024 * 1024,
            transcendentals=trans,
        )

    first = [m for m in (1, 2, 3) if m < slabs] + [1 << b for b in range(2, slabs.bit_length() - 1)]
    cots = {0: cot}
    for mask in first:
        cots[mask] = exchange(cot, "graph", mask)

    near_send, far_send = pl.pallas_call(
        pack_kernel,
        in_specs=[hbm],
        out_specs=[vmem, vmem],
        out_shape=[shape(MARGIN, H, dtype=BF16)] * 2,
        scratch_shapes=[pltpu.SemaphoreType.DMA((2,))],
        compiler_params=params(1),
        name="pack",
    )(feats)
    near = exchange(near_send, "graph", 1)
    across = [(i, i + 1) for i in range(1, slabs - 1, 2)]
    far = lax.ppermute(far_send, "graph", across + [(b, a) for a, b in across])

    ext_shape = shape(rows + 2 * MARGIN, H, dtype=BF16)
    row_shape = shape(rows, H, dtype=BF16)
    slope_shape = shape(count, H, TILE)
    acc_shape = shape(slabs, TILE, H)
    adj_shape = shape(len(rest) * QUAD, NBR, TILE, TILE, dtype=BF16)
    wcat = pltpu.VMEM((2 * H, H), BF16)

    ext, adj_v, pw_v, a_mid, act_mid, slope_mid, acc_mid = pl.pallas_call(
        lambda *refs: inner_kernel(middle, rest, *refs),
        in_specs=[smem, smem, hbm, hbm, hbm, fixed(w_msg), fixed(w_in), fixed(bias)],
        out_specs=[vmem] * 7,
        out_shape=[
            ext_shape, adj_shape, shape(*pw.shape, dtype=BF16), row_shape, row_shape,
            slope_shape, acc_shape,
        ],
        scratch_shapes=[
            wcat,
            pltpu.VMEM((len(middle) * QUAD, NBR, TILE, TILE), BF16),
            pltpu.SemaphoreType.DMA((3, count // QUAD)),
        ],
        compiler_params=params(12),
        cost_estimate=cost(2, 12, rows * H // 4),
        name="inner",
    )(src, dst, feats, adj, pw, w_msg, w_in, bias)

    ext, a_all, act_all, slope_all, p_all = pl.pallas_call(
        lambda *refs: outer_kernel(middle, rest, *refs),
        in_specs=[smem, smem, vmem, vmem, fixed(w_msg), fixed(w_in), fixed(bias)] + [vmem] * 7,
        out_specs=[vmem] * 5,
        out_shape=[
            ext_shape, row_shape, row_shape, slope_shape,
            shape(slabs * TILE, 2 * H, dtype=BF16),
        ],
        scratch_shapes=[pltpu.VMEM((slabs, TILE, H), F32), wcat],
        input_output_aliases={7: 0, 8: 1, 9: 2, 10: 3},
        compiler_params=params(12),
        cost_estimate=cost(6, 8, rows * H // 2),
        name="outer",
    )(
        src, dst, near, far, w_msg, w_in, bias, ext, a_mid, act_mid, slope_mid, acc_mid,
        adj_v, pw_v,
    )

    for b in range(2, slabs.bit_length() - 1):
        mask = 1 << b
        known = list(range(1, mask))
        got = exchange(jnp.concatenate([cots[r] for r in known], axis=0), "graph", mask)
        for n, r in enumerate(known):
            cots[mask + r] = got[n * TILE : (n + 1) * TILE]

    every = [cots[r] for r in range(slabs)]
    keep, send = pl.pallas_call(
        lambda *refs: backward_kernel(len(every), *refs),
        in_specs=[smem]
        + [vmem] * len(every)
        + [vmem] * 5
        + [fixed(w_out)],
        out_specs=[vmem, vmem],
        out_shape=[shape(PACK + 8, H)] * 2,
        scratch_shapes=[
            pltpu.VMEM((slabs * TILE, H), BF16),
            pltpu.VMEM((slabs, H, TILE), BF16),
            pltpu.VMEM((H, 2 * H), F32),
            pltpu.VMEM((H, 2 * H), F32),
            pltpu.VMEM((3, H, H), F32),
        ],
        compiler_params=params(16),
        cost_estimate=cost(3, 4),
        name="backward",
    )(dst, *every, ext, a_all, slope_all, pw_v, p_all, w_out)

    order = bit_order(slabs)
    fine, c_send, c_keep = pl.pallas_call(
        lambda *refs: tail_kernel(order, *refs),
        in_specs=[smem, vmem, vmem, vmem, fixed(w_out)],
        out_specs=[hbm, vmem, vmem],
        out_shape=[
            row_shape,
            shape(slabs // 2, TILE, H, dtype=BF16),
            shape(slabs // 2, TILE, H),
        ],
        scratch_shapes=[
            pltpu.VMEM((slabs, TILE, H), F32),
            pltpu.VMEM((2 * H, 2 * H), BF16),
            pltpu.VMEM((rows, H), BF16),
            pltpu.SemaphoreType.DMA((count // (QUAD * BODY),)),
        ],
        compiler_params=params(16),
        cost_estimate=cost(2, 4),
        name="tail",
    )(dst, ext, act_all, pw_v, w_out)

    held = c_keep + exchange(c_send, "graph", 1).astype(F32)
    mask = 2
    while mask < slabs:
        size = held.shape[0] // 2
        got = exchange(held[size:].astype(BF16), "graph", mask)
        held = held[:size] + got.astype(F32)
        mask *= 2
    coarse = held[0].astype(BF16)

    rounds = [("design", 1 << b) for b in range(1, designs.bit_length() - 1)]
    rounds += [("graph", 1 << b) for b in range(slabs.bit_length() - 1)]
    mine = keep + exchange(send, "design", 1)
    for axis, mask in rounds:
        mine = mine + exchange(mine, axis, mask)
    other = exchange(mine, "design", 1)
    scale = 1.0 / math.sqrt(designs * rows * slabs)
    g_msg, g_in, g_bias, g_out = pl.pallas_call(
        lambda *refs: finish_kernel(scale, *refs),
        in_specs=[vmem, vmem, fixed(w_msg), fixed(w_in)],
        out_specs=[vmem] * 4,
        out_shape=[shape(H, H), shape(2 * H, H), shape(1, H), shape(H, H)],
        scratch_shapes=[pltpu.VMEM((3, H, H), F32)],
        compiler_params=params(4),
        name="finish",
    )(mine, other, w_msg, w_in)
    return fine[None], coarse[None], g_msg, g_in, g_bias.reshape(H), g_out


def solution(mesh):
    in_specs = (
        P("design", "graph", None),
        P("design", "graph", None, None, None),
        P("design", "graph", None),
        P("design", "graph", None),
        P("design", "graph", None, None),
        P("design", "graph", None),
        P(),
        P(),
        P(),
        P(),
    )
    out_specs = (P("design", "graph", None), P("design", "graph", None), P(), P(), P(), P())
    return jax.shard_map(
        on_device, mesh=mesh, in_specs=in_specs, out_specs=out_specs, check_vma=False
    )
```

time: 340 us -> 62.1 us (0.18)
  waiting for transfers between devices: 88.7 us -> 14.7 us
  blocking collectives: 72.9 us -> 0 us
  other arithmetic: 62.7 us -> 0.75 us
  matrix products: 45.2 us -> 0 us
  local copies, waits for them, and re-layouts: 43 us -> 0.04 us
  Pallas kernels: 0 us -> 20.8 us
  between operations: 15.8 us -> 0.81 us
  starting transfers between devices: 10.3 us -> 24.6 us
    psum x1 -> x0, waiting for transfers between devices: 84.4 us -> none  [on_device(): lax.psum((grad_msg, grad_in, grad_bias, grad_out), ('design', 'graph'))]
    scatter-add x3 -> x0, other arithmetic: 51.9 us -> none  [the longest x1 49.6 us: on_device(): grad_ext = jnp.zeros((count + 2 * HT, TILE, H), jnp.float32).at[source.re...]
    dot_general x16 -> x0, matrix products: 45.2 us -> none  [the longest x1 8.25 us: on_device(): jnp.einsum('tkij,tkjh->tih', edge_w, picked, preferred_element_type=jnp.f...]
    psum x1 -> x0, blocking collectives: 39.8 us -> none  [on_device(): lax.psum((grad_msg, grad_in, grad_bias, grad_out), ('design', 'graph'))]
    all_gather x1 -> x0, blocking collectives: 33.1 us -> none  [on_device(): lax.all_gather(cot_tile, 'graph', axis=0, tiled=True)]
    pallas_call x0 -> x6, Pallas kernels: none -> 20.8 us  [the longest x1 5.81 us: on_device(): pl.pallas_call(lambda *refs: inner_kernel(middle, rest, *refs), in_specs=...]
    reshape x1 -> x0, local copies, waits for them, and re-layouts: 17.4 us -> none  [on_device(): returned.reshape(count * NBR, TILE, H)]
    ppermute x4 -> x16, starting transfers between devices: 10.2 us -> 24.6 us  [the longest x15 23.9 us: exchange(): lax.ppermute(x, axis, [(i, i ^ mask) for i in range(lax.axis_size(axis))])]
  transfers between devices with their start and end apart: 6 -> 16, of which waited for: 2 -> 6; matrix products, arithmetic and copies ran while one was open for 8% -> 1% of each run, Pallas kernels for 0% -> 25%
where the time goes in v2:
time: 62.1 us; the launch traced here: 61.7 us
  starting transfers between devices  24.6 us (40%)
  Pallas kernels  20.8 us (33%)
  waiting for transfers between devices  14.7 us (24%)
  between operations  0.81 us (1%)
  other arithmetic  0.75 us (1%)
    ppermute x15, starting transfers between devices, exchange(): lax.ppermute(x, axis, [(i, i ^ mask) for i in range(lax.axis_size(axis))])  23.9 us
    ppermute x15, waiting for transfers between devices, exchange(): lax.ppermute(x, axis, [(i, i ^ mask) for i in range(lax.axis_size(axis))])  14.7 us
    pallas_call x1, Pallas kernels, on_device(): pl.pallas_call(lambda *refs: inner_kernel(middle, rest, *refs), in_specs=...  5.81 us
    pallas_call x1, Pallas kernels, on_device(): pl.pallas_call(lambda *refs: outer_kernel(middle, rest, *refs), in_specs=...  4.95 us
    pallas_call x1, Pallas kernels, on_device(): pl.pallas_call(lambda *refs: tail_kernel(order, *refs), in_specs=[smem, v...  3.83 us
    pallas_call x1, Pallas kernels, on_device(): pl.pallas_call(lambda *refs: backward_kernel(len(every), *refs), in_specs...  3.6 us
    pallas_call x1, Pallas kernels, on_device(): pl.pallas_call(lambda *refs: finish_kernel(scale, *refs), in_specs=[vmem,...  1.77 us
  transfers between devices with their start and end apart: 16, of which 6 were waited for; matrix products, arithmetic and copies ran while one was open for 1% of the time, Pallas kernels for 25%

profile of v2, /device:TPU:0, one launch (start us, length us, event | category | flops | bytes accessed | tf_op | source)
XLA Modules:
  0.0 61.7 jit_solution(8074345130456981892)
XLA Ops:
  0.7 3.1 %collective-permute-start.5 = (bf16[128,128]{1,0:T(8,128)(2,1)}, bf16[128,128]{1,0:T(8,128)(2,1)S(1)}, u32[]{:S(2)}, u32[]{:S(2)}) collective-permute-start(bf16[128,128]{1,0:T(8,128)(2,1)} %bitcast.11), channel_id=1, source_target_pairs={{0,1},{1,0},{2,3},{3,2},{4,5},{5,4},{6,7},{7,6},{8,9},{9,8},{10,11... | collective-permute-start | bytes 98312 | tf_op jit(solution)/shard_map/ppermute | solution.py:48
  3.7 1.6 %collective-permute-start.6 = (bf16[128,128]{1,0:T(8,128)(2,1)}, bf16[128,128]{1,0:T(8,128)(2,1)S(1)}, u32[]{:S(2)}, u32[]{:S(2)}) collective-permute-start(bf16[128,128]{1,0:T(8,128)(2,1)} %bitcast.12), channel_id=1, source_target_pairs={{0,2},{1,3},{2,0},{3,1},{4,6},{5,7},{6,4},{7,5},{8,10},{9,11},{10,... | collective-permute-start | bytes 98312 | tf_op jit(solution)/shard_map/ppermute | solution.py:48
  5.3 3.0 %collective-permute-start.8 = (bf16[128,128]{1,0:T(8,128)(2,1)}, bf16[128,128]{1,0:T(8,128)(2,1)S(1)}, u32[]{:S(2)}, u32[]{:S(2)}) collective-permute-start(bf16[128,128]{1,0:T(8,128)(2,1)} %bitcast.14), channel_id=1, source_target_pairs={{0,4},{1,5},{2,6},{3,7},{4,0},{5,1},{6,2},{7,3},{8,12},{9,13},{10,... | collective-permute-start | bytes 98312 | tf_op jit(solution)/shard_map/ppermute | solution.py:48
  8.3 0.9 %pack.1 = (bf16[256,128]{1,0:T(8,128)(2,1)S(1)}, bf16[256,128]{1,0:T(8,128)(2,1)S(1)}) custom-call(bf16[8192,128]{1,0:T(8,128)(2,1)} %bitcast.23), custom_call_target="tpu_custom_call" | custom-call | tf_op jit(solution)/shard_map/pack/pallas_call | solution.py:385
  9.2 1.6 %collective-permute-start = (bf16[256,128]{1,0:T(8,128)(2,1)S(1)}, bf16[256,128]{1,0:T(8,128)(2,1)S(1)}, u32[]{:S(2)}, u32[]{:S(2)}) collective-permute-start(bf16[256,128]{1,0:T(8,128)(2,1)S(1)} %get-tuple-element.29), channel_id=1, source_target_pairs={{0,1},{1,0},{2,3},{3,2},{4,5},{5,4},{6,7},{7,6},{8,9},{9,8},{10,11... | collective-permute-start | bytes 196616 | tf_op jit(solution)/shard_map/ppermute | solution.py:48
  10.8 5.8 %inner.1 = (bf16[8704,128]{1,0:T(8,128)(2,1)S(1)}, bf16[48,4,128,128]{3,2,1,0:T(8,128)(2,1)S(1)}, bf16[64,128,128]{2,1,0:T(8,128)(2,1)S(1)}, bf16[8192,128]{1,0:...) custom-call(s32[4,64]{1,0:T(4,128)S(1)} %bitcast.20, ...), custom_call_target="tpu_custom_call" | custom-call | flops 536870912 | bytes 12582912 | tf_op jit(solution)/shard_map/inner/pallas_call | solution.py:405
  16.6 0.7 %collective-permute-start.1 = (bf16[256,128]{1,0:T(8,128)(2,1)S(1)}, bf16[256,128]{1,0:T(8,128)(2,1)S(1)}, u32[]{:S(2)}, u32[]{:S(2)}) collective-permute-start(bf16[256,128]{1,0:T(8,128)(2,1)S(1)} %get-tuple-element.30), channel_id=1, source_target_pairs={{1,2},{3,4},{5,6},{2,1},{4,3},{6,5},{9,10},{11,12},{13,14},{10,9},... | collective-permute-start | bytes 196616 | tf_op jit(solution)/shard_map/ppermute | solution.py:396
  17.3 4.3 %collective-permute-start.9 = (bf16[384,128]{1,0:T(8,128)(2,1)S(1)}, bf16[384,128]{1,0:T(8,128)(2,1)S(1)}, u32[]{:S(2)}, u32[]{:S(2)}) collective-permute-start(bf16[384,128]{1,0:T(8,128)(2,1)S(1)} %pad_maximum_fusion), channel_id=1, source_target_pairs={{0,4},{1,5},{2,6},{3,7},{4,0},{5,1},{6,2},{7,3},{8,12},{9,13},{10,... | collective-permute-start | bytes 294920 | tf_op jit(solution)/shard_map/ppermute | solution.py:48
  21.6 0.0 collective-permute-done.refs_2_
  21.6 0.0 collective-permute-done.1.refs_3_
  21.6 5.0 %outer.1 = (bf16[8704,128]{1,0:T(8,128)(2,1)S(1)}, bf16[8192,128]{1,0:T(8,128)(2,1)S(1)}, bf16[8192,128]{1,0:T(8,128)(2,1)S(1)}, f32[64,128,128]{2,1,0:T(8,128)S(1)}, bf16[1024,256]{1,0:T(8,128)(2,1)S(1)}) custom-call(s32[4,64]{1,0:T(4,128)S(1)} %bitcast.21, ...), custom_call_target="tpu_custom_call", output_to_operand_aliasing={{0}: (7, {}), {1}: (8, {}), {2}: (9, {}), {3}: (10, {})} | custom-call | flops 1610612736 | bytes 8388608 | tf_op jit(solution)/shard_map/outer/pallas_call | solution.py:423
  26.6 0.0 collective-permute-done.9
  26.6 0.0 collective-permute-done.8.refs_5_
  26.6 3.6 %backward.1 = (f32[200,128]{1,0:T(8,128)S(1)}, f32[200,128]{1,0:T(8,128)S(1)}) custom-call(s32[1,64]{1,0:T(1,128)S(1)} %bitcast.18, bf16[128,128]{1,0:T(8,128)(2,1)S(1)} %bitcast.15, bf16[128,128]{1,0:T(8,128)(2,1)S(1)} %collective-permute-done.5.refs_2_, bf16[128,128]{1,0:T(8,128)(2,1)S(1)} %collective-permute-done.6.refs_3_, ...), custom_call_target="tpu_custom_call" | custom-call | flops 805306368 | bytes 4194304 | tf_op jit(solution)/shard_map/backward/pallas_call | solution.py:449
  30.2 0.0 collective-permute-start.10
  30.3 1.3 %collective-permute-done.10 = f32[200,128]{1,0:T(8,128)S(1)} collective-permute-done((f32[200,128]{1,0:T(8,128)S(1)}, f32[200,128]{1,0:T(8,128)S(1)}, u32[]{:S(2)}, u32[]{:S(2)}) %collective-permute-start.10) | collective-permute-done | bytes 102432 | tf_op jit(solution)/shard_map/ppermute | solution.py:48
  31.6 1.6 %collective-permute-start.11 = (f32[200,128]{1,0:T(8,128)S(1)}, f32[200,128]{1,0:T(8,128)S(1)}, u32[]{:S(2)}, u32[]{:S(2)}) collective-permute-start(f32[200,128]{1,0:T(8,128)S(1)} %add.27), channel_id=1, source_target_pairs={{0,16},{8,24},{16,0},{24,8},{1,17},{9,25},{17,1},{25,9},{2,18},{10... | collective-permute-start | bytes 307208 | tf_op jit(solution)/shard_map/ppermute | solution.py:48
  33.1 3.8 %tail.1 = (bf16[8192,128]{1,0:T(8,128)(2,1)}, bf16[4,128,128]{2,1,0:T(8,128)(2,1)S(1)}, f32[4,128,128]{2,1,0:T(8,128)S(1)}) custom-call(s32[1,64]{1,0:T(1,128)S(1)} %bitcast.19, bf16[8704,128]{1,0:T(8,128)(2,1)S(1)} %get-tuple-element.38.refs_1_.refs_9_, bf16[8192,128]{1,0:T(8,128)(2,1)S(1)} %get-tuple-element.39.refs_2_, ...), custom_call_target="tpu_custom_call" | custom-call | flops 536870912 | bytes 4194304 | tf_op jit(solution)/shard_map/tail/pallas_call | solution.py:470
  37.0 3.1 %collective-permute-start.2 = (bf16[4,128,128]{2,1,0:T(8,128)(2,1)S(1)}, bf16[4,128,128]{2,1,0:T(8,128)(2,1)S(1)}, u32[]{:S(2)}, u32[]{:S(2)}) collective-permute-start(bf16[4,128,128]{2,1,0:T(8,128)(2,1)S(1)} %get-tuple-element.42), channel_id=1, source_target_pairs={{0,1},{1,0},{2,3},{3,2},{4,5},{5,4},{6,7},{7,6},{8,9},{9,8},{10,11... | collective-permute-start | bytes 393224 | tf_op jit(solution)/shard_map/ppermute | solution.py:48
  40.1 0.1 collective-permute-start.12
  40.1 5.6 %collective-permute-done.12 = f32[200,128]{1,0:T(8,128)S(1)} collective-permute-done((f32[200,128]{1,0:T(8,128)S(1)}, f32[200,128]{1,0:T(8,128)S(1)}, u32[]{:S(2)}, u32[]{:S(2)}) %collective-permute-start.12) | collective-permute-done | bytes 102432 | tf_op jit(solution)/shard_map/ppermute | solution.py:48
  45.8 2.4 %collective-permute-start.13 = (f32[200,128]{1,0:T(8,128)S(1)}, f32[200,128]{1,0:T(8,128)S(1)}, u32[]{:S(2)}, u32[]{:S(2)}) collective-permute-start(f32[200,128]{1,0:T(8,128)S(1)} %add.29), channel_id=1, source_target_pairs={{0,2},{1,3},{2,0},{3,1},{4,6},{5,7},{6,4},{7,5},{8,10},{9,11},{10,... | collective-permute-start | bytes 307208 | tf_op jit(solution)/shard_map/ppermute | solution.py:48
  48.3 0.1 collective-permute-start.3
  48.3 3.1 %collective-permute-done.13 = f32[200,128]{1,0:T(8,128)S(1)} collective-permute-done((f32[200,128]{1,0:T(8,128)S(1)}, f32[200,128]{1,0:T(8,128)S(1)}, u32[]{:S(2)}, u32[]{:S(2)}) %collective-permute-start.13) | collective-permute-done | bytes 102432 | tf_op jit(solution)/shard_map/ppermute | solution.py:48
  51.5 1.3 %collective-permute-start.14 = (f32[200,128]{1,0:T(8,128)S(1)}, f32[200,128]{1,0:T(8,128)S(1)}, u32[]{:S(2)}, u32[]{:S(2)}) collective-permute-start(f32[200,128]{1,0:T(8,128)S(1)} %add.30), channel_id=1, source_target_pairs={{0,4},{1,5},{2,6},{3,7},{4,0},{5,1},{6,2},{7,3},{8,12},{9,13},{10,... | collective-permute-start | bytes 307208 | tf_op jit(solution)/shard_map/ppermute | solution.py:48
  52.8 1.8 %collective-permute-start.4 = (bf16[1,128,128]{2,1,0:T(8,128)(2,1)S(1)}, bf16[1,128,128]{2,1,0:T(8,128)(2,1)S(1)}, u32[]{:S(2)}, u32[]{:S(2)}) collective-permute-start(bf16[1,128,128]{2,1,0:T(8,128)(2,1)S(1)} %slice.44), channel_id=1, source_target_pairs={{0,4},{1,5},{2,6},{3,7},{4,0},{5,1},{6,2},{7,3},{8,12},{9,13},{10,... | collective-permute-start | bytes 98312 | tf_op jit(solution)/shard_map/ppermute | solution.py:48
  54.6 4.0 %collective-permute-done.14 = f32[200,128]{1,0:T(8,128)S(1)} collective-permute-done((f32[200,128]{1,0:T(8,128)S(1)}, f32[200,128]{1,0:T(8,128)S(1)}, u32[]{:S(2)}, u32[]{:S(2)}) %collective-permute-start.14) | collective-permute-done | bytes 102432 | tf_op jit(solution)/shard_map/ppermute | solution.py:48
  58.6 0.1 collective-permute-start.15
  58.6 0.3 collective-permute-done.4
  58.9 0.6 %fusion = bf16[1,128,128]{2,1,0:T(8,128)(2,1)} fusion(f32[2,128,128]{2,1,0:T(8,128)S(1)} %slice_add_fusion, bf16[1,128,128]{2,1,0:T(8,128)(2,1)S(1)} %collective-permute-done.4), kind=kLoop, calls=%fused_computation.6 | loop fusion | flops 49152 | bytes 131072 | tf_op jit(solution)/shard_map/convert_element_type | solution.py:497
  59.5 0.4 collective-permute-done.15.refs_1_
  59.9 1.8 %finish.1 = (f32[128,128]{1,0:T(8,128)}, f32[256,128]{1,0:T(8,128)}, f32[1,128]{1,0:T(1,128)}, f32[128,128]{1,0:T(8,128)}) custom-call(f32[200,128]{1,0:T(8,128)S(1)} %add.31.refs_0_, f32[200,128]{1,0:T(8,128)S(1)} %collective-permute-done.15.refs_1_, bf16[128,128]{1,0:T(8,128)(2,1)} %refs_2_.1, bf16[256,128]{1,0:T(8,128)(2,1)} %refs_3_.1), custom_call_target="tpu_custom_call" | custom-call | tf_op jit(solution)/shard_map/finish/pallas_call | solution.py:506
  (24 shorter events, 0.2 us)
Async XLA Ops:
  0.6 10.1 %copy-start.1 = (s32[1,64,1]{1,2,0:T(1,128)S(1)}, s32[1,64,1]{1,2,0:T(1,128)}, u32[]{:S(2)}) copy-start(s32[1,64,1]{1,2,0:T(1,128)} %param.13) | copy-start | bytes 772
  0.6 10.1 %copy-start.2 = (s32[1,64,4]{1,2,0:T(4,128)S(1)}, s32[1,64,4]{1,2,0:T(4,128)}, u32[]{:S(2)}) copy-start(s32[1,64,4]{1,2,0:T(4,128)} %param.12) | copy-start | bytes 3076
  0.7 15.9 %collective-permute-start.5 = (bf16[128,128]{1,0:T(8,128)(2,1)}, bf16[128,128]{1,0:T(8,128)(2,1)S(1)}, u32[]{:S(2)}, u32[]{:S(2)}) collective-permute-start(bf16[128,128]{1,0:T(8,128)(2,1)} %bitcast.11), channel_id=1, source_target_pairs={{0,1},{1,0},{2,3},{3,2},{4,5},{5,4},{6,7},{7,6},{8,9},{9,8},{10,11... | collective-permute-start | bytes 98312 | tf_op jit(solution)/shard_map/ppermute | solution.py:48
  3.7 13.5 %collective-permute-start.6 = (bf16[128,128]{1,0:T(8,128)(2,1)}, bf16[128,128]{1,0:T(8,128)(2,1)S(1)}, u32[]{:S(2)}, u32[]{:S(2)}) collective-permute-start(bf16[128,128]{1,0:T(8,128)(2,1)} %bitcast.12), channel_id=1, source_target_pairs={{0,2},{1,3},{2,0},{3,1},{4,6},{5,7},{6,4},{7,5},{8,10},{9,11},{10,... | collective-permute-start | bytes 98312 | tf_op jit(solution)/shard_map/ppermute | solution.py:48
  5.3 12.0 %collective-permute-start.7 = (bf16[128,128]{1,0:T(8,128)(2,1)}, bf16[128,128]{1,0:T(8,128)(2,1)S(1)}, u32[]{:S(2)}, u32[]{:S(2)}) collective-permute-start(bf16[128,128]{1,0:T(8,128)(2,1)} %bitcast.13), channel_id=1, source_target_pairs={{0,3},{1,2},{2,1},{3,0},{4,7},{5,6},{6,5},{7,4},{8,11},{9,10},{10,... | collective-permute-start | bytes 98312 | tf_op jit(solution)/shard_map/ppermute | solution.py:48
  5.3 21.3 %collective-permute-start.8 = (bf16[128,128]{1,0:T(8,128)(2,1)}, bf16[128,128]{1,0:T(8,128)(2,1)S(1)}, u32[]{:S(2)}, u32[]{:S(2)}) collective-permute-start(bf16[128,128]{1,0:T(8,128)(2,1)} %bitcast.14), channel_id=1, source_target_pairs={{0,4},{1,5},{2,6},{3,7},{4,0},{5,1},{6,2},{7,3},{8,12},{9,13},{10,... | collective-permute-start | bytes 98312 | tf_op jit(solution)/shard_map/ppermute | solution.py:48
  9.2 12.4 %collective-permute-start = (bf16[256,128]{1,0:T(8,128)(2,1)S(1)}, bf16[256,128]{1,0:T(8,128)(2,1)S(1)}, u32[]{:S(2)}, u32[]{:S(2)}) collective-permute-start(bf16[256,128]{1,0:T(8,128)(2,1)S(1)} %get-tuple-element.29), channel_id=1, source_target_pairs={{0,1},{1,0},{2,3},{3,2},{4,5},{5,4},{6,7},{7,6},{8,9},{9,8},{10,11... | collective-permute-start | bytes 196616 | tf_op jit(solution)/shard_map/ppermute | solution.py:48
  16.6 5.0 %collective-permute-start.1 = (bf16[256,128]{1,0:T(8,128)(2,1)S(1)}, bf16[256,128]{1,0:T(8,128)(2,1)S(1)}, u32[]{:S(2)}, u32[]{:S(2)}) collective-permute-start(bf16[256,128]{1,0:T(8,128)(2,1)S(1)} %get-tuple-element.30), channel_id=1, source_target_pairs={{1,2},{3,4},{5,6},{2,1},{4,3},{6,5},{9,10},{11,12},{13,14},{10,9},... | collective-permute-start | bytes 196616 | tf_op jit(solution)/shard_map/ppermute | solution.py:396
  17.3 9.3 %collective-permute-start.9 = (bf16[384,128]{1,0:T(8,128)(2,1)S(1)}, bf16[384,128]{1,0:T(8,128)(2,1)S(1)}, u32[]{:S(2)}, u32[]{:S(2)}) collective-permute-start(bf16[384,128]{1,0:T(8,128)(2,1)S(1)} %pad_maximum_fusion), channel_id=1, source_target_pairs={{0,4},{1,5},{2,6},{3,7},{4,0},{5,1},{6,2},{7,3},{8,12},{9,13},{10,... | collective-permute-start | bytes 294920 | tf_op jit(solution)/shard_map/ppermute | solution.py:48
  21.6 5.0 %copy-start = (bf16[1,128,128]{2,1,0:T(8,128)(2,1)S(1)}, bf16[1,128,128]{2,1,0:T(8,128)(2,1)}, u32[]{:S(2)}) copy-start(bf16[1,128,128]{2,1,0:T(8,128)(2,1)} %param.15) | copy-start | bytes 98308
  30.2 1.3 %collective-permute-start.10 = (f32[200,128]{1,0:T(8,128)S(1)}, f32[200,128]{1,0:T(8,128)S(1)}, u32[]{:S(2)}, u32[]{:S(2)}) collective-permute-start(f32[200,128]{1,0:T(8,128)S(1)} %get-tuple-element.47), channel_id=1, source_target_pairs={{0,8},{8,0},{16,24},{24,16},{1,9},{9,1},{17,25},{25,17},{2,10},{10... | collective-permute-start | bytes 307208 | tf_op jit(solution)/shard_map/ppermute | solution.py:48
  31.6 8.5 %collective-permute-start.11 = (f32[200,128]{1,0:T(8,128)S(1)}, f32[200,128]{1,0:T(8,128)S(1)}, u32[]{:S(2)}, u32[]{:S(2)}) collective-permute-start(f32[200,128]{1,0:T(8,128)S(1)} %add.27), channel_id=1, source_target_pairs={{0,16},{8,24},{16,0},{24,8},{1,17},{9,25},{17,1},{25,9},{2,18},{10... | collective-permute-start | bytes 307208 | tf_op jit(solution)/shard_map/ppermute | solution.py:48
  37.0 11.2 %collective-permute-start.2 = (bf16[4,128,128]{2,1,0:T(8,128)(2,1)S(1)}, bf16[4,128,128]{2,1,0:T(8,128)(2,1)S(1)}, u32[]{:S(2)}, u32[]{:S(2)}) collective-permute-start(bf16[4,128,128]{2,1,0:T(8,128)(2,1)S(1)} %get-tuple-element.42), channel_id=1, source_target_pairs={{0,1},{1,0},{2,3},{3,2},{4,5},{5,4},{6,7},{7,6},{8,9},{9,8},{10,11... | collective-permute-start | bytes 393224 | tf_op jit(solution)/shard_map/ppermute | solution.py:48
  40.1 5.7 %collective-permute-start.12 = (f32[200,128]{1,0:T(8,128)S(1)}, f32[200,128]{1,0:T(8,128)S(1)}, u32[]{:S(2)}, u32[]{:S(2)}) collective-permute-start(f32[200,128]{1,0:T(8,128)S(1)} %add.28), channel_id=1, source_target_pairs={{0,1},{1,0},{2,3},{3,2},{4,5},{5,4},{6,7},{7,6},{8,9},{9,8},{10,11... | collective-permute-start | bytes 307208 | tf_op jit(solution)/shard_map/ppermute | solution.py:48
  45.8 5.7 %collective-permute-start.13 = (f32[200,128]{1,0:T(8,128)S(1)}, f32[200,128]{1,0:T(8,128)S(1)}, u32[]{:S(2)}, u32[]{:S(2)}) collective-permute-start(f32[200,128]{1,0:T(8,128)S(1)} %add.29), channel_id=1, source_target_pairs={{0,2},{1,3},{2,0},{3,1},{4,6},{5,7},{6,4},{7,5},{8,10},{9,11},{10,... | collective-permute-start | bytes 307208 | tf_op jit(solution)/shard_map/ppermute | solution.py:48
  48.3 4.5 %collective-permute-start.3 = (bf16[2,128,128]{2,1,0:T(8,128)(2,1)S(1)}, bf16[2,128,128]{2,1,0:T(8,128)(2,1)S(1)}, u32[]{:S(2)}, u32[]{:S(2)}) collective-permute-start(bf16[2,128,128]{2,1,0:T(8,128)(2,1)S(1)} %slice.43), channel_id=1, source_target_pairs={{0,2},{1,3},{2,0},{3,1},{4,6},{5,7},{6,4},{7,5},{8,10},{9,11},{10,... | collective-permute-start | bytes 196616 | tf_op jit(solution)/shard_map/ppermute | solution.py:48
  51.5 7.1 %collective-permute-start.14 = (f32[200,128]{1,0:T(8,128)S(1)}, f32[200,128]{1,0:T(8,128)S(1)}, u32[]{:S(2)}, u32[]{:S(2)}) collective-permute-start(f32[200,128]{1,0:T(8,128)S(1)} %add.30), channel_id=1, source_target_pairs={{0,4},{1,5},{2,6},{3,7},{4,0},{5,1},{6,2},{7,3},{8,12},{9,13},{10,... | collective-permute-start | bytes 307208 | tf_op jit(solution)/shard_map/ppermute | solution.py:48
  52.8 6.1 %collective-permute-start.4 = (bf16[1,128,128]{2,1,0:T(8,128)(2,1)S(1)}, bf16[1,128,128]{2,1,0:T(8,128)(2,1)S(1)}, u32[]{:S(2)}, u32[]{:S(2)}) collective-permute-start(bf16[1,128,128]{2,1,0:T(8,128)(2,1)S(1)} %slice.44), channel_id=1, source_target_pairs={{0,4},{1,5},{2,6},{3,7},{4,0},{5,1},{6,2},{7,3},{8,12},{9,13},{10,... | collective-permute-start | bytes 98312 | tf_op jit(solution)/shard_map/ppermute | solution.py:48
  58.6 1.4 %collective-permute-start.15 = (f32[200,128]{1,0:T(8,128)S(1)}, f32[200,128]{1,0:T(8,128)S(1)}, u32[]{:S(2)}, u32[]{:S(2)}) collective-permute-start(f32[200,128]{1,0:T(8,128)S(1)} %add.31.refs_0_), channel_id=1, source_target_pairs={{0,8},{8,0},{16,24},{24,16},{1,9},{9,1},{17,25},{25,17},{2,10},{10... | collective-permute-start | bytes 307208 | tf_op jit(solution)/shard_map/ppermute | solution.py:48

commit v3 on v2

v3 whole, which is shorter than its diff:
```python
import math

import jax
import jax.numpy as jnp
from jax import lax
from jax.experimental import pallas as pl
from jax.experimental.pallas import tpu as pltpu
from jax.sharding import PartitionSpec as P


H = 128
TILE = 128
NBR = 4
HT = 2
QUAD = 4
F32 = jnp.float32
BF16 = jnp.bfloat16
MARGIN = HT * TILE
HALF = H // 2
PACK = 3 * HALF
LOW_ROUNDS = 1


def dot(a, b, ca=1, cb=0):
    return lax.dot_general(a, b, (((ca,), (cb,)), ((), ())), preferred_element_type=F32)


def split(x):
    hi = x.astype(BF16)
    return hi, (x - hi.astype(F32)).astype(BF16)


def diagonal(a, b):
    top = jnp.concatenate([a, jnp.zeros(b.shape, b.dtype)], axis=1)
    low = jnp.concatenate([jnp.zeros(a.shape, a.dtype), b], axis=1)
    return jnp.concatenate([top, low], axis=0)


def beside(a, b):
    return jnp.concatenate([a, b], axis=1)


def bit_order(count):
    bits = count.bit_length() - 1
    return [sum(((q >> b) & 1) << (bits - 1 - b) for b in range(bits)) for q in range(count)]


def exchange(x, axis, mask):
    return lax.ppermute(x, axis, [(i, i ^ mask) for i in range(lax.axis_size(axis))])


def rows_at(tile, count=1):
    if isinstance(tile, int):
        return pl.ds(tile * TILE, count * TILE)
    return pl.ds(pl.multiple_of(tile * TILE, TILE), count * TILE)


def pack_kernel(nodes, cot, near, far, sem):
    odd = lax.axis_index("graph") & 1
    gap = nodes.shape[0] - MARGIN
    near_at = pl.multiple_of((1 - odd) * gap, TILE)
    far_at = pl.multiple_of(odd * gap, TILE)
    copies = [
        pltpu.make_async_copy(cot, near.at[pl.ds(0, TILE)], sem.at[0]),
        pltpu.make_async_copy(
            nodes.at[pl.ds(near_at, MARGIN)], near.at[pl.ds(TILE, MARGIN)], sem.at[1]
        ),
        pltpu.make_async_copy(nodes.at[pl.ds(far_at, MARGIN)], far, sem.at[2]),
    ]
    for copy in copies:
        copy.start()
    for copy in copies:
        copy.wait()


def join_weights(w_msg, w_in, wcat):
    wcat[:H] = (0.5 * w_in[:H].astype(F32)).astype(BF16)
    wcat[H:] = (0.5 * dot(w_msg[...], w_in[H:])).astype(BF16)


def shares(quads):
    order = sorted(range(quads), key=lambda q: abs(2 * q - quads + 1))
    one, two = quads * 3 // 8, quads * 6 // 8
    return sorted(order[:one]), sorted(order[one:two]), sorted(order[two:])


def run_stages(count, *stages):
    held = {}
    for tick in range(count + len(stages) - 1):
        for k, stage in enumerate(stages):
            i = tick - k
            if 0 <= i < count:
                held[k, i] = stage(i, held.get((k - 1, i)))


def forward_quads(quads, src, dst, nodes, adj, pw, wcat, bias, outs, acc, edges=None):
    a_out, act_out, slope_out = outs
    me = lax.axis_index("graph")
    h_bias = 0.5 * bias[...]
    total = slope_out.shape[0]
    ends = {0: 0, total // QUAD - 1: 2 * (QUAD + 2 * HT) - total - 2 * HT}

    def gather(i, _):
        sums = []
        for j in range(QUAD):
            t = quads[i] * QUAD + j
            held, shift = (edges, ends[quads[i]]) if quads[i] in ends else (nodes, -HT)
            picked = [held[rows_at(src[k, t] + shift), :] for k in range(NBR)]
            weights = jnp.concatenate([adj[t, k] for k in range(NBR)], axis=1)
            sums.append(dot(weights, jnp.concatenate(picked, axis=0)).astype(BF16))
        summed = jnp.concatenate(sums, axis=0)
        a_out[rows_at(quads[i] * QUAD, QUAD), :] = summed
        return summed

    def activate(i, summed):
        first = quads[i] * QUAD
        own = nodes[rows_at(first, QUAD), :]
        h = dot(beside(own, summed), wcat[...]) + h_bias
        s = jnp.tanh(h)
        hs = h * s
        act = (h + hs).astype(BF16)
        act_out[rows_at(first, QUAD), :] = act
        slope = (1.0 + s) * ((1.0 + h) - hs)
        for j in range(QUAD):
            slope_out[first + j] = slope[j * TILE : (j + 1) * TILE].T
        return act

    def pool(i, act):
        add_pooled(quads[i] * QUAD, act, dst, me, pw, acc)

    run_stages(len(quads), gather, activate, pool)


def add_pooled(first, values, dst, me, pw, acc):
    for j in range(0, QUAD, 2):
        a, b = values[j * TILE : (j + 1) * TILE], values[(j + 1) * TILE : (j + 2) * TILE]
        t = first + j
        term = dot(beside(pw[t], pw[t + 1]), diagonal(a, b))
        acc[dst[0, t] ^ me] += term[:, :H]
        acc[dst[0, t + 1] ^ me] += term[:, H:]


def start_kernel(
    quads, src, dst, nodes, adj, pw, w_msg, w_in, bias, a_out, act_out, slope_out, acc, wcat
):
    join_weights(w_msg, w_in, wcat)
    acc[...] = jnp.zeros_like(acc)
    outs = (a_out, act_out, slope_out)
    forward_quads(quads, src, dst, nodes, adj, pw, wcat, bias, outs, acc)


def middle_kernel(
    quads, src, dst, nodes, adj, pw, wcat, bias, a_in, act_in, slope_in, acc_in,
    a_out, act_out, slope_out, acc,
):
    outs = (a_out, act_out, slope_out)
    forward_quads(quads, src, dst, nodes, adj, pw, wcat, bias, outs, acc)


def last_kernel(
    quads, order, src, dst, near, far, nodes, adj, pw, wcat, bias, w_out,
    a_in, act_in, slope_in, acc_in,
    a_out, act_out, slope_out, p_out, fine, send, keep,
    acc, pooled, edges, wdiag, out_v, sem,
):
    me = lax.axis_index("graph")
    odd = me & 1
    size = edges.shape[0]
    span = size // 2 - MARGIN
    edges[MARGIN : MARGIN + span] = nodes[:span]
    edges[size - MARGIN - span : size - MARGIN] = nodes[nodes.shape[0] - span :]
    edges[pl.ds(pl.multiple_of((1 - odd) * (size - MARGIN), TILE), MARGIN), :] = near[TILE:]
    edges[pl.ds(pl.multiple_of(odd * (size - MARGIN), TILE), MARGIN), :] = far[...]
    wdiag[...] = diagonal(w_out[...], w_out[...])
    acc[...] = acc_in[...]
    pooled[...] = jnp.zeros_like(pooled)
    outs = (a_out, act_out, slope_out)
    forward_quads(quads, src, dst, nodes, adj, pw, wcat, bias, outs, acc, edges)
    for r in range(acc.shape[0]):
        hi, lo = split(acc[r])
        p_out[r * TILE : (r + 1) * TILE, :H] = hi
        p_out[r * TILE : (r + 1) * TILE, H:] = lo

    half = QUAD * TILE // 2
    count = nodes.shape[0] // (QUAD * TILE)
    copies = []

    def project(i, _):
        act = act_out[rows_at(i * QUAD, QUAD), :]
        return dot(beside(act[:half], act[half:]), wdiag[...])

    def update(i, delta):
        part = rows_at(i * QUAD, QUAD)
        own = nodes[part, :].astype(F32)
        out = jnp.concatenate([own[:half] + delta[:, :H], own[half:] + delta[:, H:]], axis=0)
        out = out.astype(BF16)
        out_v[part, :] = out
        copies.append(pltpu.make_async_copy(out_v.at[part], fine.at[part], sem.at[i]))
        copies[-1].start()
        return out

    def pool(i, out):
        add_pooled(i * QUAD, out, dst, me, pw, pooled)

    run_stages(count, project, update, pool)
    slabs = len(order)
    for q, r in enumerate(order):
        if q < slabs // 2:
            keep[q] = pooled[r]
        else:
            send[q - slabs // 2] = pooled[r].astype(BF16)
    for copy in copies:
        copy.wait()


def backward_kernel(pieces, dst, *refs):
    cots = refs[:pieces]
    (nodes, a_in, slope_in, pw, p_in, w_out) = refs[pieces : pieces + 6]
    keep, send, cot_all, cot_w, total, bias, mats = refs[pieces + 6 :]
    me = lax.axis_index("graph")
    core = lax.axis_index("design") & 1
    at = 0
    for cot in cots:
        size = cot.shape[0]
        cot_all[at : at + size] = cot[...]
        at += size
    for r in range(cot_w.shape[0]):
        tile = cot_all[r * TILE : (r + 1) * TILE]
        cot_w[r] = (0.5 * dot(w_out[...], tile, 1, 1)).astype(BF16)
    both = dot(cot_all[...], p_in[...], 0, 0)
    mats[0] = both[:, :H] + both[:, H:]
    total[...] = jnp.zeros_like(total)
    bias[...] = jnp.zeros_like(bias)

    firsts = list(range(0, slope_in.shape[0], QUAD))

    def unpool(i, _):
        parts = []
        for j in range(0, QUAD, 2):
            t = firsts[i] + j
            left = beside(cot_w[dst[0, t] ^ me], cot_w[dst[0, t + 1] ^ me])
            parts.append(dot(left, diagonal(pw[t], pw[t + 1])))
        return parts

    def slopes(i, parts):
        done = []
        for j, part in enumerate(parts):
            t = firsts[i] + 2 * j
            grad = part * beside(slope_in[t], slope_in[t + 1])
            bias[...] += grad
            done.append(grad.astype(BF16))
        return jnp.concatenate(done, axis=1)

    def weights(i, grad_pre):
        own = nodes[rows_at(firsts[i], QUAD), :]
        total[...] += dot(grad_pre, beside(own, a_in[rows_at(firsts[i], QUAD), :]))

    run_stages(len(firsts), unpool, slopes, weights)

    mats[1] = total[:, :H]
    mats[2] = total[:, H:]
    column = jnp.sum(bias[...], axis=1, keepdims=True)
    row = jnp.broadcast_to(column, (H, H)).T[:8]
    for out, half in ((keep, core), (send, 1 - core)):
        for m in range(3):
            at = pl.multiple_of(half * HALF, HALF)
            out[m * HALF : (m + 1) * HALF] = mats[m, pl.ds(at, HALF), :]
        out[PACK:] = row


def finish_kernel(scale, held, other, w_msg, w_in, g_msg, g_in, g_bias, g_out, mats):
    core = lax.axis_index("design") & 1
    for part, half in ((held, core), (other, 1 - core)):
        for m in range(3):
            at = pl.multiple_of(half * HALF, HALF)
            mats[m, pl.ds(at, HALF), :] = part[m * HALF : (m + 1) * HALF] * scale
    g_out[...] = mats[0].T
    g_in[:H] = mats[1].T
    hi, lo = split(mats[2])
    g_in[H:] = dot(w_msg[...], hi, 0, 1) + dot(w_msg[...], lo, 0, 1)
    w_low = w_in[H:]
    g_msg[...] = dot(hi, w_low, 0, 1) + dot(lo, w_low, 0, 1)
    g_bias[...] = jnp.where(core == 0, held[PACK : PACK + 1], other[PACK : PACK + 1]) * scale


def layer(
    nodes, adjacency, tile_src, pool_dst, pool_weight, coarse_cot, w_msg, w_in, b_in, w_out
):
    def stay(x):
        return pltpu.with_memory_space_constraint(x, pltpu.HBM)

    feats = nodes[0]
    adj = adjacency[0]
    src = tile_src[0].T
    dst = pool_dst[0].T
    pw = pool_weight[0]
    cot = coarse_cot[0]
    rows = feats.shape[0]
    count = rows // TILE
    slabs = lax.axis_size("graph")
    designs = lax.axis_size("design")
    assert slabs & (slabs - 1) == 0 and designs & (designs - 1) == 0
    assert slabs > 1 and designs > 1
    assert count % (8 * QUAD) == 0
    one, two, three = shares(count // QUAD)
    bias = b_in.reshape(1, H)

    smem = pl.BlockSpec(memory_space=pltpu.SMEM)
    vmem = pl.BlockSpec(memory_space=pltpu.VMEM)
    hbm = pl.BlockSpec(memory_space=pl.ANY)

    def shape(*dims, dtype=F32):
        return jax.ShapeDtypeStruct(dims, dtype)

    def params(mib):
        return pltpu.CompilerParams(vmem_limit_bytes=mib * 1024 * 1024)

    def cost(units, mib, trans=0):
        return pl.CostEstimate(
            flops=2 * units * rows * H * H,
            bytes_accessed=mib * 1024 * 1024,
            transcendentals=trans,
        )

    near_send, far_send = pl.pallas_call(
        pack_kernel,
        in_specs=[hbm, hbm],
        out_specs=[vmem, vmem],
        out_shape=[shape(TILE + MARGIN, H, dtype=BF16), shape(MARGIN, H, dtype=BF16)],
        scratch_shapes=[pltpu.SemaphoreType.DMA((3,))],
        compiler_params=params(1),
        cost_estimate=cost(40, 40),
        name="pack",
    )(stay(feats), stay(cot))
    near = exchange(near_send, "graph", 1)
    across = [(i, i + 1) for i in range(1, slabs - 1, 2)]
    far = lax.ppermute(far_send, "graph", across + [(b, a) for a, b in across])

    row_shape = shape(rows, H, dtype=BF16)
    slope_shape = shape(count, H, TILE)
    acc_shape = shape(slabs, TILE, H)
    wcat_shape = shape(2 * H, H, dtype=BF16)
    state = [row_shape, row_shape, slope_shape]

    *held, wcat = pl.pallas_call(
        lambda *refs: start_kernel(one, *refs),
        in_specs=[smem, smem, vmem, vmem, vmem, vmem, vmem, vmem],
        out_specs=[vmem] * 5,
        out_shape=[*state, acc_shape, wcat_shape],
        compiler_params=params(8),
        cost_estimate=cost(3, 8, rows * H * 3 // 8),
        name="start",
    )(src, dst, feats, adj, pw, w_msg, w_in, bias)

    cots = [near_send[:TILE], near[:TILE]]
    pair = exchange(jnp.concatenate(cots, axis=0), "graph", 2) if slabs > 2 else None

    held = pl.pallas_call(
        lambda *refs: middle_kernel(two, *refs),
        in_specs=[smem, smem, vmem, vmem, vmem, vmem, vmem] + [vmem] * 4,
        out_specs=[vmem] * 4,
        out_shape=[*state, acc_shape],
        input_output_aliases={7: 0, 8: 1, 9: 2, 10: 3},
        compiler_params=params(8),
        cost_estimate=cost(3, 8, rows * H * 3 // 8),
        name="middle",
    )(src, dst, feats, adj, pw, wcat, bias, *held)

    if slabs > 2:
        cots.append(pair)
    for b in range(2, slabs.bit_length() - 1):
        cots.append(exchange(jnp.concatenate(cots, axis=0), "graph", 1 << b))

    order = bit_order(slabs)
    a_all, _, slope_all, p_all, fine, c_send, c_keep = pl.pallas_call(
        lambda *refs: last_kernel(three, order, *refs),
        in_specs=[smem, smem, vmem, vmem, vmem, vmem, vmem, vmem, vmem, vmem]
        + [vmem] * 4,
        out_specs=[vmem] * 4 + [hbm] + [vmem] * 2,
        out_shape=[
            *state,
            shape(slabs * TILE, 2 * H, dtype=BF16),
            row_shape,
            shape(slabs // 2, TILE, H, dtype=BF16),
            shape(slabs // 2, TILE, H),
        ],
        scratch_shapes=[
            pltpu.VMEM((slabs, TILE, H), F32),
            pltpu.VMEM((slabs, TILE, H), F32),
            pltpu.VMEM((2 * (QUAD + 2 * HT) * TILE, H), BF16),
            pltpu.VMEM((2 * H, 2 * H), BF16),
            pltpu.VMEM((rows, H), BF16),
            pltpu.SemaphoreType.DMA((count // QUAD,)),
        ],
        input_output_aliases={10: 0, 11: 1, 12: 2},
        compiler_params=params(16),
        cost_estimate=cost(4, 8, rows * H // 4),
        name="last",
    )(src, dst, near, far, feats, adj, pw, wcat, bias, w_out, *held)
    c_got = exchange(c_send, "graph", 1)

    every = cots
    keep, send = pl.pallas_call(
        lambda *refs: backward_kernel(len(every), *refs),
        in_specs=[smem]
        + [vmem] * len(every)
        + [vmem] * 5
        + [vmem],
        out_specs=[vmem, vmem],
        out_shape=[shape(PACK + 8, H)] * 2,
        scratch_shapes=[
            pltpu.VMEM((slabs * TILE, H), BF16),
            pltpu.VMEM((slabs, H, TILE), BF16),
            pltpu.VMEM((H, 2 * H), F32),
            pltpu.VMEM((H, 2 * H), F32),
            pltpu.VMEM((3, H, H), F32),
        ],
        compiler_params=params(16),
        cost_estimate=cost(3, 4),
        name="backward",
    )(dst, *every, feats, a_all, slope_all, pw, p_all, w_out)

    held = c_keep + c_got.astype(F32)
    mask = 2
    while mask < slabs:
        size = held.shape[0] // 2
        got = exchange(held[size:].astype(BF16), "graph", mask)
        held = held[:size] + got.astype(F32)
        mask *= 2
    coarse = held[0].astype(BF16)

    rounds = [("design", 1 << b) for b in range(1, designs.bit_length() - 1)]
    rounds += [("graph", 1 << b) for b in range(slabs.bit_length() - 1)]
    mine = keep + exchange(send, "design", 1)
    for n, (axis, mask) in enumerate(rounds):
        if n < len(rounds) - LOW_ROUNDS:
            mine = mine + exchange(mine, axis, mask)
        else:
            low = mine.astype(BF16)
            mine = low.astype(F32) + exchange(low, axis, mask).astype(F32)
    other = exchange(mine, "design", 1)
    scale = 1.0 / math.sqrt(designs * rows * slabs)
    g_msg, g_in, g_bias, g_out = pl.pallas_call(
        lambda *refs: finish_kernel(scale, *refs),
        in_specs=[vmem] * 4,
        out_specs=[vmem] * 4,
        out_shape=[shape(H, H), shape(2 * H, H), shape(1, H), shape(H, H)],
        scratch_shapes=[pltpu.VMEM((3, H, H), F32)],
        compiler_params=params(4),
        name="finish",
    )(mine, other, w_msg, w_in)
    return fine[None], coarse[None], g_msg, g_in, g_bias.reshape(H), g_out


def solution(mesh):
    in_specs = (
        P("design", "graph", None),
        P("design", "graph", None, None, None),
        P("design", "graph", None),
        P("design", "graph", None),
        P("design", "graph", None, None),
        P("design", "graph", None),
        P(),
        P(),
        P(),
        P(),
    )
    out_specs = (P("design", "graph", None), P("design", "graph", None), P(), P(), P(), P())
    return jax.shard_map(layer, mesh=mesh, in_specs=in_specs, out_specs=out_specs, check_vma=False)
```

time: 62.1 us -> 48.7 us (0.78)
  Pallas kernels: 20.8 us -> 13.2 us
  starting transfers between devices: 24.6 us -> 18.4 us
    pallas_call x6, Pallas kernels: 20.8 us -> 13.2 us  [the longest x1 3.99 us: layer(): pl.pallas_call(lambda *refs: last_kernel(three, order, *refs), in_specs=[...]
    ppermute x15 -> x12, starting transfers between devices: 23.9 us -> 17.8 us  [exchange(): lax.ppermute(x, axis, [(i, i ^ mask) for i in range(lax.axis_size(axis))])]
    ppermute x15 -> x12, waiting for transfers between devices: 14.7 us -> 15.2 us  [exchange(): lax.ppermute(x, axis, [(i, i ^ mask) for i in range(lax.axis_size(axis))])]
  transfers between devices with their start and end apart: 16 -> 13, of which waited for: 6 -> 8; matrix products, arithmetic and copies ran while one was open for 1% -> 2% of each run, Pallas kernels for 25% -> 18%
where the time goes in v3:
time: 48.7 us; the launch traced here: 48.6 us
  starting transfers between devices  18.4 us (38%)
  waiting for transfers between devices  15.2 us (31%)
  Pallas kernels  13.2 us (27%)
  between operations  0.91 us (2%)
  other arithmetic  0.76 us (2%)
    ppermute x12, starting transfers between devices, exchange(): lax.ppermute(x, axis, [(i, i ^ mask) for i in range(lax.axis_size(axis))])  17.8 us
    ppermute x12, waiting for transfers between devices, exchange(): lax.ppermute(x, axis, [(i, i ^ mask) for i in range(lax.axis_size(axis))])  15.2 us
    pallas_call x1, Pallas kernels, layer(): pl.pallas_call(lambda *refs: last_kernel(three, order, *refs), in_specs=[...  3.99 us
    pallas_call x1, Pallas kernels, layer(): pl.pallas_call(lambda *refs: backward_kernel(len(every), *refs), in_specs...  2.52 us
    pallas_call x1, Pallas kernels, layer(): pl.pallas_call(lambda *refs: start_kernel(one, *refs), in_specs=[smem, sm...  2.42 us
    pallas_call x1, Pallas kernels, layer(): pl.pallas_call(lambda *refs: middle_kernel(two, *refs), in_specs=[smem, s...  2.33 us
    pallas_call x1, Pallas kernels, layer(): pl.pallas_call(pack_kernel, in_specs=[hbm, hbm], out_specs=[vmem, vmem],...  1.06 us
  transfers between devices with their start and end apart: 13, of which 8 were waited for; matrix products, arithmetic and copies ran while one was open for 2% of the time, Pallas kernels for 18%

profile of v3, /device:TPU:0, one launch (start us, length us, event | category | flops | bytes accessed | tf_op | source)
XLA Modules:
  0.0 48.6 jit_solution(2523934260773905382)
XLA Ops:
  0.6 0.0 slice-start
  0.6 0.0 slice-start.1
  0.7 1.1 %pack.1 = (bf16[384,128]{1,0:T(8,128)(2,1)S(1)}, bf16[256,128]{1,0:T(8,128)(2,1)S(1)}) custom-call(bf16[8192,128]{1,0:T(8,128)(2,1)} %bitcast.16, bf16[128,128]{1,0:T(8,128)(2,1)} %bitcast.36), custom_call_target="tpu_custom_call" | custom-call | flops 10737418240 | bytes 41943040 | tf_op jit(solution)/shard_map/pack/pallas_call | solution.py:325
  1.8 3.1 %collective-permute-start = (bf16[384,128]{1,0:T(8,128)(2,1)S(1)}, bf16[384,128]{1,0:T(8,128)(2,1)S(1)}, u32[]{:S(2)}, u32[]{:S(2)}) collective-permute-start(bf16[384,128]{1,0:T(8,128)(2,1)S(1)} %get-tuple-element.29), channel_id=1, source_target_pairs={{0,1},{1,0},{2,3},{3,2},{4,5},{5,4},{6,7},{7,6},{8,9},{9,8},{10,11... | collective-permute-start | bytes 294920 | tf_op jit(solution)/shard_map/ppermute | solution.py:49
  4.9 0.7 %collective-permute-start.1 = (bf16[256,128]{1,0:T(8,128)(2,1)S(1)}, bf16[256,128]{1,0:T(8,128)(2,1)S(1)}, u32[]{:S(2)}, u32[]{:S(2)}) collective-permute-start(bf16[256,128]{1,0:T(8,128)(2,1)S(1)} %get-tuple-element.30), channel_id=1, source_target_pairs={{1,2},{3,4},{5,6},{2,1},{4,3},{6,5},{9,10},{11,12},{13,14},{10,9},... | collective-permute-start | bytes 196616 | tf_op jit(solution)/shard_map/ppermute | solution.py:337
  5.5 2.1 %collective-permute-done.refs_2_ = bf16[384,128]{1,0:T(8,128)(2,1)S(1)} collective-permute-done((bf16[384,128]{1,0:T(8,128)(2,1)S(1)}, bf16[384,128]{1,0:T(8,128)(2,1)S(1)}, u32[]{:S(2)}, u32[]{:S(2)}) %collective-permute-start) | collective-permute-done | bytes 98336 | tf_op jit(solution)/shard_map/ppermute | solution.py:49
  7.7 1.9 %collective-permute-start.5 = (bf16[256,128]{1,0:T(8,128)(2,1)S(1)}, bf16[256,128]{1,0:T(8,128)(2,1)S(1)}, u32[]{:S(2)}, u32[]{:S(2)}) collective-permute-start(bf16[256,128]{1,0:T(8,128)(2,1)S(1)} %pad_maximum_fusion.1), channel_id=1, source_target_pairs={{0,2},{1,3},{2,0},{3,1},{4,6},{5,7},{6,4},{7,5},{8,10},{9,11},{10,... | collective-permute-start | bytes 196616 | tf_op jit(solution)/shard_map/ppermute | solution.py:49
  9.7 2.4 %start.1 = (bf16[8192,128]{1,0:T(8,128)(2,1)S(1)}, bf16[8192,128]{1,0:T(8,128)(2,1)S(1)}, f32[64,128,128]{2,1,0:T(8,128)S(1)}, f32[8,128,128]{2,1,0:T(8,128)S(1)}, bf16[256,128]{1,0:T(8,128)(2,1)S(1)}) custom-call(s32[4,64]{1,0:T(4,128)S(1)} %bitcast.25, s32[1,64]{1,0:T(1,128)S(1)} %bitcast.28, bf16[8192,128]{1,0:T(8,128)(2,1)S(1)} %bitcast.17, ...), custom_call_target="tpu_custom_call" | custom-call | flops 805306368 | bytes 8388608 | tf_op jit(solution)/shard_map/start/pallas_call | solution.py:345
  12.1 0.0 collective-permute-done.5.refs_3_
  12.1 2.8 %collective-permute-start.6 = (bf16[512,128]{1,0:T(8,128)(2,1)S(1)}, bf16[512,128]{1,0:T(8,128)(2,1)S(1)}, u32[]{:S(2)}, u32[]{:S(2)}) collective-permute-start(bf16[512,128]{1,0:T(8,128)(2,1)S(1)} %pad_maximum_fusion), channel_id=1, source_target_pairs={{0,4},{1,5},{2,6},{3,7},{4,0},{5,1},{6,2},{7,3},{8,12},{9,13},{10,... | collective-permute-start | bytes 393224 | tf_op jit(solution)/shard_map/ppermute | solution.py:49
  15.0 2.3 %middle.1 = (bf16[8192,128]{1,0:T(8,128)(2,1)S(1)}, bf16[8192,128]{1,0:T(8,128)(2,1)S(1)}, f32[64,128,128]{2,1,0:T(8,128)S(1)}, f32[8,128,128]{2,1,0:T(8,128)S(1)}) custom-call(s32[4,64]{1,0:T(4,128)S(1)} %bitcast.26, s32[1,64]{1,0:T(1,128)S(1)} %bitcast.29, ...), custom_call_target="tpu_custom_call", output_to_operand_aliasing={{0}: (7, {}), {1}: (8, {}), {2}: (9, {}), {3}: (10, {})} | custom-call | flops 805306368 | bytes 8388608 | tf_op jit(solution)/shard_map/middle/pallas_call | solution.py:358
  17.3 4.0 %last.1 = (bf16[8192,128]{1,0:T(8,128)(2,1)S(1)}, bf16[8192,128]{1,0:T(8,128)(2,1)S(1)}, f32[64,128,128]{2,1,0:T(8,128)S(1)}, bf16[1024,256]{1,0:T(8,128)(2,1)S(...) custom-call(s32[4,64]{1,0:T(4,128)S(1)} %bitcast.27, ...), custom_call_target="tpu_custom_call", output_to_operand_aliasing={{0}: (10, {}), {1}: (11, {}), {2}: (12, {})} | custom-call | flops 1073741824 | bytes 8388608 | tf_op jit(solution)/shard_map/last/pallas_call | solution.py:375
  21.3 2.5 %backward.1 = (f32[200,128]{1,0:T(8,128)S(1)}, f32[200,128]{1,0:T(8,128)S(1)}) custom-call(s32[1,64]{1,0:T(1,128)S(1)} %bitcast.31, bf16[128,128]{1,0:T(8,128)(2,1)S(1)} %slice.24.refs_1_, bf16[128,128]{1,0:T(8,128)(2,1)S(1)} %slice.30.refs_2_, bf16[256,128]{1,0:T(8,128)(2,1)S(1)} %collective-permute-done.5.refs_3_, ...), custom_call_target="tpu_custom_call" | custom-call | flops 805306368 | bytes 4194304 | tf_op jit(solution)/shard_map/backward/pallas_call | solution.py:403
  23.8 0.1 collective-permute-start.7
  23.9 1.3 %collective-permute-done.7 = f32[200,128]{1,0:T(8,128)S(1)} collective-permute-done((f32[200,128]{1,0:T(8,128)S(1)}, f32[200,128]{1,0:T(8,128)S(1)}, u32[]{:S(2)}, u32[]{:S(2)}) %collective-permute-start.7) | collective-permute-done | bytes 102432 | tf_op jit(solution)/shard_map/ppermute | solution.py:49
  25.2 1.6 %collective-permute-start.8 = (f32[200,128]{1,0:T(8,128)S(1)}, f32[200,128]{1,0:T(8,128)S(1)}, u32[]{:S(2)}, u32[]{:S(2)}) collective-permute-start(f32[200,128]{1,0:T(8,128)S(1)} %add.27), channel_id=1, source_target_pairs={{0,16},{8,24},{16,0},{24,8},{1,17},{9,25},{17,1},{25,9},{2,18},{10... | collective-permute-start | bytes 307208 | tf_op jit(solution)/shard_map/ppermute | solution.py:49
  26.8 2.1 %collective-permute-start.2 = (bf16[4,128,128]{2,1,0:T(8,128)(2,1)S(1)}, bf16[4,128,128]{2,1,0:T(8,128)(2,1)S(1)}, u32[]{:S(2)}, u32[]{:S(2)}) collective-permute-start(bf16[4,128,128]{2,1,0:T(8,128)(2,1)S(1)} %get-tuple-element.42), channel_id=1, source_target_pairs={{0,1},{1,0},{2,3},{3,2},{4,5},{5,4},{6,7},{7,6},{8,9},{9,8},{10,11... | collective-permute-start | bytes 393224 | tf_op jit(solution)/shard_map/ppermute | solution.py:49
  28.9 1.3 %collective-permute-done.8 = f32[200,128]{1,0:T(8,128)S(1)} collective-permute-done((f32[200,128]{1,0:T(8,128)S(1)}, f32[200,128]{1,0:T(8,128)S(1)}, u32[]{:S(2)}, u32[]{:S(2)}) %collective-permute-start.8) | collective-permute-done | bytes 102432 | tf_op jit(solution)/shard_map/ppermute | solution.py:49
  30.3 2.2 %collective-permute-start.9 = (f32[200,128]{1,0:T(8,128)S(1)}, f32[200,128]{1,0:T(8,128)S(1)}, u32[]{:S(2)}, u32[]{:S(2)}) collective-permute-start(f32[200,128]{1,0:T(8,128)S(1)} %add.28), channel_id=1, source_target_pairs={{0,1},{1,0},{2,3},{3,2},{4,5},{5,4},{6,7},{7,6},{8,9},{9,8},{10,11... | collective-permute-start | bytes 307208 | tf_op jit(solution)/shard_map/ppermute | solution.py:49
  32.5 2.6 %collective-permute-done.9 = f32[200,128]{1,0:T(8,128)S(1)} collective-permute-done((f32[200,128]{1,0:T(8,128)S(1)}, f32[200,128]{1,0:T(8,128)S(1)}, u32[]{:S(2)}, u32[]{:S(2)}) %collective-permute-start.9) | collective-permute-done | bytes 102432 | tf_op jit(solution)/shard_map/ppermute | solution.py:49
  35.1 1.5 %collective-permute-start.10 = (f32[200,128]{1,0:T(8,128)S(1)}, f32[200,128]{1,0:T(8,128)S(1)}, u32[]{:S(2)}, u32[]{:S(2)}) collective-permute-start(f32[200,128]{1,0:T(8,128)S(1)} %add.29), channel_id=1, source_target_pairs={{0,2},{1,3},{2,0},{3,1},{4,6},{5,7},{6,4},{7,5},{8,10},{9,11},{10,... | collective-permute-start | bytes 307208 | tf_op jit(solution)/shard_map/ppermute | solution.py:49
  36.7 0.6 %collective-permute-start.3 = (bf16[2,128,128]{2,1,0:T(8,128)(2,1)S(1)}, bf16[2,128,128]{2,1,0:T(8,128)(2,1)S(1)}, u32[]{:S(2)}, u32[]{:S(2)}) collective-permute-start(bf16[2,128,128]{2,1,0:T(8,128)(2,1)S(1)} %slice.37), channel_id=1, source_target_pairs={{0,2},{1,3},{2,0},{3,1},{4,6},{5,7},{6,4},{7,5},{8,10},{9,11},{10,... | collective-permute-start | bytes 196616 | tf_op jit(solution)/shard_map/ppermute | solution.py:49
  37.3 2.5 %collective-permute-done.10 = f32[200,128]{1,0:T(8,128)S(1)} collective-permute-done((f32[200,128]{1,0:T(8,128)S(1)}, f32[200,128]{1,0:T(8,128)S(1)}, u32[]{:S(2)}, u32[]{:S(2)}) %collective-permute-start.10) | collective-permute-done | bytes 102432 | tf_op jit(solution)/shard_map/ppermute | solution.py:49
  39.9 0.4 collective-permute-start.11
  40.3 1.3 %collective-permute-done.3 = bf16[2,128,128]{2,1,0:T(8,128)(2,1)S(1)} collective-permute-done((bf16[2,128,128]{2,1,0:T(8,128)(2,1)S(1)}, bf16[2,128,128]{2,1,0:T(8,128)(2,1)S(1)}, u32[]{:S(2)}, u32[]{:S(2)}) %collective-permute-start.3) | collective-permute-done | bytes 65568 | tf_op jit(solution)/shard_map/ppermute | solution.py:49
  41.6 1.3 %collective-permute-start.4 = (bf16[1,128,128]{2,1,0:T(8,128)(2,1)S(1)}, bf16[1,128,128]{2,1,0:T(8,128)(2,1)S(1)}, u32[]{:S(2)}, u32[]{:S(2)}) collective-permute-start(bf16[1,128,128]{2,1,0:T(8,128)(2,1)S(1)} %slice.38), channel_id=1, source_target_pairs={{0,4},{1,5},{2,6},{3,7},{4,0},{5,1},{6,2},{7,3},{8,12},{9,13},{10,... | collective-permute-start | bytes 98312 | tf_op jit(solution)/shard_map/ppermute | solution.py:49
  43.0 2.0 %collective-permute-done.11 = bf16[200,128]{1,0:T(8,128)(2,1)S(1)} collective-permute-done((bf16[200,128]{1,0:T(8,128)(2,1)S(1)}, bf16[200,128]{1,0:T(8,128)(2,1)S(1)}, u32[]{:S(2)}, u32[]{:S(2)}) %collective-permute-start.11) | collective-permute-done | bytes 51232 | tf_op jit(solution)/shard_map/ppermute | solution.py:49
  45.0 0.1 collective-permute-start.12
  45.0 2.0 %collective-permute-done.4 = bf16[1,128,128]{2,1,0:T(8,128)(2,1)S(1)} collective-permute-done((bf16[1,128,128]{2,1,0:T(8,128)(2,1)S(1)}, bf16[1,128,128]{2,1,0:T(8,128)(2,1)S(1)}, u32[]{:S(2)}, u32[]{:S(2)}) %collective-permute-start.4) | collective-permute-done | bytes 32800 | tf_op jit(solution)/shard_map/ppermute | solution.py:49
  47.0 0.6 %fusion = bf16[1,128,128]{2,1,0:T(8,128)(2,1)} fusion(f32[2,128,128]{2,1,0:T(8,128)S(1)} %slice_add_fusion, bf16[1,128,128]{2,1,0:T(8,128)(2,1)S(1)} %collective-permute-done.4), kind=kLoop, calls=%fused_computation.8 | loop fusion | flops 49152 | bytes 131072 | tf_op jit(solution)/shard_map/convert_element_type | solution.py:430
  47.6 0.0 collective-permute-done.12.refs_1_
  47.6 0.9 %finish.1 = (f32[128,128]{1,0:T(8,128)}, f32[256,128]{1,0:T(8,128)}, f32[1,128]{1,0:T(1,128)}, f32[128,128]{1,0:T(8,128)}) custom-call(f32[200,128]{1,0:T(8,128)S(1)} %convert_add_fusion.1.refs_0_, f32[200,128]{1,0:T(8,128)S(1)} %collective-permute-done.12.refs_1_, bf16[128,128]{1,0:T(8,128)(2,1)S(1)} %copy-done.4, bf16[256,128]{1,0:T(8,128)(2,1)S(1)} %copy-done.2), custom_call_target="tpu_custom_call" | custom-call | tf_op jit(solution)/shard_map/finish/pallas_call | solution.py:443
  (35 shorter events, 0.2 us)
Async XLA Ops:
  0.6 9.0 %slice-start = ((s8[8388608]{0:T(1024)(128)(4,1)}), s8[4194304]{0:T(1024)(128)(4,1)S(1)}, s32[]{:S(2)}) async-start(s8[8388608]{0:T(1024)(128)(4,1)} %bitcast.11), calls=%async_computation | async-start | bytes 8388608
  0.6 9.0 %slice-start.1 = ((s8[8388608]{0:T(1024)(128)(4,1)}), s8[4194304]{0:T(1024)(128)(4,1)S(1)}, s32[]{:S(2)}) async-start(s8[8388608]{0:T(1024)(128)(4,1)} %bitcast.11), calls=%async_computation.1 | async-start | bytes 8388608
  0.7 9.0 %copy-start = (bf16[1,8192,128]{2,1,0:T(8,128)(2,1)S(1)}, bf16[1,8192,128]{2,1,0:T(8,128)(2,1)}, u32[]{:S(2)}) copy-start(bf16[1,8192,128]{2,1,0:T(8,128)(2,1)} %param.10) | copy-start | bytes 6291460
  0.7 9.0 %copy-start.1 = (bf16[1,64,128,128]{3,2,1,0:T(8,128)(2,1)S(1)}, bf16[1,64,128,128]{3,2,1,0:T(8,128)(2,1)}, u32[]{:S(2)}) copy-start(bf16[1,64,128,128]{3,2,1,0:T(8,128)(2,1)} %param.14) | copy-start | bytes 6291460
  0.7 8.9 %copy-start.2 = (bf16[256,128]{1,0:T(8,128)(2,1)S(1)}, bf16[256,128]{1,0:T(8,128)(2,1)}, u32[]{:S(2)}) copy-start(bf16[256,128]{1,0:T(8,128)(2,1)} %refs_3_.1) | copy-start | bytes 196612
  0.7 8.9 %copy-start.4 = (bf16[128,128]{1,0:T(8,128)(2,1)S(1)}, bf16[128,128]{1,0:T(8,128)(2,1)}, u32[]{:S(2)}) copy-start(bf16[128,128]{1,0:T(8,128)(2,1)} %refs_2_.1) | copy-start | bytes 98308
  0.7 8.9 %copy-start.5 = (s32[1,64,4]{1,2,0:T(4,128)S(1)}, s32[1,64,4]{1,2,0:T(4,128)}, u32[]{:S(2)}) copy-start(s32[1,64,4]{1,2,0:T(4,128)} %param.12) | copy-start | bytes 3076
  0.7 8.9 %copy-start.6 = (s32[1,64,1]{1,2,0:T(1,128)S(1)}, s32[1,64,1]{1,2,0:T(1,128)}, u32[]{:S(2)}) copy-start(s32[1,64,1]{1,2,0:T(1,128)} %param.13) | copy-start | bytes 772
  0.7 8.9 %copy-start.7 = (f32[128]{0:T(128)S(1)}, f32[128]{0:T(128)}, u32[]{:S(2)}) copy-start(f32[128]{0:T(128)} %param.18) | copy-start | bytes 1540
  1.8 5.9 %collective-permute-start = (bf16[384,128]{1,0:T(8,128)(2,1)S(1)}, bf16[384,128]{1,0:T(8,128)(2,1)S(1)}, u32[]{:S(2)}, u32[]{:S(2)}) collective-permute-start(bf16[384,128]{1,0:T(8,128)(2,1)S(1)} %get-tuple-element.29), channel_id=1, source_target_pairs={{0,1},{1,0},{2,3},{3,2},{4,5},{5,4},{6,7},{7,6},{8,9},{9,8},{10,11... | collective-permute-start | bytes 294920 | tf_op jit(solution)/shard_map/ppermute | solution.py:49
  4.9 12.4 %collective-permute-start.1 = (bf16[256,128]{1,0:T(8,128)(2,1)S(1)}, bf16[256,128]{1,0:T(8,128)(2,1)S(1)}, u32[]{:S(2)}, u32[]{:S(2)}) collective-permute-start(bf16[256,128]{1,0:T(8,128)(2,1)S(1)} %get-tuple-element.30), channel_id=1, source_target_pairs={{1,2},{3,4},{5,6},{2,1},{4,3},{6,5},{9,10},{11,12},{13,14},{10,9},... | collective-permute-start | bytes 196616 | tf_op jit(solution)/shard_map/ppermute | solution.py:337
  7.7 4.4 %collective-permute-start.5 = (bf16[256,128]{1,0:T(8,128)(2,1)S(1)}, bf16[256,128]{1,0:T(8,128)(2,1)S(1)}, u32[]{:S(2)}, u32[]{:S(2)}) collective-permute-start(bf16[256,128]{1,0:T(8,128)(2,1)S(1)} %pad_maximum_fusion.1), channel_id=1, source_target_pairs={{0,2},{1,3},{2,0},{3,1},{4,6},{5,7},{6,4},{7,5},{8,10},{9,11},{10,... | collective-permute-start | bytes 196616 | tf_op jit(solution)/shard_map/ppermute | solution.py:49
  12.1 9.2 %collective-permute-start.6 = (bf16[512,128]{1,0:T(8,128)(2,1)S(1)}, bf16[512,128]{1,0:T(8,128)(2,1)S(1)}, u32[]{:S(2)}, u32[]{:S(2)}) collective-permute-start(bf16[512,128]{1,0:T(8,128)(2,1)S(1)} %pad_maximum_fusion), channel_id=1, source_target_pairs={{0,4},{1,5},{2,6},{3,7},{4,0},{5,1},{6,2},{7,3},{8,12},{9,13},{10,... | collective-permute-start | bytes 393224 | tf_op jit(solution)/shard_map/ppermute | solution.py:49
  15.0 2.3 %copy-start.3 = (bf16[128,128]{1,0:T(8,128)(2,1)S(1)}, bf16[128,128]{1,0:T(8,128)(2,1)}, u32[]{:S(2)}) copy-start(bf16[128,128]{1,0:T(8,128)(2,1)} %refs_10_.1) | copy-start | bytes 98308
  23.8 1.4 %collective-permute-start.7 = (f32[200,128]{1,0:T(8,128)S(1)}, f32[200,128]{1,0:T(8,128)S(1)}, u32[]{:S(2)}, u32[]{:S(2)}) collective-permute-start(f32[200,128]{1,0:T(8,128)S(1)} %get-tuple-element.47), channel_id=1, source_target_pairs={{0,8},{8,0},{16,24},{24,16},{1,9},{9,1},{17,25},{25,17},{2,10},{10... | collective-permute-start | bytes 307208 | tf_op jit(solution)/shard_map/ppermute | solution.py:49
  25.2 5.0 %collective-permute-start.8 = (f32[200,128]{1,0:T(8,128)S(1)}, f32[200,128]{1,0:T(8,128)S(1)}, u32[]{:S(2)}, u32[]{:S(2)}) collective-permute-start(f32[200,128]{1,0:T(8,128)S(1)} %add.27), channel_id=1, source_target_pairs={{0,16},{8,24},{16,0},{24,8},{1,17},{9,25},{17,1},{25,9},{2,18},{10... | collective-permute-start | bytes 307208 | tf_op jit(solution)/shard_map/ppermute | solution.py:49
  26.8 9.9 %collective-permute-start.2 = (bf16[4,128,128]{2,1,0:T(8,128)(2,1)S(1)}, bf16[4,128,128]{2,1,0:T(8,128)(2,1)S(1)}, u32[]{:S(2)}, u32[]{:S(2)}) collective-permute-start(bf16[4,128,128]{2,1,0:T(8,128)(2,1)S(1)} %get-tuple-element.42), channel_id=1, source_target_pairs={{0,1},{1,0},{2,3},{3,2},{4,5},{5,4},{6,7},{7,6},{8,9},{9,8},{10,11... | collective-permute-start | bytes 393224 | tf_op jit(solution)/shard_map/ppermute | solution.py:49
  30.3 4.8 %collective-permute-start.9 = (f32[200,128]{1,0:T(8,128)S(1)}, f32[200,128]{1,0:T(8,128)S(1)}, u32[]{:S(2)}, u32[]{:S(2)}) collective-permute-start(f32[200,128]{1,0:T(8,128)S(1)} %add.28), channel_id=1, source_target_pairs={{0,1},{1,0},{2,3},{3,2},{4,5},{5,4},{6,7},{7,6},{8,9},{9,8},{10,11... | collective-permute-start | bytes 307208 | tf_op jit(solution)/shard_map/ppermute | solution.py:49
  35.1 4.7 %collective-permute-start.10 = (f32[200,128]{1,0:T(8,128)S(1)}, f32[200,128]{1,0:T(8,128)S(1)}, u32[]{:S(2)}, u32[]{:S(2)}) collective-permute-start(f32[200,128]{1,0:T(8,128)S(1)} %add.29), channel_id=1, source_target_pairs={{0,2},{1,3},{2,0},{3,1},{4,6},{5,7},{6,4},{7,5},{8,10},{9,11},{10,... | collective-permute-start | bytes 307208 | tf_op jit(solution)/shard_map/ppermute | solution.py:49
  36.7 4.9 %collective-permute-start.3 = (bf16[2,128,128]{2,1,0:T(8,128)(2,1)S(1)}, bf16[2,128,128]{2,1,0:T(8,128)(2,1)S(1)}, u32[]{:S(2)}, u32[]{:S(2)}) collective-permute-start(bf16[2,128,128]{2,1,0:T(8,128)(2,1)S(1)} %slice.37), channel_id=1, source_target_pairs={{0,2},{1,3},{2,0},{3,1},{4,6},{5,7},{6,4},{7,5},{8,10},{9,11},{10,... | collective-permute-start | bytes 196616 | tf_op jit(solution)/shard_map/ppermute | solution.py:49
  39.9 5.1 %collective-permute-start.11 = (bf16[200,128]{1,0:T(8,128)(2,1)S(1)}, bf16[200,128]{1,0:T(8,128)(2,1)S(1)}, u32[]{:S(2)}, u32[]{:S(2)}) collective-permute-start(bf16[200,128]{1,0:T(8,128)(2,1)S(1)} %add_convert_fusion), channel_id=1, source_target_pairs={{0,4},{1,5},{2,6},{3,7},{4,0},{5,1},{6,2},{7,3},{8,12},{9,13},{10,... | collective-permute-start | bytes 153608 | tf_op jit(solution)/shard_map/ppermute | solution.py:49
  41.6 5.4 %collective-permute-start.4 = (bf16[1,128,128]{2,1,0:T(8,128)(2,1)S(1)}, bf16[1,128,128]{2,1,0:T(8,128)(2,1)S(1)}, u32[]{:S(2)}, u32[]{:S(2)}) collective-permute-start(bf16[1,128,128]{2,1,0:T(8,128)(2,1)S(1)} %slice.38), channel_id=1, source_target_pairs={{0,4},{1,5},{2,6},{3,7},{4,0},{5,1},{6,2},{7,3},{8,12},{9,13},{10,... | collective-permute-start | bytes 98312 | tf_op jit(solution)/shard_map/ppermute | solution.py:49
  45.0 2.7 %collective-permute-start.12 = (f32[200,128]{1,0:T(8,128)S(1)}, f32[200,128]{1,0:T(8,128)S(1)}, u32[]{:S(2)}, u32[]{:S(2)}) collective-permute-start(f32[200,128]{1,0:T(8,128)S(1)} %convert_add_fusion.1.refs_0_), channel_id=1, source_target_pairs={{0,8},{8,0},{16,24},{24,16},{1,9},{9,1},{17,25},{25,17},{2,10},{10... | collective-permute-start | bytes 307208 | tf_op jit(solution)/shard_map/ppermute | solution.py:49

commit v4 on v3

--- a/solution.py
+++ b/solution.py
@@ -40,13 +40,32 @@
     return jnp.concatenate([a, b], axis=1)
 
 
-def bit_order(count):
-    bits = count.bit_length() - 1
-    return [sum(((q >> b) & 1) << (bits - 1 - b) for b in range(bits)) for q in range(count)]
+def halving_order(masks):
+    order = [0]
+    for mask in reversed(masks):
+        order = order + [r + mask for r in order]
+    return order
 
 
 def exchange(x, axis, mask):
     return lax.ppermute(x, axis, [(i, i ^ mask) for i in range(lax.axis_size(axis))])
+
+
+def narrow(x, fine):
+    high = lax.reduce_precision(x, exponent_bits=8, mantissa_bits=7)
+    parts = [high.astype(BF16)]
+    if fine:
+        parts.append((x - high)[2 * HALF :].astype(BF16))
+    return jnp.concatenate(parts, axis=0)
+
+
+def widen(low):
+    rows = PACK + 8
+    x = low[:rows].astype(F32)
+    if low.shape[0] > rows:
+        rest = jnp.zeros((2 * HALF, H), F32)
+        x = x + jnp.concatenate([rest, low[rows:].astype(F32)], axis=0)
+    return x
 
 
 def rows_at(tile, count=1):
@@ -55,16 +74,14 @@
     return pl.ds(pl.multiple_of(tile * TILE, TILE), count * TILE)
 
 
-def pack_kernel(nodes, cot, near, far, sem):
+def pack_kernel(nodes, cot, own, near, far, sem):
     odd = lax.axis_index("graph") & 1
     gap = nodes.shape[0] - MARGIN
     near_at = pl.multiple_of((1 - odd) * gap, TILE)
     far_at = pl.multiple_of(odd * gap, TILE)
     copies = [
-        pltpu.make_async_copy(cot, near.at[pl.ds(0, TILE)], sem.at[0]),
-        pltpu.make_async_copy(
-            nodes.at[pl.ds(near_at, MARGIN)], near.at[pl.ds(TILE, MARGIN)], sem.at[1]
-        ),
+        pltpu.make_async_copy(cot, own, sem.at[0]),
+        pltpu.make_async_copy(nodes.at[pl.ds(near_at, MARGIN)], near, sem.at[1]),
         pltpu.make_async_copy(nodes.at[pl.ds(far_at, MARGIN)], far, sem.at[2]),
     ]
     for copy in copies:
@@ -158,10 +175,9 @@
 
 
 def last_kernel(
-    quads, order, src, dst, near, far, nodes, adj, pw, wcat, bias, w_out,
+    quads, src, dst, near, far, nodes, adj, pw, wcat, bias,
     a_in, act_in, slope_in, acc_in,
-    a_out, act_out, slope_out, p_out, fine, send, keep,
-    acc, pooled, edges, wdiag, out_v, sem,
+    a_out, act_out, slope_out, p_out, acc, edges,
 ):
     me = lax.axis_index("graph")
     odd = me & 1
@@ -169,11 +185,12 @@
     span = size // 2 - MARGIN
     edges[MARGIN : MARGIN + span] = nodes[:span]
     edges[size - MARGIN - span : size - MARGIN] = nodes[nodes.shape[0] - span :]
-    edges[pl.ds(pl.multiple_of((1 - odd) * (size - MARGIN), TILE), MARGIN), :] = near[TILE:]
-    edges[pl.ds(pl.multiple_of(odd * (size - MARGIN), TILE), MARGIN), :] = far[...]
-    wdiag[...] = diagonal(w_out[...], w_out[...])
+    edges[pl.ds(pl.multiple_of((1 - odd) * (size - MARGIN), TILE), MARGIN), :] = near[...]
+    at_end = (me == 0) | (me == lax.axis_size("graph") - 1)
+    edges[pl.ds(pl.multiple_of(odd * (size - MARGIN), TILE), MARGIN), :] = jnp.where(
+        at_end, jnp.zeros_like(far), far[...]
+    )
     acc[...] = acc_in[...]
-    pooled[...] = jnp.zeros_like(pooled)
     outs = (a_out, act_out, slope_out)
     forward_quads(quads, src, dst, nodes, adj, pw, wcat, bias, outs, acc, edges)
     for r in range(acc.shape[0]):
@@ -181,12 +198,19 @@
         p_out[r * TILE : (r + 1) * TILE, :H] = hi
         p_out[r * TILE : (r + 1) * TILE, H:] = lo
 
+
+def tail_kernel(
+    order, dst, nodes, act_in, pw, w_out, fine, send, keep, pooled, wdiag, out_v, sem
+):
+    me = lax.axis_index("graph")
+    wdiag[...] = diagonal(w_out[...], w_out[...])
+    pooled[...] = jnp.zeros_like(pooled)
     half = QUAD * TILE // 2
     count = nodes.shape[0] // (QUAD * TILE)
     copies = []
 
     def project(i, _):
-        act = act_out[rows_at(i * QUAD, QUAD), :]
+        act = act_in[rows_at(i * QUAD, QUAD), :]
         return dot(beside(act[:half], act[half:]), wdiag[...])
 
     def update(i, delta):
@@ -213,17 +237,16 @@
         copy.wait()
 
 
-def backward_kernel(pieces, dst, *refs):
+def backward_kernel(places, dst, *refs):
+    pieces = len(places)
     cots = refs[:pieces]
     (nodes, a_in, slope_in, pw, p_in, w_out) = refs[pieces : pieces + 6]
     keep, send, cot_all, cot_w, total, bias, mats = refs[pieces + 6 :]
     me = lax.axis_index("graph")
     core = lax.axis_index("design") & 1
-    at = 0
-    for cot in cots:
-        size = cot.shape[0]
-        cot_all[at : at + size] = cot[...]
-        at += size
+    for cot, spots in zip(cots, places):
+        for n, r in enumerate(spots):
+            cot_all[r * TILE : (r + 1) * TILE] = cot[n * TILE : (n + 1) * TILE]
     for r in range(cot_w.shape[0]):
         tile = cot_all[r * TILE : (r + 1) * TILE]
         cot_w[r] = (0.5 * dot(w_out[...], tile, 1, 1)).astype(BF16)
@@ -322,19 +345,42 @@
             transcendentals=trans,
         )
 
-    near_send, far_send = pl.pallas_call(
+    bits = slabs.bit_length() - 1
+    masks = [1 << b for b in range(2, bits)] + [1 << b for b in range(min(bits, 2))]
+    pieces, places = [cot], [[0]]
+
+    def gather(mask):
+        sent = pieces[0] if len(pieces) == 1 else jnp.concatenate(pieces, axis=0)
+        got = exchange(sent, "graph", mask)
+        known = [r ^ mask for spots in places for r in spots]
+        pieces.append(got)
+        places.append(known)
+
+    gather(masks[0])
+    own_cot, near_send, far_send = pl.pallas_call(
         pack_kernel,
         in_specs=[hbm, hbm],
-        out_specs=[vmem, vmem],
-        out_shape=[shape(TILE + MARGIN, H, dtype=BF16), shape(MARGIN, H, dtype=BF16)],
+        out_specs=[vmem] * 3,
+        out_shape=[shape(TILE, H, dtype=BF16)] + [shape(MARGIN, H, dtype=BF16)] * 2,
         scratch_shapes=[pltpu.SemaphoreType.DMA((3,))],
         compiler_params=params(1),
         cost_estimate=cost(40, 40),
         name="pack",
     )(stay(feats), stay(cot))
+    pieces[0] = own_cot
+    cross = {}
+    for d in range(designs):
+        for g in range(slabs):
+            beyond = g + 1 if g % 2 else g - 1
+            inside = 0 <= beyond < slabs
+            cross[d * slabs + g] = d * slabs + beyond if inside else (d ^ 1) * slabs + g
+    far = lax.ppermute(far_send, ("design", "graph"), list(cross.items()))
     near = exchange(near_send, "graph", 1)
-    across = [(i, i + 1) for i in range(1, slabs - 1, 2)]
-    far = lax.ppermute(far_send, "graph", across + [(b, a) for a, b in across])
+    for mask in masks[1:]:
+        if mask > 2:
+            gather(mask)
+    if masks[0] > 1:
+        gather(1)
 
     row_shape = shape(rows, H, dtype=BF16)
     slope_shape = shape(count, H, TILE)
@@ -352,8 +398,8 @@
         name="start",
     )(src, dst, feats, adj, pw, w_msg, w_in, bias)
 
-    cots = [near_send[:TILE], near[:TILE]]
-    pair = exchange(jnp.concatenate(cots, axis=0), "graph", 2) if slabs > 2 else None
+    if slabs > 2:
+        gather(2)
 
     held = pl.pallas_call(
         lambda *refs: middle_kernel(two, *refs),
@@ -366,44 +412,25 @@
         name="middle",
     )(src, dst, feats, adj, pw, wcat, bias, *held)
 
-    if slabs > 2:
-        cots.append(pair)
-    for b in range(2, slabs.bit_length() - 1):
-        cots.append(exchange(jnp.concatenate(cots, axis=0), "graph", 1 << b))
-
-    order = bit_order(slabs)
-    a_all, _, slope_all, p_all, fine, c_send, c_keep = pl.pallas_call(
-        lambda *refs: last_kernel(three, order, *refs),
-        in_specs=[smem, smem, vmem, vmem, vmem, vmem, vmem, vmem, vmem, vmem]
-        + [vmem] * 4,
-        out_specs=[vmem] * 4 + [hbm] + [vmem] * 2,
-        out_shape=[
-            *state,
-            shape(slabs * TILE, 2 * H, dtype=BF16),
-            row_shape,
-            shape(slabs // 2, TILE, H, dtype=BF16),
-            shape(slabs // 2, TILE, H),
-        ],
+    a_all, act_all, slope_all, p_all = pl.pallas_call(
+        lambda *refs: last_kernel(three, *refs),
+        in_specs=[smem, smem] + [vmem] * 11,
+        out_specs=[vmem] * 4,
+        out_shape=[*state, shape(slabs * TILE, 2 * H, dtype=BF16)],
         scratch_shapes=[
             pltpu.VMEM((slabs, TILE, H), F32),
-            pltpu.VMEM((slabs, TILE, H), F32),
             pltpu.VMEM((2 * (QUAD + 2 * HT) * TILE, H), BF16),
-            pltpu.VMEM((2 * H, 2 * H), BF16),
-            pltpu.VMEM((rows, H), BF16),
-            pltpu.SemaphoreType.DMA((count // QUAD,)),
         ],
-        input_output_aliases={10: 0, 11: 1, 12: 2},
-        compiler_params=params(16),
-        cost_estimate=cost(4, 8, rows * H // 4),
+        input_output_aliases={9: 0, 10: 1, 11: 2},
+        compiler_params=params(8),
+        cost_estimate=cost(2, 4, rows * H // 4),
         name="last",
-    )(src, dst, near, far, feats, adj, pw, wcat, bias, w_out, *held)
-    c_got = exchange(c_send, "graph", 1)
-
-    every = cots
+    )(src, dst, near, far, feats, adj, pw, wcat, bias, *held)
+
     keep, send = pl.pallas_call(
-        lambda *refs: backward_kernel(len(every), *refs),
+        lambda *refs: backward_kernel(places, *refs),
         in_specs=[smem]
-        + [vmem] * len(every)
+        + [vmem] * len(pieces)
         + [vmem] * 5
         + [vmem],
         out_specs=[vmem, vmem],
@@ -418,26 +445,41 @@
         compiler_params=params(16),
         cost_estimate=cost(3, 4),
         name="backward",
-    )(dst, *every, feats, a_all, slope_all, pw, p_all, w_out)
-
-    held = c_keep + c_got.astype(F32)
-    mask = 2
-    while mask < slabs:
+    )(dst, *pieces, feats, a_all, slope_all, pw, p_all, w_out)
+
+    halving = [2, 1] + masks[:-2] if slabs > 2 else masks
+    order = halving_order(halving)
+    fine, c_send, held = pl.pallas_call(
+        lambda *refs: tail_kernel(order, *refs),
+        in_specs=[smem] + [vmem] * 4,
+        out_specs=[hbm, vmem, vmem],
+        out_shape=[
+            row_shape,
+            shape(slabs // 2, TILE, H, dtype=BF16),
+            shape(slabs // 2, TILE, H),
+        ],
+        scratch_shapes=[
+            pltpu.VMEM((slabs, TILE, H), F32),
+            pltpu.VMEM((2 * H, 2 * H), BF16),
+            pltpu.VMEM((rows, H), BF16),
+            pltpu.SemaphoreType.DMA((count // QUAD,)),
+        ],
+        compiler_params=params(12),
+        cost_estimate=cost(2, 4),
+        name="tail",
+    )(dst, feats, act_all, pw, w_out)
+    for mask in halving:
+        held = held + exchange(c_send, "graph", mask).astype(F32)
         size = held.shape[0] // 2
-        got = exchange(held[size:].astype(BF16), "graph", mask)
-        held = held[:size] + got.astype(F32)
-        mask *= 2
+        held, c_send = held[:size] if size else held, held[size:].astype(BF16)
     coarse = held[0].astype(BF16)
 
     rounds = [("design", 1 << b) for b in range(1, designs.bit_length() - 1)]
     rounds += [("graph", 1 << b) for b in range(slabs.bit_length() - 1)]
     mine = keep + exchange(send, "design", 1)
     for n, (axis, mask) in enumerate(rounds):
-        if n < len(rounds) - LOW_ROUNDS:
-            mine = mine + exchange(mine, axis, mask)
-        else:
-            low = mine.astype(BF16)
-            mine = low.astype(F32) + exchange(low, axis, mask).astype(F32)
+        low = narrow(mine, n < len(rounds) - LOW_ROUNDS)
+        mine = widen(low) + widen(exchange(low, axis, mask))
     other = exchange(mine, "design", 1)
     scale = 1.0 / math.sqrt(designs * rows * slabs)
     g_msg, g_in, g_bias, g_out = pl.pallas_call(

time: 48.7 us -> 49.8 us (1.023)
  starting transfers between devices: 18.4 us -> 19.4 us
  Pallas kernels: 13.2 us -> 14 us
  waiting for transfers between devices: 15.2 us -> 14.4 us
    ppermute x12 -> x13, starting transfers between devices: 17.8 us -> 19.4 us  [exchange(): lax.ppermute(x, axis, [(i, i ^ mask) for i in range(lax.axis_size(axis))])]
    ppermute x12 -> x13, waiting for transfers between devices: 15.2 us -> 14.3 us  [exchange(): lax.ppermute(x, axis, [(i, i ^ mask) for i in range(lax.axis_size(axis))])]
    pallas_call x3 -> x4, Pallas kernels: 7.57 us -> 8.3 us  [the longest x1 2.76 us: layer(): pl.pallas_call(lambda *refs: tail_kernel(order, *refs), in_specs=[smem] +...]
    ppermute x1, starting transfers between devices: 0.65 us -> 0.01 us  [layer(): far = lax.ppermute(far_send, ('design', 'graph'), list(cross.items()))]
  transfers between devices with their start and end apart: 13 -> 14, of which waited for: 8 -> 8; matrix products, arithmetic and copies ran while one was open for 2% -> 2% of each run, Pallas kernels for 18% -> 21%
where the time goes in v4:
time: 49.8 us; the launch traced here: 49.6 us
  starting transfers between devices  19.4 us (39%)
  waiting for transfers between devices  14.4 us (29%)
  Pallas kernels  14 us (28%)
  between operations  0.95 us (2%)
  other arithmetic  0.87 us (2%)
    ppermute x13, starting transfers between devices, exchange(): lax.ppermute(x, axis, [(i, i ^ mask) for i in range(lax.axis_size(axis))])  19.4 us
    ppermute x13, waiting for transfers between devices, exchange(): lax.ppermute(x, axis, [(i, i ^ mask) for i in range(lax.axis_size(axis))])  14.3 us
    pallas_call x1, Pallas kernels, layer(): pl.pallas_call(lambda *refs: tail_kernel(order, *refs), in_specs=[smem] +...  2.76 us
    pallas_call x1, Pallas kernels, layer(): pl.pallas_call(lambda *refs: backward_kernel(places, *refs), in_specs=[sm...  2.47 us
    pallas_call x1, Pallas kernels, layer(): pl.pallas_call(lambda *refs: start_kernel(one, *refs), in_specs=[smem, sm...  2.42 us
    pallas_call x1, Pallas kernels, layer(): pl.pallas_call(lambda *refs: middle_kernel(two, *refs), in_specs=[smem, s...  2.34 us
    pallas_call x1, Pallas kernels, layer(): pl.pallas_call(lambda *refs: last_kernel(three, *refs), in_specs=[smem, s...  2.01 us
    pallas_call x1, Pallas kernels, layer(): pl.pallas_call(pack_kernel, in_specs=[hbm, hbm], out_specs=[vmem] * 3, ou...  1.06 us
  transfers between devices with their start and end apart: 14, of which 8 were waited for; matrix products, arithmetic and copies ran while one was open for 2% of the time, Pallas kernels for 21%

profile of v4, /device:TPU:0, one launch (start us, length us, event | category | flops | bytes accessed | tf_op | source)
XLA Modules:
  0.0 49.6 jit_solution(14121200185592068928)
XLA Ops:
  0.6 4.1 %collective-permute-start.5 = (bf16[128,128]{1,0:T(8,128)(2,1)}, bf16[128,128]{1,0:T(8,128)(2,1)S(1)}, u32[]{:S(2)}, u32[]{:S(2)}) collective-permute-start(bf16[128,128]{1,0:T(8,128)(2,1)} %bitcast.39), channel_id=1, source_target_pairs={{0,4},{1,5},{2,6},{3,7},{4,0},{5,1},{6,2},{7,3},{8,12},{9,13},{10,... | collective-permute-start | bytes 98312 | tf_op jit(solution)/shard_map/ppermute | solution.py:51
  4.8 1.1 %pack.1 = (bf16[128,128]{1,0:T(8,128)(2,1)S(1)}, bf16[256,128]{1,0:T(8,128)(2,1)S(1)}, bf16[256,128]{1,0:T(8,128)(2,1)S(1)}) custom-call(bf16[8192,128]{1,0:T(8,128)(2,1)} %bitcast.16, bf16[128,128]{1,0:T(8,128)(2,1)} %bitcast.40), custom_call_target="tpu_custom_call" | custom-call | flops 10737418240 | bytes 41943040 | tf_op jit(solution)/shard_map/pack/pallas_call | solution.py:360
  5.9 1.3 %collective-permute-done.5.refs_2_ = bf16[128,128]{1,0:T(8,128)(2,1)S(1)} collective-permute-done((bf16[128,128]{1,0:T(8,128)(2,1)}, bf16[128,128]{1,0:T(8,128)(2,1)S(1)}, u32[]{:S(2)}, u32[]{:S(2)}) %collective-permute-start.5) | collective-permute-done | bytes 32800 | tf_op jit(solution)/shard_map/ppermute | solution.py:51
  7.2 1.7 %collective-permute-start.6 = (bf16[256,128]{1,0:T(8,128)(2,1)S(1)}, bf16[256,128]{1,0:T(8,128)(2,1)S(1)}, u32[]{:S(2)}, u32[]{:S(2)}) collective-permute-start(bf16[256,128]{1,0:T(8,128)(2,1)S(1)} %pad_maximum_fusion.4), channel_id=1, source_target_pairs={{0,1},{1,0},{2,3},{3,2},{4,5},{5,4},{6,7},{7,6},{8,9},{9,8},{10,11... | collective-permute-start | bytes 196616 | tf_op jit(solution)/shard_map/ppermute | solution.py:51
  9.0 0.3 collective-permute-start
  9.3 0.0 collective-permute-start.1
  9.3 2.2 %collective-permute-done.6.refs_3_ = bf16[256,128]{1,0:T(8,128)(2,1)S(1)} collective-permute-done((bf16[256,128]{1,0:T(8,128)(2,1)S(1)}, bf16[256,128]{1,0:T(8,128)(2,1)S(1)}, u32[]{:S(2)}, u32[]{:S(2)}) %collective-permute-start.6) | collective-permute-done | bytes 65568 | tf_op jit(solution)/shard_map/ppermute | solution.py:51
  11.5 2.3 %collective-permute-start.7 = (bf16[512,128]{1,0:T(8,128)(2,1)S(1)}, bf16[512,128]{1,0:T(8,128)(2,1)S(1)}, u32[]{:S(2)}, u32[]{:S(2)}) collective-permute-start(bf16[512,128]{1,0:T(8,128)(2,1)S(1)} %pad_maximum_fusion), channel_id=1, source_target_pairs={{0,2},{1,3},{2,0},{3,1},{4,6},{5,7},{6,4},{7,5},{8,10},{9,11},{10,... | collective-permute-start | bytes 393224 | tf_op jit(solution)/shard_map/ppermute | solution.py:51
  13.9 2.4 %start.1 = (bf16[8192,128]{1,0:T(8,128)(2,1)S(1)}, bf16[8192,128]{1,0:T(8,128)(2,1)S(1)}, f32[64,128,128]{2,1,0:T(8,128)S(1)}, f32[8,128,128]{2,1,0:T(8,128)S(1)}, bf16[256,128]{1,0:T(8,128)(2,1)S(1)}) custom-call(s32[4,64]{1,0:T(4,128)S(1)} %bitcast.27, s32[1,64]{1,0:T(1,128)S(1)} %bitcast.30, bf16[8192,128]{1,0:T(8,128)(2,1)S(1)} %bitcast.17, ...), custom_call_target="tpu_custom_call" | custom-call | flops 805306368 | bytes 8388608 | tf_op jit(solution)/shard_map/start/pallas_call | solution.py:391
  16.3 2.3 %middle.1 = (bf16[8192,128]{1,0:T(8,128)(2,1)S(1)}, bf16[8192,128]{1,0:T(8,128)(2,1)S(1)}, f32[64,128,128]{2,1,0:T(8,128)S(1)}, f32[8,128,128]{2,1,0:T(8,128)S(1)}) custom-call(s32[4,64]{1,0:T(4,128)S(1)} %bitcast.28, s32[1,64]{1,0:T(1,128)S(1)} %bitcast.31, ...), custom_call_target="tpu_custom_call", output_to_operand_aliasing={{0}: (7, {}), {1}: (8, {}), {2}: (9, {}), {3}: (10, {})} | custom-call | flops 805306368 | bytes 8388608 | tf_op jit(solution)/shard_map/middle/pallas_call | solution.py:404
  18.7 0.0 copy-start.3
  18.7 2.0 %last.1 = (bf16[8192,128]{1,0:T(8,128)(2,1)S(1)}, bf16[8192,128]{1,0:T(8,128)(2,1)S(1)}, f32[64,128,128]{2,1,0:T(8,128)S(1)}, bf16[1024,256]{1,0:T(8,128)(2,1)S(1)}) custom-call(s32[4,64]{1,0:T(4,128)S(1)} %bitcast.29, s32[1,64]{1,0:T(1,128)S(1)} %bitcast.32, ...), custom_call_target="tpu_custom_call", output_to_operand_aliasing={{0}: (9, {}), {1}: (10, {}), {2}: (11, {})} | custom-call | flops 536870912 | bytes 4194304 | tf_op jit(solution)/shard_map/last/pallas_call | solution.py:415
  20.7 0.0 collective-permute-done.7.refs_4_
  20.7 2.5 %backward.1 = (f32[200,128]{1,0:T(8,128)S(1)}, f32[200,128]{1,0:T(8,128)S(1)}) custom-call(s32[1,64]{1,0:T(1,128)S(1)} %bitcast.33, bf16[128,128]{1,0:T(8,128)(2,1)S(1)} %get-tuple-element.46.refs_1_, bf16[128,128]{1,0:T(8,128)(2,1)S(1)} %collective-permute-done.5.refs_2_, bf16[256,128]{1,0:T(8,128)(2,1)S(1)} %collective-permute-done.6.refs_3_, ...), custom_call_target="tpu_custom_call" | custom-call | flops 805306368 | bytes 4194304 | tf_op jit(solution)/shard_map/backward/pallas_call | solution.py:430
  23.2 0.1 collective-permute-start.8
  23.3 1.3 %collective-permute-done.8 = f32[200,128]{1,0:T(8,128)S(1)} collective-permute-done((f32[200,128]{1,0:T(8,128)S(1)}, f32[200,128]{1,0:T(8,128)S(1)}, u32[]{:S(2)}, u32[]{:S(2)}) %collective-permute-start.8) | collective-permute-done | bytes 102432 | tf_op jit(solution)/shard_map/ppermute | solution.py:51
  24.7 1.6 %collective-permute-start.9 = (bf16[272,128]{1,0:T(8,128)(2,1)S(1)}, bf16[272,128]{1,0:T(8,128)(2,1)S(1)}, u32[]{:S(2)}, u32[]{:S(2)}) collective-permute-start(bf16[272,128]{1,0:T(8,128)(2,1)S(1)} %pad_maximum_fusion.1), channel_id=1, source_target_pairs={{0,16},{8,24},{16,0},{24,8},{1,17},{9,25},{17,1},{25,9},{2,18},{10... | collective-permute-start | bytes 208904 | tf_op jit(solution)/shard_map/ppermute | solution.py:51
  26.2 2.8 %collective-permute-done.9 = bf16[272,128]{1,0:T(8,128)(2,1)S(1)} collective-permute-done((bf16[272,128]{1,0:T(8,128)(2,1)S(1)}, bf16[272,128]{1,0:T(8,128)(2,1)S(1)}, u32[]{:S(2)}, u32[]{:S(2)}) %collective-permute-start.9) | collective-permute-done | bytes 69664 | tf_op jit(solution)/shard_map/ppermute | solution.py:51
  29.1 1.6 %collective-permute-start.10 = (bf16[272,128]{1,0:T(8,128)(2,1)S(1)}, bf16[272,128]{1,0:T(8,128)(2,1)S(1)}, u32[]{:S(2)}, u32[]{:S(2)}) collective-permute-start(bf16[272,128]{1,0:T(8,128)(2,1)S(1)} %pad_maximum_fusion.2), channel_id=1, source_target_pairs={{0,1},{1,0},{2,3},{3,2},{4,5},{5,4},{6,7},{7,6},{8,9},{9,8},{10,11... | collective-permute-start | bytes 208904 | tf_op jit(solution)/shard_map/ppermute | solution.py:51
  30.7 2.8 %tail.1 = (bf16[8192,128]{1,0:T(8,128)(2,1)}, bf16[4,128,128]{2,1,0:T(8,128)(2,1)S(1)}, f32[4,128,128]{2,1,0:T(8,128)S(1)}) custom-call(s32[1,64]{1,0:T(1,128)S(1)} %bitcast.34, bf16[8192,128]{1,0:T(8,128)(2,1)S(1)} %bitcast.21, bf16[8192,128]{1,0:T(8,128)(2,1)S(1)} %get-tuple-element.42.refs_2_, bf16[64,128,128]{2,1,0:T(8,128)(2,1)S(1)} %bitcast.26, ...), custom_call_target="tpu_custom_call" | custom-call | flops 536870912 | bytes 4194304 | tf_op jit(solution)/shard_map/tail/pallas_call | solution.py:452
  33.5 0.6 %collective-permute-start.2 = (bf16[4,128,128]{2,1,0:T(8,128)(2,1)S(1)}, bf16[4,128,128]{2,1,0:T(8,128)(2,1)S(1)}, u32[]{:S(2)}, u32[]{:S(2)}) collective-permute-start(bf16[4,128,128]{2,1,0:T(8,128)(2,1)S(1)} %get-tuple-element.45), channel_id=1, source_target_pairs={{0,2},{1,3},{2,0},{3,1},{4,6},{5,7},{6,4},{7,5},{8,10},{9,11},{10,... | collective-permute-start | bytes 393224 | tf_op jit(solution)/shard_map/ppermute | solution.py:51
  34.1 1.6 %collective-permute-start.11 = (bf16[272,128]{1,0:T(8,128)(2,1)S(1)}, bf16[272,128]{1,0:T(8,128)(2,1)S(1)}, u32[]{:S(2)}, u32[]{:S(2)}) collective-permute-start(bf16[272,128]{1,0:T(8,128)(2,1)S(1)} %pad_maximum_fusion.3), channel_id=1, source_target_pairs={{0,2},{1,3},{2,0},{3,1},{4,6},{5,7},{6,4},{7,5},{8,10},{9,11},{10,... | collective-permute-start | bytes 208904 | tf_op jit(solution)/shard_map/ppermute | solution.py:51
  35.7 2.8 %collective-permute-done.2 = bf16[4,128,128]{2,1,0:T(8,128)(2,1)S(1)} collective-permute-done((bf16[4,128,128]{2,1,0:T(8,128)(2,1)S(1)}, bf16[4,128,128]{2,1,0:T(8,128)(2,1)S(1)}, u32[]{:S(2)}, u32[]{:S(2)}) %collective-permute-start.2) | collective-permute-done | bytes 131104 | tf_op jit(solution)/shard_map/ppermute | solution.py:51
  38.5 0.6 %collective-permute-start.3 = (bf16[2,128,128]{2,1,0:T(8,128)(2,1)S(1)}, bf16[2,128,128]{2,1,0:T(8,128)(2,1)S(1)}, u32[]{:S(2)}, u32[]{:S(2)}) collective-permute-start(bf16[2,128,128]{2,1,0:T(8,128)(2,1)S(1)} %slice.94), channel_id=1, source_target_pairs={{0,1},{1,0},{2,3},{3,2},{4,5},{5,4},{6,7},{7,6},{8,9},{9,8},{10,11... | collective-permute-start | bytes 196616 | tf_op jit(solution)/shard_map/ppermute | solution.py:51
  39.1 0.1 collective-permute-done.11
  39.3 2.8 %collective-permute-start.12 = (bf16[200,128]{1,0:T(8,128)(2,1)S(1)}, bf16[200,128]{1,0:T(8,128)(2,1)S(1)}, u32[]{:S(2)}, u32[]{:S(2)}) collective-permute-start(bf16[200,128]{1,0:T(8,128)(2,1)S(1)} %reduce-precision_convert_fusion), channel_id=1, source_target_pairs={{0,4},{1,5},{2,6},{3,7},{4,0},{5,1},{6,2},{7,3},{8,12},{9,13},{10,... | collective-permute-start | bytes 153608 | tf_op jit(solution)/shard_map/ppermute | solution.py:51
  42.0 0.8 %collective-permute-done.3 = bf16[2,128,128]{2,1,0:T(8,128)(2,1)S(1)} collective-permute-done((bf16[2,128,128]{2,1,0:T(8,128)(2,1)S(1)}, bf16[2,128,128]{2,1,0:T(8,128)(2,1)S(1)}, u32[]{:S(2)}, u32[]{:S(2)}) %collective-permute-start.3) | collective-permute-done | bytes 65568 | tf_op jit(solution)/shard_map/ppermute | solution.py:51
  42.9 2.2 %collective-permute-start.4 = (bf16[1,128,128]{2,1,0:T(8,128)(2,1)S(1)}, bf16[1,128,128]{2,1,0:T(8,128)(2,1)S(1)}, u32[]{:S(2)}, u32[]{:S(2)}) collective-permute-start(bf16[1,128,128]{2,1,0:T(8,128)(2,1)S(1)} %slice.95), channel_id=1, source_target_pairs={{0,4},{1,5},{2,6},{3,7},{4,0},{5,1},{6,2},{7,3},{8,12},{9,13},{10,... | collective-permute-start | bytes 98312 | tf_op jit(solution)/shard_map/ppermute | solution.py:51
  45.1 0.1 collective-permute-start.13
  45.2 2.9 %collective-permute-done.4 = bf16[1,128,128]{2,1,0:T(8,128)(2,1)S(1)} collective-permute-done((bf16[1,128,128]{2,1,0:T(8,128)(2,1)S(1)}, bf16[1,128,128]{2,1,0:T(8,128)(2,1)S(1)}, u32[]{:S(2)}, u32[]{:S(2)}) %collective-permute-start.4) | collective-permute-done | bytes 32800 | tf_op jit(solution)/shard_map/ppermute | solution.py:51
  48.1 0.6 %fusion = bf16[1,128,128]{2,1,0:T(8,128)(2,1)} fusion(f32[2,128,128]{2,1,0:T(8,128)S(1)} %slice_add_fusion, bf16[1,128,128]{2,1,0:T(8,128)(2,1)S(1)} %collective-permute-done.4), kind=kLoop, calls=%fused_computation.13 | loop fusion | flops 49152 | bytes 131072 | tf_op jit(solution)/shard_map/convert_element_type | solution.py:475
  48.7 0.9 %finish.1 = (f32[128,128]{1,0:T(8,128)}, f32[256,128]{1,0:T(8,128)}, f32[1,128]{1,0:T(1,128)}, f32[128,128]{1,0:T(8,128)}) custom-call(f32[200,128]{1,0:T(8,128)S(1)} %convert_add_fusion.1.refs_0_, f32[200,128]{1,0:T(8,128)S(1)} %collective-permute-done.13.refs_1_, bf16[128,128]{1,0:T(8,128)(2,1)S(1)} %copy-done.4, bf16[256,128]{1,0:T(8,128)(2,1)S(1)} %copy-done.2), custom_call_target="tpu_custom_call" | custom-call | tf_op jit(solution)/shard_map/finish/pallas_call | solution.py:485
  (48 shorter events, 0.3 us)
Async XLA Ops:
  0.6 6.6 %collective-permute-start.5 = (bf16[128,128]{1,0:T(8,128)(2,1)}, bf16[128,128]{1,0:T(8,128)(2,1)S(1)}, u32[]{:S(2)}, u32[]{:S(2)}) collective-permute-start(bf16[128,128]{1,0:T(8,128)(2,1)} %bitcast.39), channel_id=1, source_target_pairs={{0,4},{1,5},{2,6},{3,7},{4,0},{5,1},{6,2},{7,3},{8,12},{9,13},{10,... | collective-permute-start | bytes 98312 | tf_op jit(solution)/shard_map/ppermute | solution.py:51
  4.8 9.1 %slice-start = ((s8[8388608]{0:T(1024)(128)(4,1)}), s8[4194304]{0:T(1024)(128)(4,1)S(1)}, s32[]{:S(2)}) async-start(s8[8388608]{0:T(1024)(128)(4,1)} %bitcast.11), calls=%async_computation | async-start | bytes 8388608
  4.8 9.1 %slice-start.1 = ((s8[8388608]{0:T(1024)(128)(4,1)}), s8[4194304]{0:T(1024)(128)(4,1)S(1)}, s32[]{:S(2)}) async-start(s8[8388608]{0:T(1024)(128)(4,1)} %bitcast.11), calls=%async_computation.1 | async-start | bytes 8388608
  4.8 9.1 %copy-start = (bf16[1,8192,128]{2,1,0:T(8,128)(2,1)S(1)}, bf16[1,8192,128]{2,1,0:T(8,128)(2,1)}, u32[]{:S(2)}) copy-start(bf16[1,8192,128]{2,1,0:T(8,128)(2,1)} %param.10) | copy-start | bytes 6291460
  4.8 9.1 %copy-start.1 = (bf16[1,64,128,128]{3,2,1,0:T(8,128)(2,1)S(1)}, bf16[1,64,128,128]{3,2,1,0:T(8,128)(2,1)}, u32[]{:S(2)}) copy-start(bf16[1,64,128,128]{3,2,1,0:T(8,128)(2,1)} %param.14) | copy-start | bytes 6291460
  4.8 9.1 %copy-start.2 = (bf16[256,128]{1,0:T(8,128)(2,1)S(1)}, bf16[256,128]{1,0:T(8,128)(2,1)}, u32[]{:S(2)}) copy-start(bf16[256,128]{1,0:T(8,128)(2,1)} %refs_3_.1) | copy-start | bytes 196612
  4.8 9.1 %copy-start.4 = (bf16[128,128]{1,0:T(8,128)(2,1)S(1)}, bf16[128,128]{1,0:T(8,128)(2,1)}, u32[]{:S(2)}) copy-start(bf16[128,128]{1,0:T(8,128)(2,1)} %refs_2_.1) | copy-start | bytes 98308
  4.8 9.1 %copy-start.5 = (s32[1,64,4]{1,2,0:T(4,128)S(1)}, s32[1,64,4]{1,2,0:T(4,128)}, u32[]{:S(2)}) copy-start(s32[1,64,4]{1,2,0:T(4,128)} %param.12) | copy-start | bytes 3076
  4.8 9.1 %copy-start.6 = (s32[1,64,1]{1,2,0:T(1,128)S(1)}, s32[1,64,1]{1,2,0:T(1,128)}, u32[]{:S(2)}) copy-start(s32[1,64,1]{1,2,0:T(1,128)} %param.13) | copy-start | bytes 772
  4.8 9.1 %copy-start.7 = (f32[128]{0:T(128)S(1)}, f32[128]{0:T(128)}, u32[]{:S(2)}) copy-start(f32[128]{0:T(128)} %param.18) | copy-start | bytes 1540
  7.2 4.3 %collective-permute-start.6 = (bf16[256,128]{1,0:T(8,128)(2,1)S(1)}, bf16[256,128]{1,0:T(8,128)(2,1)S(1)}, u32[]{:S(2)}, u32[]{:S(2)}) collective-permute-start(bf16[256,128]{1,0:T(8,128)(2,1)S(1)} %pad_maximum_fusion.4), channel_id=1, source_target_pairs={{0,1},{1,0},{2,3},{3,2},{4,5},{5,4},{6,7},{7,6},{8,9},{9,8},{10,11... | collective-permute-start | bytes 196616 | tf_op jit(solution)/shard_map/ppermute | solution.py:51
  9.0 9.7 %collective-permute-start = (bf16[256,128]{1,0:T(8,128)(2,1)S(1)}, bf16[256,128]{1,0:T(8,128)(2,1)S(1)}, u32[]{:S(2)}, u32[]{:S(2)}) collective-permute-start(bf16[256,128]{1,0:T(8,128)(2,1)S(1)} %get-tuple-element.31), channel_id=1, source_target_pairs={{0,1},{1,0},{2,3},{3,2},{4,5},{5,4},{6,7},{7,6},{8,9},{9,8},{10,11... | collective-permute-start | bytes 196616 | tf_op jit(solution)/shard_map/ppermute | solution.py:51
  9.3 9.4 %collective-permute-start.1 = (bf16[256,128]{1,0:T(8,128)(2,1)S(1)}, bf16[256,128]{1,0:T(8,128)(2,1)S(1)}, u32[]{:S(2)}, u32[]{:S(2)}) collective-permute-start(bf16[256,128]{1,0:T(8,128)(2,1)S(1)} %get-tuple-element.32), channel_id=1, source_target_pairs={{0,8},{1,2},{2,1},{3,4},{4,3},{5,6},{6,5},{7,15},{8,0},{9,10},{10,... | collective-permute-start | bytes 196616 | tf_op jit(solution)/shard_map/ppermute | solution.py:377
  11.5 9.2 %collective-permute-start.7 = (bf16[512,128]{1,0:T(8,128)(2,1)S(1)}, bf16[512,128]{1,0:T(8,128)(2,1)S(1)}, u32[]{:S(2)}, u32[]{:S(2)}) collective-permute-start(bf16[512,128]{1,0:T(8,128)(2,1)S(1)} %pad_maximum_fusion), channel_id=1, source_target_pairs={{0,2},{1,3},{2,0},{3,1},{4,6},{5,7},{6,4},{7,5},{8,10},{9,11},{10,... | collective-permute-start | bytes 393224 | tf_op jit(solution)/shard_map/ppermute | solution.py:51
  18.7 2.0 %copy-start.3 = (bf16[128,128]{1,0:T(8,128)(2,1)S(1)}, bf16[128,128]{1,0:T(8,128)(2,1)}, u32[]{:S(2)}) copy-start(bf16[128,128]{1,0:T(8,128)(2,1)} %refs_10_.1) | copy-start | bytes 98308
  23.2 1.4 %collective-permute-start.8 = (f32[200,128]{1,0:T(8,128)S(1)}, f32[200,128]{1,0:T(8,128)S(1)}, u32[]{:S(2)}, u32[]{:S(2)}) collective-permute-start(f32[200,128]{1,0:T(8,128)S(1)} %get-tuple-element.51), channel_id=1, source_target_pairs={{0,8},{8,0},{16,24},{24,16},{1,9},{9,1},{17,25},{25,17},{2,10},{10... | collective-permute-start | bytes 307208 | tf_op jit(solution)/shard_map/ppermute | solution.py:51
  24.7 4.4 %collective-permute-start.9 = (bf16[272,128]{1,0:T(8,128)(2,1)S(1)}, bf16[272,128]{1,0:T(8,128)(2,1)S(1)}, u32[]{:S(2)}, u32[]{:S(2)}) collective-permute-start(bf16[272,128]{1,0:T(8,128)(2,1)S(1)} %pad_maximum_fusion.1), channel_id=1, source_target_pairs={{0,16},{8,24},{16,0},{24,8},{1,17},{9,25},{17,1},{25,9},{2,18},{10... | collective-permute-start | bytes 208904 | tf_op jit(solution)/shard_map/ppermute | solution.py:51
  29.1 4.9 %collective-permute-start.10 = (bf16[272,128]{1,0:T(8,128)(2,1)S(1)}, bf16[272,128]{1,0:T(8,128)(2,1)S(1)}, u32[]{:S(2)}, u32[]{:S(2)}) collective-permute-start(bf16[272,128]{1,0:T(8,128)(2,1)S(1)} %pad_maximum_fusion.2), channel_id=1, source_target_pairs={{0,1},{1,0},{2,3},{3,2},{4,5},{5,4},{6,7},{7,6},{8,9},{9,8},{10,11... | collective-permute-start | bytes 208904 | tf_op jit(solution)/shard_map/ppermute | solution.py:51
  33.5 5.0 %collective-permute-start.2 = (bf16[4,128,128]{2,1,0:T(8,128)(2,1)S(1)}, bf16[4,128,128]{2,1,0:T(8,128)(2,1)S(1)}, u32[]{:S(2)}, u32[]{:S(2)}) collective-permute-start(bf16[4,128,128]{2,1,0:T(8,128)(2,1)S(1)} %get-tuple-element.45), channel_id=1, source_target_pairs={{0,2},{1,3},{2,0},{3,1},{4,6},{5,7},{6,4},{7,5},{8,10},{9,11},{10,... | collective-permute-start | bytes 393224 | tf_op jit(solution)/shard_map/ppermute | solution.py:51
  34.1 5.1 %collective-permute-start.11 = (bf16[272,128]{1,0:T(8,128)(2,1)S(1)}, bf16[272,128]{1,0:T(8,128)(2,1)S(1)}, u32[]{:S(2)}, u32[]{:S(2)}) collective-permute-start(bf16[272,128]{1,0:T(8,128)(2,1)S(1)} %pad_maximum_fusion.3), channel_id=1, source_target_pairs={{0,2},{1,3},{2,0},{3,1},{4,6},{5,7},{6,4},{7,5},{8,10},{9,11},{10,... | collective-permute-start | bytes 208904 | tf_op jit(solution)/shard_map/ppermute | solution.py:51
  38.5 4.3 %collective-permute-start.3 = (bf16[2,128,128]{2,1,0:T(8,128)(2,1)S(1)}, bf16[2,128,128]{2,1,0:T(8,128)(2,1)S(1)}, u32[]{:S(2)}, u32[]{:S(2)}) collective-permute-start(bf16[2,128,128]{2,1,0:T(8,128)(2,1)S(1)} %slice.94), channel_id=1, source_target_pairs={{0,1},{1,0},{2,3},{3,2},{4,5},{5,4},{6,7},{7,6},{8,9},{9,8},{10,11... | collective-permute-start | bytes 196616 | tf_op jit(solution)/shard_map/ppermute | solution.py:51
  39.3 5.8 %collective-permute-start.12 = (bf16[200,128]{1,0:T(8,128)(2,1)S(1)}, bf16[200,128]{1,0:T(8,128)(2,1)S(1)}, u32[]{:S(2)}, u32[]{:S(2)}) collective-permute-start(bf16[200,128]{1,0:T(8,128)(2,1)S(1)} %reduce-precision_convert_fusion), channel_id=1, source_target_pairs={{0,4},{1,5},{2,6},{3,7},{4,0},{5,1},{6,2},{7,3},{8,12},{9,13},{10,... | collective-permute-start | bytes 153608 | tf_op jit(solution)/shard_map/ppermute | solution.py:51
  42.9 5.2 %collective-permute-start.4 = (bf16[1,128,128]{2,1,0:T(8,128)(2,1)S(1)}, bf16[1,128,128]{2,1,0:T(8,128)(2,1)S(1)}, u32[]{:S(2)}, u32[]{:S(2)}) collective-permute-start(bf16[1,128,128]{2,1,0:T(8,128)(2,1)S(1)} %slice.95), channel_id=1, source_target_pairs={{0,4},{1,5},{2,6},{3,7},{4,0},{5,1},{6,2},{7,3},{8,12},{9,13},{10,... | collective-permute-start | bytes 98312 | tf_op jit(solution)/shard_map/ppermute | solution.py:51
  45.1 3.6 %collective-permute-start.13 = (f32[200,128]{1,0:T(8,128)S(1)}, f32[200,128]{1,0:T(8,128)S(1)}, u32[]{:S(2)}, u32[]{:S(2)}) collective-permute-start(f32[200,128]{1,0:T(8,128)S(1)} %convert_add_fusion.1.refs_0_), channel_id=1, source_target_pairs={{0,8},{8,0},{16,24},{24,16},{1,9},{9,1},{17,25},{25,17},{2,10},{10... | collective-permute-start | bytes 307208 | tf_op jit(solution)/shard_map/ppermute | solution.py:51
